TPU v7x, 32 devices: a whole 2x2x4 slice. The times are simulated.
32 devices in a mesh: block: 8 (over y, x, core), sub: 4 (over z).
Axes of the slice: x: 2, y: 2, z: 4, core: 2. Of those that a mesh axis runs over, the one named last changes fastest.
Arguments:
- source: float32 [8, 16, 128, 128], P('block', 'sub'), may hold values from -48 to 48
- trans_x: float32 [8, 16, 128, 128], P('block', 'sub'), may hold values from 0.1 to 10
- trans_y: float32 [8, 16, 128, 128], P('block', 'sub'), may hold values from 0.1 to 10
- trans_z: float32 [8, 16, 128, 128], P('block', 'sub'), may hold values from 0.1 to 10
- mortar_bot: float32 [8, 16, 128, 256], P('block', 'sub'), may hold values from -0.375 to 0.375
- mortar_top: float32 [8, 16, 128, 256], P('block', 'sub'), may hold values from -0.375 to 0.375
Outputs:
- pressure: float32 [8, 16, 128, 128], P('block', 'sub')
- mortar: float32 [8, 256], P('block', 'sub')
All inputs are finite; a program needn't handle non-finite values.
Results may differ from a plain program's by a relative error of at most 0.0003.
Values sent between devices are 32-bit elements; how exact they have to be, the bound alone decides.
No kernel may reach another device: no remote copies, remote signals or barrier semaphores. Data moves between devices by JAX's collectives and lax.ppermute only.
A program may use at most 64 MiB of HBM per device.

v0:
```python
import jax
import jax.numpy as jnp
from jax import lax
from jax.experimental import pallas as pl
from jax.experimental.pallas import tpu as pltpu
from jax.sharding import PartitionSpec as P


PASSES = 3
RELAX = 0.8
KEEP = 1.0 - RELAX
MORTAR_STEP = 0.05
F32 = jnp.float32
EDGE = 6
MIDDLE = 3
HALO = 2
SLAB = 8
SPAN = 2 * SLAB
DIRECT = 4
ITEMS = 5


def prev(v, axis):
    return pltpu.roll(v, 1, axis)


def following(v, axis):
    return pltpu.roll(v, v.shape[axis] - 1, axis)


class Layer:
    def __init__(self, trans_y, trans_z, has_bot, has_top):
        rows = lax.broadcasted_iota(jnp.int32, trans_y.shape, 0)
        self.cy = jnp.where(rows > 0, trans_y, 0.0)
        self.cz, self.zsum = along_z(trans_z, has_bot, has_top)
        self.diag = self.cy + following(self.cy, 0) + self.zsum

    def around(self, p):
        return (
            self.cy * prev(p, 0)
            + following(self.cy * p, 0)
            + self.cz * prev(p, 1)
            + following(self.cz * p, 1)
        )


def along_z(trans_z, has_bot, has_top):
    cols = lax.broadcasted_iota(jnp.int32, trans_z.shape, 1)
    first = cols == 0
    last = cols == trans_z.shape[1] - 1
    cz = jnp.where(first, 0.0, trans_z)
    ends = jnp.where(first, trans_z * has_bot, jnp.where(last, trans_z * has_top, 0.0))
    return cz, cz + following(cz, 1) + ends


class Thin:
    def __init__(self, trans_y, trans_z, zsum, has_bot, has_top):
        rows = lax.broadcasted_iota(jnp.int32, trans_y.shape, 0)
        cols = lax.broadcasted_iota(jnp.int32, trans_y.shape, 1)
        self.cy = jnp.where(cols > 0, trans_y, 0.0)
        self.cz = jnp.where(rows == SLAB, 0.0, trans_z)
        self.dbot = jnp.where(rows == SLAB, trans_z, 0.0) * has_bot
        self.dtop = jnp.where(rows == SLAB - 1, trans_z, 0.0) * has_top
        self.diag = self.cy + following(self.cy, 1) + zsum

    def around(self, p):
        return (
            self.cy * prev(p, 1)
            + following(self.cy * p, 1)
            + self.cz * prev(p, 0)
            + following(self.cz * p, 0)
        )


def flags():
    block = lax.axis_index("block")
    sub = lax.axis_index("sub")
    has_bot = (block > 0).astype(F32)
    has_top = (block < lax.axis_size("block") - 1).astype(F32)
    has_below = (sub > 0).astype(F32)
    has_above = (sub < lax.axis_size("sub") - 1).astype(F32)
    return has_bot, has_top, has_below, has_above


def by_parity(axis, first, second, upward, downward):
    even = lax.rem(lax.axis_index(axis), 2) == 0

    @pl.when(even)
    def _():
        upward(first)
        downward(second)

    @pl.when(jnp.logical_not(even))
    def _():
        upward(second)
        downward(first)


def sort_pair(pair, above, below):
    def take_above(ref):
        above[...] = ref[...]

    def take_below(ref):
        below[...] = ref[...]

    by_parity("sub", *pair, take_above, take_below)


def pack_kernel(src, tx, ty, tz, src_v, tx_v, ty_v, tz_v, slabs, out_a, out_b, sems):
    copies = [
        pltpu.make_async_copy(here, there, sems.at[i])
        for i, (here, there) in enumerate(
            ((tz, tz_v), (src, src_v), (tx, tx_v), (ty, ty_v))
        )
    ]
    for copy in copies:
        copy.start()
    for copy in copies:
        copy.wait()
    count, rows, cells = src_v.shape[1:]
    has_bot, has_top, _, _ = flags()
    items = []
    for x in range(count):
        zsum = along_z(tz_v[0, x], has_bot, has_top)[1]
        items += [tx_v[0, x], src_v[0, x], ty_v[0, x], tz_v[0, x], zsum]
    slot = lax.broadcasted_iota(jnp.int32, (rows, cells), 1) // SPAN
    each = cells // SPAN
    for start in range(0, len(items), each):
        packed = jnp.zeros((rows, cells), F32)
        for j, item in enumerate(items[start : start + each]):
            turned = pltpu.roll(item, (SPAN * j + SLAB) % cells, 1)
            packed = jnp.where(slot == j, turned, packed)
        slabs[start * SPAN : (start + each) * SPAN] = packed.T
    length = out_a.shape[0]
    last = count * ITEMS * SPAN

    def upward(ref):
        ref[0 : HALO * ITEMS * SPAN] = slabs[last - HALO * ITEMS * SPAN : last]
        ref[HALO * ITEMS * SPAN :] = slabs[0:SPAN]

    def downward(ref):
        ref[...] = slabs[0:length]

    by_parity("sub", out_a, out_b, upward, downward)


def thin_round(slabs, above, below, reach, count):
    has_bot, has_top, has_below, has_above = flags()

    def item(x, which):
        if x < 0:
            start = ((x + HALO) * ITEMS + which) * SPAN
            return below[start : start + SPAN]
        if x >= count:
            start = ((x - count) * ITEMS + which) * SPAN
            return above[start : start + SPAN]
        start = (x * ITEMS + which) * SPAN
        return slabs[start : start + SPAN]

    cx = {x: item(x, 0) for x in range(-reach, count + reach + 1)}
    cx[0] = cx[0] * has_below
    cx[count] = cx[count] * has_above
    span = range(-reach, count + reach)
    source = {x: item(x, 1) for x in span}
    layers = {x: Thin(item(x, 2), item(x, 3), item(x, 4), has_bot, has_top) for x in span}
    weight = {x: RELAX / (layers[x].diag + cx[x] + cx[x + 1]) for x in span}
    return source, cx, layers, weight


def thin_pass(p, rhs, cx, layers, weight, low, high):
    return {
        x: KEEP * p[x]
        + weight[x] * (rhs[x] + cx[x] * p[x - 1] + cx[x + 1] * p[x + 1] + layers[x].around(p[x]))
        for x in range(low, high)
    }


def edge_data(ref, p, x, beyond, link, rhs, cx, layers, weight):
    ref[0] = p[x]
    ref[1] = KEEP * p[x] + weight[x] * (rhs[x] + link * p[beyond] + layers[x].around(p[x]))
    step = thin_pass(p, rhs, cx, layers, weight, beyond, beyond + 1)
    ref[2] = rhs[x] + link * step[beyond]


def three_passes(p, above, below, rhs, cx, layers, weight, count):
    sides = ((count, count - 1, cx[count], above), (-1, 0, cx[0], below))
    for x, _, _, got in sides:
        p[x] = got[0]
    after = thin_pass(p, rhs, cx, layers, weight, 0, count)
    for x, near, link, got in sides:
        after[x] = got[1] + weight[x] * link * p[near]
    last = thin_pass(after, rhs, cx, layers, weight, 0, count)
    for x, near, link, got in sides:
        last[x] = KEEP * after[x] + weight[x] * (
            got[2] + link * after[near] + layers[x].around(after[x])
        )
    return thin_pass(last, rhs, cx, layers, weight, 0, count)


def traces(flux_bot, flux_top, bot, top, rows):
    count = len(flux_bot)
    stacked = jnp.concatenate(flux_bot + flux_top, axis=0)
    fill = jnp.zeros((rows - stacked.shape[0], stacked.shape[1]), F32)
    columns = jnp.concatenate([stacked, fill], axis=0).T
    return [
        sum(
            jnp.sum(columns[:, face * count + x : face * count + x + 1] * basis[0, x], axis=0, keepdims=True)
            for x in range(count)
        )
        for face, basis in enumerate((bot, top))
    ]


def first_thin(slabs, bot, top, got_a, got_b, p_out, sh_a, sh_b, above, below):
    count, rows = bot.shape[1:3]
    sort_pair((got_a, got_b), above, below)
    source, cx, layers, weight = thin_round(slabs, above, below, HALO, count)
    p = {x: weight[x] * source[x] for x in range(-HALO, count + HALO)}
    for margin in range(HALO - 1, -1, -1):
        p = thin_pass(p, source, cx, layers, weight, -margin, count + margin)
    for x in range(count):
        p_out[x] = p[x]
    flux_bot = [(layers[x].dbot * p[x])[SLAB : SLAB + 1] for x in range(count)]
    flux_top = [(layers[x].dtop * p[x])[SLAB - 1 : SLAB] for x in range(count)]
    cbot, ctop = traces(flux_bot, flux_top, bot, top, rows)

    def to_above(ref):
        ref[...] = ctop

    def to_below(ref):
        ref[...] = cbot

    by_parity("block", sh_a, sh_b, to_above, to_below)


def with_faces(source, layers, data, count):
    gbot = {x: data[x : x + 1] for x in range(count)}
    gtop = {x: data[count + x : count + x + 1] for x in range(count)}
    rhs = {
        x: source[x] + layers[x].dbot * gbot[x] + layers[x].dtop * gtop[x]
        for x in range(count)
    }
    return gbot, gtop, rhs


def face_kernel(slabs, bot, top, got_a, got_b, p_in, *rest):
    parts = rest[:-6]
    data_out, edge_a, edge_b, mortar_out, above, below = rest[-6:]
    count, rows = bot.shape[1:3]
    sort_pair((got_a, got_b), above, below)
    jumps = MORTAR_STEP * sum(part[...] for part in parts)
    even = lax.rem(lax.axis_index("block"), 2) == 0
    own = jnp.where(even, jumps[0:1], jumps[1:2])
    under = jnp.where(even, jumps[1:2], jumps[0:1])
    mortar_out[...] = own
    lanes = lax.broadcasted_iota(jnp.int32, (rows, rows), 1)
    columns = jnp.zeros((rows, rows), F32)
    for face, (ref, values) in enumerate(((bot, under), (top, own))):
        for x in range(count):
            data = jnp.sum(ref[0, x] * values, axis=1, keepdims=True)
            columns = jnp.where(lanes == face * count + x, data, columns)
    data = columns.T[0 : 2 * count]
    data_out[...] = data
    source, cx, layers, weight = thin_round(slabs, above, below, 0, count)
    rhs = with_faces(source, layers, data, count)[2]
    p = {x: p_in[x] for x in range(count)}
    last = count - 1
    by_parity(
        "sub",
        edge_a,
        edge_b,
        lambda ref: edge_data(ref, p, last, last - 1, cx[last], rhs, cx, layers, weight),
        lambda ref: edge_data(ref, p, 0, 1, cx[1], rhs, cx, layers, weight),
    )


def second_thin(
    slabs, bot, top, got_a, got_b, p_in, data, edge_a, edge_b,
    p_out, cbot_out, ctop_out, above, below, edge_above, edge_below,
):
    count, rows = bot.shape[1:3]
    sort_pair((got_a, got_b), above, below)
    sort_pair((edge_a, edge_b), edge_above, edge_below)
    source, cx, layers, weight = thin_round(slabs, above, below, 1, count)
    gbot, gtop, rhs = with_faces(source, layers, data, count)
    p = {x: p_in[x] for x in range(count)}
    p = three_passes(p, edge_above, edge_below, rhs, cx, layers, weight, count)
    for x in range(count):
        p_out[x * SPAN : (x + 1) * SPAN] = p[x]
    flux_bot = [(layers[x].dbot * (p[x] - gbot[x]))[SLAB : SLAB + 1] for x in range(count)]
    flux_top = [(layers[x].dtop * (p[x] - gtop[x]))[SLAB - 1 : SLAB] for x in range(count)]
    cbot_out[...], ctop_out[...] = traces(flux_bot, flux_top, bot, top, rows)


def edge_kernel(src, tx, ty, tz, out_a, out_b):
    count = src.shape[1]
    has_bot, has_top, has_below, _ = flags()

    def layer(x):
        return Layer(ty[0, x], tz[0, x], has_bot, has_top)

    low = layer(0)
    w_low = RELAX / (low.diag + tx[0, 0] * has_below + tx[0, 1])
    p_low = w_low * src[0, 0]
    p_next = RELAX * src[0, 1] / (layer(1).diag + tx[0, 1] + tx[0, 2])
    q_low = KEEP * p_low + w_low * (src[0, 0] + tx[0, 1] * p_next + low.around(p_low))
    top = count - 1
    p_top = RELAX * src[0, top - 1] / (layer(top - 1).diag + tx[0, top - 1] + tx[0, top])

    def upward(ref):
        for i, v in enumerate((tx[0, top], p_top, src[0, top], src[0, top], ty[0, top], tz[0, top])):
            ref[i] = v

    def downward(ref):
        for i, v in enumerate((tx[0, 0], p_low, q_low, w_low, ty[0, 0], tz[0, 0])):
            ref[i] = v

    by_parity("sub", out_a, out_b, upward, downward)


def whole_setup(src, tx, ty, tz, above, below):
    count = src.shape[1]
    has_bot, has_top, has_below, has_above = flags()
    cx = {x: tx[0, x] for x in range(1, count)}
    cx[-1] = below[0]
    cx[0] = tx[0, 0] * has_below
    cx[count] = above[0] * has_above
    source = {x: src[0, x] for x in range(count)}
    source[-1] = below[2]
    layers = {x: Layer(ty[0, x], tz[0, x], has_bot, has_top) for x in range(count)}
    layers[-1] = Layer(below[4], below[5], has_bot, has_top)
    weight = {x: RELAX / (layers[x].diag + cx[x] + cx[x + 1]) for x in range(-1, count)}
    return source, cx, layers, weight


def first_whole(src, tx, ty, tz, got_a, got_b, after, p_out, mid_a, mid_b, above, below):
    count = src.shape[1]
    sort_pair((got_a, got_b), above, below)
    source, cx, layers, w = whole_setup(src, tx, ty, tz, above, below)
    p1 = {x: w[x] * source[x] for x in range(-1, count)}
    p1[-2] = below[1]
    p1[count] = above[1]
    p2 = thin_pass(p1, source, cx, layers, w, -1, count)
    p2[count] = above[2] + above[3] * cx[count] * p1[count - 1]
    p3 = thin_pass(p2, source, cx, layers, w, 0, count)
    for x in range(count):
        p_out[x] = p3[x]
    last = count - 1
    by_parity(
        "sub",
        mid_a,
        mid_b,
        lambda ref: edge_data(ref, p3, last, last - 1, cx[last], source, cx, layers, w),
        lambda ref: edge_data(ref, p3, 0, 1, cx[1], source, cx, layers, w),
    )


def second_whole(src, tx, ty, tz, got_a, got_b, p_in, mid_a, mid_b, thin, p_out, above, below, p_above, p_below):
    count, rows, cells = src.shape[1:]
    sort_pair((got_a, got_b), above, below)
    sort_pair((mid_a, mid_b), p_above, p_below)
    source, cx, layers, w = whole_setup(src, tx, ty, tz, above, below)
    has_bot, has_top, _, _ = flags()
    layers[count] = Layer(above[4], above[5], has_bot, has_top)
    w[count] = above[3]
    p3 = {x: p_in[x] for x in range(count)}
    p6 = three_passes(p3, p_above, p_below, source, cx, layers, w, count)
    cols = lax.broadcasted_iota(jnp.int32, (rows, cells), 1)
    face = (cols < PASSES) | (cols >= cells - PASSES)
    each = cells // SPAN
    for start in range(0, count, each):
        here = thin[start * SPAN : (start + each) * SPAN]
        if here.shape[0] < cells:
            here = jnp.concatenate([here, jnp.zeros((cells - here.shape[0], rows), F32)], axis=0)
        back = here.T
        for x in range(start, min(start + each, count)):
            shift = (cells - (x - start) * SPAN - SLAB) % cells
            p_out[0, x] = jnp.where(face, pltpu.roll(back, shift, 1), p6[x])


def call(kernel, outs, args, scratch=(), copies=0):
    space = pltpu.HBM if copies else pltpu.VMEM
    args = [pltpu.with_memory_space_constraint(a, space) for a in args]
    return pl.pallas_call(
        kernel,
        out_shape=[pltpu.VMEM(shape, F32) for shape in outs],
        in_specs=[pl.BlockSpec(memory_space=space)] * len(args),
        out_specs=[pl.BlockSpec(memory_space=pltpu.VMEM)] * len(outs),
        scratch_shapes=[pltpu.VMEM(shape, F32) for shape in scratch]
        + ([pltpu.SemaphoreType.DMA((copies,))] if copies else []),
        compiler_params=pltpu.CompilerParams(vmem_limit_bytes=16 << 20),
    )(*args)


def sub_swaps(blocks, subs):
    flat = lambda b, s: b * subs + s
    first = [(flat(b, s), flat(b, s ^ 1)) for b in range(blocks) for s in range(subs)]
    second = []
    for b in range(blocks):
        for s in range(subs):
            other = s + 1 if s % 2 else s - 1
            inside = 0 <= other < subs
            second.append((flat(b, s), flat(b, other) if inside else flat(b ^ 1, s)))
    return first, second


def work(source, trans_x, trans_y, trans_z, mortar_bot, mortar_top):
    count, rows, cells = source.shape[1:]
    width = mortar_bot.shape[3]
    subs = lax.axis_size("sub")
    blocks = lax.axis_size("block")
    assert subs % 2 == 0 and blocks % 2 == 0 and count > HALO
    names = ("block", "sub")
    pair_one, pair_two = sub_swaps(blocks, subs)

    def trade(a, b):
        first = lax.ppermute(a, names, pair_one)
        return first, lax.ppermute(b, names, pair_two)

    face = (rows, cells)
    each = cells // SPAN
    slab_rows = -(-count * ITEMS // each) * cells
    sent = (HALO * ITEMS + 1) * SPAN
    *coeffs, slabs, near_a, near_b = call(
        pack_kernel,
        [source.shape] * 4 + [(slab_rows, rows)] + [(sent, rows)] * 2,
        (source, trans_x, trans_y, trans_z),
        copies=4,
    )
    near = trade(near_a, near_b)
    edges = call(edge_kernel, [(EDGE,) + face] * 2, coeffs)
    edges = trade(*edges)
    slab = (SPAN, rows)
    third, share_a, share_b = call(
        first_thin,
        [(count,) + slab] + [(1, width)] * 2,
        (slabs, mortar_bot, mortar_top) + near,
        [(sent, rows)] * 2,
    )

    block_one = [(b, b ^ 1) for b in range(blocks)]
    block_two = [(b, (b + 1 if b % 2 else b - 1) % blocks) for b in range(blocks)]

    def everyone(value):
        if subs > DIRECT:
            return [lax.psum(value, "sub")]
        parts = [value]
        for k in range(subs - 1, 0, -1):
            parts.append(lax.ppermute(value, "sub", [(i, i ^ k) for i in range(subs)]))
        return parts

    other_a = lax.ppermute(share_a, "block", block_one)
    other_b = lax.ppermute(share_b, "block", block_two)
    jumps = jnp.concatenate([share_a + other_a, share_b + other_b], axis=0)
    parts = everyone(jumps)
    whole, mid_a, mid_b = call(
        first_whole,
        [(count,) + face] + [(MIDDLE,) + face] * 2,
        tuple(coeffs) + edges + (jumps,),
        [(EDGE,) + face] * 2,
    )
    middle = trade(mid_a, mid_b)
    data, edge_a, edge_b, mortar = call(
        face_kernel,
        [(2 * count, rows)] + [(MIDDLE,) + slab] * 2 + [(1, width)],
        (slabs, mortar_bot, mortar_top) + near + (third,) + tuple(parts),
        [(sent, rows)] * 2,
    )
    got = trade(edge_a, edge_b)
    slab_out, cbot, ctop = call(
        second_thin,
        [(each * SPAN, rows)] + [(1, width)] * 2,
        (slabs, mortar_bot, mortar_top) + near + (third, data) + got,
        [(sent, rows)] * 2 + [(MIDDLE,) + slab] * 2,
    )
    upper = lax.ppermute(cbot, "block", [((b + 1) % blocks, b) for b in range(blocks)])
    total = mortar + MORTAR_STEP * sum(everyone(ctop + upper))
    share = width // subs
    final = lax.dynamic_slice_in_dim(total[0], lax.axis_index("sub") * share, share, 0)
    (pressure,) = call(
        second_whole,
        [source.shape],
        tuple(coeffs) + edges + (whole,) + middle + (slab_out,),
        [(EDGE,) + face] * 2 + [(MIDDLE,) + face] * 2,
    )
    return pressure, final[None]


def solution(mesh):
    spec = P("block", "sub", None, None)
    return jax.shard_map(
        work,
        mesh=mesh,
        in_specs=(spec,) * 6,
        out_specs=(spec, P("block", "sub")),
        check_vma=False,
    )
```

profile of v0, /device:TPU:0, one launch (start us, length us, event | category | flops | bytes accessed | tf_op | source)
XLA Modules:
  0.0 50.3 jit_solution(781888600084795404)
XLA Ops:
  0.6 1.8 %shard_map.77 = (f32[1,4,128,128]{3,2,1,0:T(8,128)S(1)}, f32[1,4,128,128]{3,2,1,0:T(8,128)S(1)}, f32[1,4,128,128]{3,2,1,0:T(8,128)S(1)}, f32[1,4,128,128]{3,2,1,...) custom-call(f32[1,4,128,128]{3,2,1,0:T(8,128)} %src.1, ...), custom_call_target="tpu_custom_call" | custom-call | tf_op jit(solution)/shard_map/pallas_call | solution.py:384
  2.8 3.1 %collective-permute-start = (f32[6,128,128]{2,1,0:T(8,128)S(1)}, f32[6,128,128]{2,1,0:T(8,128)S(1)}, u32[]{:S(2)}, u32[]{:S(2)}) collective-permute-start(f32[6,128,128]{2,1,0:T(8,128)S(1)} %get-tuple-element.28), channel_id=1, source_target_pairs={{0,1},{1,0},{2,3},{3,2},{4,5},{5,4},{6,7},{7,6},{8,9},{9,8},{10,11... | collective-permute-start | bytes 1179656 | tf_op jit(solution)/shard_map/ppermute | solution.py:417
  5.9 3.1 %collective-permute-start.2 = (f32[176,128]{1,0:T(8,128)S(1)}, f32[176,128]{1,0:T(8,128)S(1)}, u32[]{:S(2)}, u32[]{:S(2)}) collective-permute-start(f32[176,128]{1,0:T(8,128)S(1)} %get-tuple-element.31), channel_id=1, source_target_pairs={{0,1},{1,0},{2,3},{3,2},{4,5},{5,4},{6,7},{7,6},{8,9},{9,8},{10,11... | collective-permute-start | bytes 270344 | tf_op jit(solution)/shard_map/ppermute | solution.py:417
  9.0 7.9 %collective-permute-done.2.got_a = f32[176,128]{1,0:T(8,128)S(1)} collective-permute-done((f32[176,128]{1,0:T(8,128)S(1)}, f32[176,128]{1,0:T(8,128)S(1)}, u32[]{:S(2)}, u32[]{:S(2)}) %collective-permute-start.2) | collective-permute-done | bytes 90144 | tf_op jit(solution)/shard_map/ppermute | solution.py:417
  16.9 0.7 %shard_map.79 = (f32[4,16,128]{2,1,0:T(8,128)S(1)}, f32[1,256]{1,0:T(1,128)S(1)}, f32[1,256]{1,0:T(1,128)S(1)}) custom-call(f32[384,128]{1,0:T(8,128)S(1)} %get-tuple-element.30.slabs, f32[1,4,128,256]{3,2,1,0:T(8,128)S(1)} %copy-done, f32[1,4,128,256]{3,2,1,0:T(8,128)S(1)} %copy-done.1, f32[176,128]{1,0:T(8,128)S(1)} %collective-permute-done.2.got_a, ...), custom_call_target="tpu_custom_call" | custom-call | tf_op jit(solution)/shard_map/pallas_call | solution.py:384
  17.7 2.7 %collective-permute-start.5 = (f32[1,256]{1,0:T(1,128)S(1)}, f32[1,256]{1,0:T(1,128)S(1)}, u32[]{:S(2)}, u32[]{:S(2)}) collective-permute-start(f32[1,256]{1,0:T(1,128)S(1)} %get-tuple-element.34), channel_id=1, source_target_pairs={{0,28},{4,8},{8,4},{12,16},{16,12},{20,24},{24,20},{28,0},{1,29},{... | collective-permute-start | bytes 3080 | tf_op jit(solution)/shard_map/ppermute | solution.py:453
  20.4 1.3 %collective-permute-done.5 = f32[1,256]{1,0:T(1,128)S(1)} collective-permute-done((f32[1,256]{1,0:T(1,128)S(1)}, f32[1,256]{1,0:T(1,128)S(1)}, u32[]{:S(2)}, u32[]{:S(2)}) %collective-permute-start.5) | collective-permute-done | bytes 1056 | tf_op jit(solution)/shard_map/ppermute | solution.py:453
  21.7 0.9 %shard_map.80 = (f32[4,128,128]{2,1,0:T(8,128)S(1)}, f32[3,128,128]{2,1,0:T(8,128)S(1)}, f32[3,128,128]{2,1,0:T(8,128)S(1)}) custom-call(f32[1,4,128,128]{3,2,1,0:T(8,128)S(1)} %get-tuple-element.24.src, f32[1,4,128,128]{3,2,1,0:T(8,128)S(1)} %get-tuple-element.25.tx, f32[1,4,128,128]{3,2,1,0:T(8,128)S(1)} %get-tuple-element.26.ty, ...), custom_call_target="tpu_custom_call" | custom-call | tf_op jit(solution)/shard_map/pallas_call | solution.py:384
  22.7 2.9 %collective-permute-start.6 = (f32[3,128,128]{2,1,0:T(8,128)S(1)}, f32[3,128,128]{2,1,0:T(8,128)S(1)}, u32[]{:S(2)}, u32[]{:S(2)}) collective-permute-start(f32[3,128,128]{2,1,0:T(8,128)S(1)} %get-tuple-element.36), channel_id=1, source_target_pairs={{0,1},{1,0},{2,3},{3,2},{4,5},{5,4},{6,7},{7,6},{8,9},{9,8},{10,11... | collective-permute-start | bytes 589832 | tf_op jit(solution)/shard_map/ppermute | solution.py:417
  25.5 2.0 %collective-permute-start.10 = (f32[2,256]{1,0:T(2,128)S(1)}, f32[2,256]{1,0:T(2,128)S(1)}, u32[]{:S(2)}, u32[]{:S(2)}) collective-permute-start(f32[2,256]{1,0:T(2,128)S(1)} %pad_maximum_fusion.after.rest_0_), channel_id=1, source_target_pairs={{0,1},{1,0},{2,3},{3,2},{4,5},{5,4},{6,7},{7,6},{8,9},{9,8},{10,11... | collective-permute-start | bytes 6152 | tf_op jit(solution)/shard_map/ppermute | solution.py:449
  27.6 1.2 %collective-permute-start.9 = (f32[2,256]{1,0:T(2,128)S(1)}, f32[2,256]{1,0:T(2,128)S(1)}, u32[]{:S(2)}, u32[]{:S(2)}) collective-permute-start(f32[2,256]{1,0:T(2,128)S(1)} %pad_maximum_fusion.after.rest_0_), channel_id=1, source_target_pairs={{0,2},{1,3},{2,0},{3,1},{4,6},{5,7},{6,4},{7,5},{8,10},{9,11},{10,... | collective-permute-start | bytes 6152 | tf_op jit(solution)/shard_map/ppermute | solution.py:449
  28.8 1.2 %collective-permute-start.8 = (f32[2,256]{1,0:T(2,128)S(1)}, f32[2,256]{1,0:T(2,128)S(1)}, u32[]{:S(2)}, u32[]{:S(2)}) collective-permute-start(f32[2,256]{1,0:T(2,128)S(1)} %pad_maximum_fusion.after.rest_0_), channel_id=1, source_target_pairs={{0,3},{1,2},{2,1},{3,0},{4,7},{5,6},{6,5},{7,4},{8,11},{9,10},{10,... | collective-permute-start | bytes 6152 | tf_op jit(solution)/shard_map/ppermute | solution.py:449
  30.5 1.6 %collective-permute-done.9.rest_2_ = f32[2,256]{1,0:T(2,128)S(1)} collective-permute-done((f32[2,256]{1,0:T(2,128)S(1)}, f32[2,256]{1,0:T(2,128)S(1)}, u32[]{:S(2)}, u32[]{:S(2)}) %collective-permute-start.9) | collective-permute-done | bytes 2080 | tf_op jit(solution)/shard_map/ppermute | solution.py:449
  32.1 2.1 %collective-permute-done.8.rest_1_ = f32[2,256]{1,0:T(2,128)S(1)} collective-permute-done((f32[2,256]{1,0:T(2,128)S(1)}, f32[2,256]{1,0:T(2,128)S(1)}, u32[]{:S(2)}, u32[]{:S(2)}) %collective-permute-start.8) | collective-permute-done | bytes 2080 | tf_op jit(solution)/shard_map/ppermute | solution.py:449
  34.7 3.7 %collective-permute-done.11.edge_a = f32[3,16,128]{2,1,0:T(8,128)S(1)} collective-permute-done((f32[3,16,128]{2,1,0:T(8,128)S(1)}, f32[3,16,128]{2,1,0:T(8,128)S(1)}, u32[]{:S(2)}, u32[]{:S(2)}) %collective-permute-start.11) | collective-permute-done | bytes 24608 | tf_op jit(solution)/shard_map/ppermute | solution.py:417
  38.4 0.7 %shard_map.82 = (f32[128,128]{1,0:T(8,128)S(1)}, f32[1,256]{1,0:T(1,128)S(1)}, f32[1,256]{1,0:T(1,128)S(1)}) custom-call(f32[384,128]{1,0:T(8,128)S(1)} %get-tuple-element.30.slabs, f32[1,4,128,256]{3,2,1,0:T(8,128)S(1)} %copy-done, f32[1,4,128,256]{3,2,1,0:T(8,128)S(1)} %copy-done.1, f32[176,128]{1,0:T(8,128)S(1)} %collective-permute-done.2.got_a, ...), custom_call_target="tpu_custom_call" | custom-call | tf_op jit(solution)/shard_map/pallas_call | solution.py:384
  39.1 1.3 %collective-permute-done.13 = f32[1,256]{1,0:T(1,128)S(1)} collective-permute-done((f32[1,256]{1,0:T(1,128)S(1)}, f32[1,256]{1,0:T(1,128)S(1)}, u32[]{:S(2)}, u32[]{:S(2)}) %collective-permute-start.13) | collective-permute-done | bytes 1056 | tf_op jit(solution)/shard_map/ppermute | solution.py:476
  40.4 2.0 %collective-permute-start.16 = (f32[1,256]{1,0:T(1,128)S(1)}, f32[1,256]{1,0:T(1,128)S(1)}, u32[]{:S(2)}, u32[]{:S(2)}) collective-permute-start(f32[1,256]{1,0:T(1,128)S(1)} %add.26), channel_id=1, source_target_pairs={{0,1},{1,0},{2,3},{3,2},{4,5},{5,4},{6,7},{7,6},{8,9},{9,8},{10,11... | collective-permute-start | bytes 3080 | tf_op jit(solution)/shard_map/ppermute | solution.py:449
  42.6 2.2 %collective-permute-start.14 = (f32[1,256]{1,0:T(1,128)S(1)}, f32[1,256]{1,0:T(1,128)S(1)}, u32[]{:S(2)}, u32[]{:S(2)}) collective-permute-start(f32[1,256]{1,0:T(1,128)S(1)} %add.26), channel_id=1, source_target_pairs={{0,3},{1,2},{2,1},{3,0},{4,7},{5,6},{6,5},{7,4},{8,11},{9,10},{10,... | collective-permute-start | bytes 3080 | tf_op jit(solution)/shard_map/ppermute | solution.py:449
  44.8 2.1 %collective-permute-done.15 = f32[1,256]{1,0:T(1,128)S(1)} collective-permute-done((f32[1,256]{1,0:T(1,128)S(1)}, f32[1,256]{1,0:T(1,128)S(1)}, u32[]{:S(2)}, u32[]{:S(2)}) %collective-permute-start.15) | collective-permute-done | bytes 1056 | tf_op jit(solution)/shard_map/ppermute | solution.py:449
  46.9 1.1 %collective-permute-done.14 = f32[1,256]{1,0:T(1,128)S(1)} collective-permute-done((f32[1,256]{1,0:T(1,128)S(1)}, f32[1,256]{1,0:T(1,128)S(1)}, u32[]{:S(2)}, u32[]{:S(2)}) %collective-permute-start.14) | collective-permute-done | bytes 1056 | tf_op jit(solution)/shard_map/ppermute | solution.py:449
  48.0 0.6 %fusion = f32[1,64]{1,0:T(1,128)} fusion(f32[1,256]{1,0:T(1,128)S(1)} %get-tuple-element.43, s32[]{:T(128)S(6)} %select_n.3, f32[1,256]{1,0:T(1,128)S(1)} %collective-permute-done.16, f32[1,256]{1,0:T(1,128)S(1)} %collective-permute-done.15, f32[1,256]{1,0:T(1,128)S(1)} %collective-permute-done.14, f32[1,256]{1,0:T(1,128)S(1)} %add.26), kind=kLoop, calls=%fused_computation.6 | loop fusion | flops 320 | bytes 1540 | tf_op jit(solution)/shard_map/add | solution.py:477
  48.6 1.0 %shard_map.83 = f32[1,4,128,128]{3,2,1,0:T(8,128)S(1)} custom-call(f32[1,4,128,128]{3,2,1,0:T(8,128)S(1)} %get-tuple-element.24.src, f32[1,4,128,128]{3,2,1,0:T(8,128)S(1)} %get-tuple-element.25.tx, f32[1,4,128,128]{3,2,1,0:T(8,128)S(1)} %get-tuple-element.26.ty, f32[1,4,128,128]{3,2,1,0:T(8,128)S(1)} %get-tuple-element.27.tz, ...), custom_call_target="tpu_custom_call" | custom-call | tf_op jit(solution)/shard_map/pallas_call | solution.py:384
  49.6 0.7 %copy.8 = f32[1,4,128,128]{3,2,1,0:T(8,128)} copy(f32[1,4,128,128]{3,2,1,0:T(8,128)S(1)} %shard_map.83) | data formatting | bytes 524288
  (27 shorter events, 1.6 us)
Async XLA Ops:
  2.5 14.4 %copy-start = (f32[1,4,128,256]{3,2,1,0:T(8,128)S(1)}, f32[1,4,128,256]{3,2,1,0:T(8,128)}, u32[]{:S(2)}) copy-start(f32[1,4,128,256]{3,2,1,0:T(8,128)} %bot.5) | copy-start | bytes 1572868
  2.5 14.4 %copy-start.1 = (f32[1,4,128,256]{3,2,1,0:T(8,128)S(1)}, f32[1,4,128,256]{3,2,1,0:T(8,128)}, u32[]{:S(2)}) copy-start(f32[1,4,128,256]{3,2,1,0:T(8,128)} %top.5) | copy-start | bytes 1572868
  2.8 19.0 %collective-permute-start = (f32[6,128,128]{2,1,0:T(8,128)S(1)}, f32[6,128,128]{2,1,0:T(8,128)S(1)}, u32[]{:S(2)}, u32[]{:S(2)}) collective-permute-start(f32[6,128,128]{2,1,0:T(8,128)S(1)} %get-tuple-element.28), channel_id=1, source_target_pairs={{0,1},{1,0},{2,3},{3,2},{4,5},{5,4},{6,7},{7,6},{8,9},{9,8},{10,11... | collective-permute-start | bytes 1179656 | tf_op jit(solution)/shard_map/ppermute | solution.py:417
  5.9 15.8 %collective-permute-start.1 = (f32[6,128,128]{2,1,0:T(8,128)S(1)}, f32[6,128,128]{2,1,0:T(8,128)S(1)}, u32[]{:S(2)}, u32[]{:S(2)}) collective-permute-start(f32[6,128,128]{2,1,0:T(8,128)S(1)} %get-tuple-element.29), channel_id=1, source_target_pairs={{0,4},{1,2},{2,1},{3,7},{4,0},{5,6},{6,5},{7,3},{8,12},{9,10},{10,... | collective-permute-start | bytes 1179656 | tf_op jit(solution)/shard_map/ppermute | solution.py:418
  5.9 11.0 %collective-permute-start.2 = (f32[176,128]{1,0:T(8,128)S(1)}, f32[176,128]{1,0:T(8,128)S(1)}, u32[]{:S(2)}, u32[]{:S(2)}) collective-permute-start(f32[176,128]{1,0:T(8,128)S(1)} %get-tuple-element.31), channel_id=1, source_target_pairs={{0,1},{1,0},{2,3},{3,2},{4,5},{5,4},{6,7},{7,6},{8,9},{9,8},{10,11... | collective-permute-start | bytes 270344 | tf_op jit(solution)/shard_map/ppermute | solution.py:417
  9.0 7.9 %collective-permute-start.3 = (f32[176,128]{1,0:T(8,128)S(1)}, f32[176,128]{1,0:T(8,128)S(1)}, u32[]{:S(2)}, u32[]{:S(2)}) collective-permute-start(f32[176,128]{1,0:T(8,128)S(1)} %get-tuple-element.32), channel_id=1, source_target_pairs={{0,4},{1,2},{2,1},{3,7},{4,0},{5,6},{6,5},{7,3},{8,12},{9,10},{10,... | collective-permute-start | bytes 270344 | tf_op jit(solution)/shard_map/ppermute | solution.py:418
  17.6 2.8 %collective-permute-start.4 = (f32[1,256]{1,0:T(1,128)S(1)}, f32[1,256]{1,0:T(1,128)S(1)}, u32[]{:S(2)}, u32[]{:S(2)}) collective-permute-start(f32[1,256]{1,0:T(1,128)S(1)} %get-tuple-element.33), channel_id=1, source_target_pairs={{0,4},{4,0},{8,12},{12,8},{16,20},{20,16},{24,28},{28,24},{1,5},{5... | collective-permute-start | bytes 3080 | tf_op jit(solution)/shard_map/ppermute | solution.py:452
  17.7 4.0 %collective-permute-start.5 = (f32[1,256]{1,0:T(1,128)S(1)}, f32[1,256]{1,0:T(1,128)S(1)}, u32[]{:S(2)}, u32[]{:S(2)}) collective-permute-start(f32[1,256]{1,0:T(1,128)S(1)} %get-tuple-element.34), channel_id=1, source_target_pairs={{0,28},{4,8},{8,4},{12,16},{16,12},{20,24},{24,20},{28,0},{1,29},{... | collective-permute-start | bytes 3080 | tf_op jit(solution)/shard_map/ppermute | solution.py:453
  22.7 25.9 %collective-permute-start.6 = (f32[3,128,128]{2,1,0:T(8,128)S(1)}, f32[3,128,128]{2,1,0:T(8,128)S(1)}, u32[]{:S(2)}, u32[]{:S(2)}) collective-permute-start(f32[3,128,128]{2,1,0:T(8,128)S(1)} %get-tuple-element.36), channel_id=1, source_target_pairs={{0,1},{1,0},{2,3},{3,2},{4,5},{5,4},{6,7},{7,6},{8,9},{9,8},{10,11... | collective-permute-start | bytes 589832 | tf_op jit(solution)/shard_map/ppermute | solution.py:417
  25.5 23.0 %collective-permute-start.7 = (f32[3,128,128]{2,1,0:T(8,128)S(1)}, f32[3,128,128]{2,1,0:T(8,128)S(1)}, u32[]{:S(2)}, u32[]{:S(2)}) collective-permute-start(f32[3,128,128]{2,1,0:T(8,128)S(1)} %get-tuple-element.37), channel_id=1, source_target_pairs={{0,4},{1,2},{2,1},{3,7},{4,0},{5,6},{6,5},{7,3},{8,12},{9,10},{10,... | collective-permute-start | bytes 589832 | tf_op jit(solution)/shard_map/ppermute | solution.py:418
  25.5 4.9 %collective-permute-start.10 = (f32[2,256]{1,0:T(2,128)S(1)}, f32[2,256]{1,0:T(2,128)S(1)}, u32[]{:S(2)}, u32[]{:S(2)}) collective-permute-start(f32[2,256]{1,0:T(2,128)S(1)} %pad_maximum_fusion.after.rest_0_), channel_id=1, source_target_pairs={{0,1},{1,0},{2,3},{3,2},{4,5},{5,4},{6,7},{7,6},{8,9},{9,8},{10,11... | collective-permute-start | bytes 6152 | tf_op jit(solution)/shard_map/ppermute | solution.py:449
  27.6 4.5 %collective-permute-start.9 = (f32[2,256]{1,0:T(2,128)S(1)}, f32[2,256]{1,0:T(2,128)S(1)}, u32[]{:S(2)}, u32[]{:S(2)}) collective-permute-start(f32[2,256]{1,0:T(2,128)S(1)} %pad_maximum_fusion.after.rest_0_), channel_id=1, source_target_pairs={{0,2},{1,3},{2,0},{3,1},{4,6},{5,7},{6,4},{7,5},{8,10},{9,11},{10,... | collective-permute-start | bytes 6152 | tf_op jit(solution)/shard_map/ppermute | solution.py:449
  28.8 5.4 %collective-permute-start.8 = (f32[2,256]{1,0:T(2,128)S(1)}, f32[2,256]{1,0:T(2,128)S(1)}, u32[]{:S(2)}, u32[]{:S(2)}) collective-permute-start(f32[2,256]{1,0:T(2,128)S(1)} %pad_maximum_fusion.after.rest_0_), channel_id=1, source_target_pairs={{0,3},{1,2},{2,1},{3,0},{4,7},{5,6},{6,5},{7,4},{8,11},{9,10},{10,... | collective-permute-start | bytes 6152 | tf_op jit(solution)/shard_map/ppermute | solution.py:449
  34.5 3.9 %collective-permute-start.11 = (f32[3,16,128]{2,1,0:T(8,128)S(1)}, f32[3,16,128]{2,1,0:T(8,128)S(1)}, u32[]{:S(2)}, u32[]{:S(2)}) collective-permute-start(f32[3,16,128]{2,1,0:T(8,128)S(1)} %get-tuple-element.40), channel_id=1, source_target_pairs={{0,1},{1,0},{2,3},{3,2},{4,5},{5,4},{6,7},{7,6},{8,9},{9,8},{10,11... | collective-permute-start | bytes 73736 | tf_op jit(solution)/shard_map/ppermute | solution.py:417
  34.6 3.8 %collective-permute-start.12 = (f32[3,16,128]{2,1,0:T(8,128)S(1)}, f32[3,16,128]{2,1,0:T(8,128)S(1)}, u32[]{:S(2)}, u32[]{:S(2)}) collective-permute-start(f32[3,16,128]{2,1,0:T(8,128)S(1)} %get-tuple-element.41), channel_id=1, source_target_pairs={{0,4},{1,2},{2,1},{3,7},{4,0},{5,6},{6,5},{7,3},{8,12},{9,10},{10,... | collective-permute-start | bytes 73736 | tf_op jit(solution)/shard_map/ppermute | solution.py:418
  39.1 1.4 %collective-permute-start.13 = (f32[1,256]{1,0:T(1,128)S(1)}, f32[1,256]{1,0:T(1,128)S(1)}, u32[]{:S(2)}, u32[]{:S(2)}) collective-permute-start(f32[1,256]{1,0:T(1,128)S(1)} %get-tuple-element.45), channel_id=1, source_target_pairs={{4,0},{8,4},{12,8},{16,12},{20,16},{24,20},{28,24},{0,28},{5,1},{9... | collective-permute-start | bytes 3080 | tf_op jit(solution)/shard_map/ppermute | solution.py:476
  40.4 4.4 %collective-permute-start.16 = (f32[1,256]{1,0:T(1,128)S(1)}, f32[1,256]{1,0:T(1,128)S(1)}, u32[]{:S(2)}, u32[]{:S(2)}) collective-permute-start(f32[1,256]{1,0:T(1,128)S(1)} %add.26), channel_id=1, source_target_pairs={{0,1},{1,0},{2,3},{3,2},{4,5},{5,4},{6,7},{7,6},{8,9},{9,8},{10,11... | collective-permute-start | bytes 3080 | tf_op jit(solution)/shard_map/ppermute | solution.py:449
  42.4 4.5 %collective-permute-start.15 = (f32[1,256]{1,0:T(1,128)S(1)}, f32[1,256]{1,0:T(1,128)S(1)}, u32[]{:S(2)}, u32[]{:S(2)}) collective-permute-start(f32[1,256]{1,0:T(1,128)S(1)} %add.26), channel_id=1, source_target_pairs={{0,2},{1,3},{2,0},{3,1},{4,6},{5,7},{6,4},{7,5},{8,10},{9,11},{10,... | collective-permute-start | bytes 3080 | tf_op jit(solution)/shard_map/ppermute | solution.py:449
  42.6 5.4 %collective-permute-start.14 = (f32[1,256]{1,0:T(1,128)S(1)}, f32[1,256]{1,0:T(1,128)S(1)}, u32[]{:S(2)}, u32[]{:S(2)}) collective-permute-start(f32[1,256]{1,0:T(1,128)S(1)} %add.26), channel_id=1, source_target_pairs={{0,3},{1,2},{2,1},{3,0},{4,7},{5,6},{6,5},{7,4},{8,11},{9,10},{10,... | collective-permute-start | bytes 3080 | tf_op jit(solution)/shard_map/ppermute | solution.py:449
where the time goes:
time: 50.5 us; the launch traced here: 50.3 us
  waiting for transfers between devices  21.6 us (43%)
  starting transfers between devices  20.9 us (41%)
  Pallas kernels  5.74 us (11%)
  between operations  0.76 us (2%)
  local copies, waits for them, and re-layouts  0.72 us (1%)
  other arithmetic  0.61 us (1%)
    ppermute x4, waiting for transfers between devices, trade(): first = lax.ppermute(a, names, pair_one)  11.6 us
    ppermute x4, starting transfers between devices, trade(): first = lax.ppermute(a, names, pair_one)  9.21 us
    ppermute x6, starting transfers between devices, everyone(): parts.append(lax.ppermute(value, 'sub', [(i, i ^ k) for i in range(subs)]))  8.79 us
    ppermute x6, waiting for transfers between devices, everyone(): parts.append(lax.ppermute(value, 'sub', [(i, i ^ k) for i in range(subs)]))  7.38 us
    pallas_call x7, Pallas kernels, call(): pl.pallas_call(kernel, out_shape=[pltpu.VMEM(shape, F32) for shape in out...  5.74 us
    ppermute x1, starting transfers between devices, work(): other_b = lax.ppermute(share_b, 'block', block_two)  2.71 us
    ppermute x1, waiting for transfers between devices, work(): other_b = lax.ppermute(share_b, 'block', block_two)  1.29 us
    ppermute x1, waiting for transfers between devices, work(): lax.ppermute(cbot, 'block', [((b + 1) % blocks, b) for b in range(blocks)])  1.29 us
  transfers between devices with their start and end apart: 17, of which 9 were waited for; matrix products, arithmetic and copies ran while one was open for 1% of the time, Pallas kernels for 3%

commit v1 on v0

v1 whole, which is shorter than its diff:
```python
import jax
import jax.numpy as jnp
from jax import lax
from jax.experimental import pallas as pl
from jax.experimental.pallas import tpu as pltpu
from jax.sharding import PartitionSpec as P


PASSES = 3
RELAX = 0.8
KEEP = 1.0 - RELAX
MORTAR_STEP = 0.05
F32 = jnp.float32
EDGE = 6
MIDDLE = 3
HALO = 2
SLAB = 8
SPAN = 2 * SLAB
DIRECT = 4
ITEMS = 5


def prev(v, axis):
    return pltpu.roll(v, 1, axis)


def following(v, axis):
    return pltpu.roll(v, v.shape[axis] - 1, axis)


class Layer:
    def __init__(self, trans_y, trans_z, has_bot, has_top):
        rows = lax.broadcasted_iota(jnp.int32, trans_y.shape, 0)
        self.cy = jnp.where(rows > 0, trans_y, 0.0)
        self.cz, self.zsum = along_z(trans_z, has_bot, has_top)
        self.diag = self.cy + following(self.cy, 0) + self.zsum

    def around(self, p):
        return (
            self.cy * prev(p, 0)
            + following(self.cy * p, 0)
            + self.cz * prev(p, 1)
            + following(self.cz * p, 1)
        )


def along_z(trans_z, has_bot, has_top):
    cols = lax.broadcasted_iota(jnp.int32, trans_z.shape, 1)
    first = cols == 0
    last = cols == trans_z.shape[1] - 1
    cz = jnp.where(first, 0.0, trans_z)
    ends = jnp.where(first, trans_z * has_bot, jnp.where(last, trans_z * has_top, 0.0))
    return cz, cz + following(cz, 1) + ends


class Thin:
    def __init__(self, trans_y, trans_z, zsum, live):
        rows = lax.broadcasted_iota(jnp.int32, trans_y.shape, 0)
        cols = lax.broadcasted_iota(jnp.int32, trans_y.shape, 1)
        self.cy = jnp.where(cols > 0, trans_y, 0.0)
        self.cz = jnp.where(rows == SLAB, 0.0, trans_z)
        self.face = jnp.where((rows == SLAB) | (rows == SLAB - 1), trans_z, 0.0) * live
        self.diag = self.cy + following(self.cy, 1) + zsum

    def around(self, p):
        return (
            self.cy * prev(p, 1)
            + following(self.cy * p, 1)
            + self.cz * prev(p, 0)
            + following(self.cz * p, 0)
        )


def flags():
    block = lax.axis_index("block")
    sub = lax.axis_index("sub")
    has_bot = (block > 0).astype(F32)
    has_top = (block < lax.axis_size("block") - 1).astype(F32)
    has_below = (sub > 0).astype(F32)
    has_above = (sub < lax.axis_size("sub") - 1).astype(F32)
    return has_bot, has_top, has_below, has_above


def by_parity(axis, first, second, upward, downward):
    even = lax.rem(lax.axis_index(axis), 2) == 0

    @pl.when(even)
    def _():
        upward(first)
        downward(second)

    @pl.when(jnp.logical_not(even))
    def _():
        upward(second)
        downward(first)


def sort_pair(pair, above, below):
    def take_above(ref):
        above[...] = ref[...]

    def take_below(ref):
        below[...] = ref[...]

    by_parity("sub", *pair, take_above, take_below)


def pack_kernel(src, tx, ty, tz, src_v, tx_v, ty_v, tz_v, slabs, firsts, sems):
    copies = [
        pltpu.make_async_copy(here, there, sems.at[i])
        for i, (here, there) in enumerate(
            ((tz, tz_v), (src, src_v), (tx, tx_v), (ty, ty_v))
        )
    ]
    for copy in copies:
        copy.start()
    for copy in copies:
        copy.wait()
    count, rows, cells = src_v.shape[1:]
    has_bot, has_top, _, _ = flags()
    items = []
    for x in range(count):
        zsum = along_z(tz_v[0, x], has_bot, has_top)[1]
        items += [tx_v[0, x], src_v[0, x], ty_v[0, x], tz_v[0, x], zsum]
    slot = lax.broadcasted_iota(jnp.int32, (rows, cells), 1) // SPAN
    each = cells // SPAN
    for start in range(0, len(items), each):
        packed = jnp.zeros((rows, cells), F32)
        here = items[start : start + each]
        for j, item in enumerate(here):
            turned = pltpu.roll(item, (SPAN * j + SLAB) % cells, 1)
            packed = jnp.where(slot == j, turned, packed)
        turned = packed.T
        for j in range(len(here)):
            k = start + j
            slabs[k] = turned[j * SPAN : (j + 1) * SPAN]
            firsts[k] = turned[j * SPAN + SLAB : (j + 1) * SPAN]


def edge_parts(items, make, has_below):
    tx, src = (lambda x: items(0, x)), (lambda x: items(1, x))
    low = make(0)
    w_low = RELAX / (low.diag + tx(0) * has_below + tx(1))
    p_low = w_low * src(0)
    p_next = RELAX * src(1) / (make(1).diag + tx(1) + tx(2))
    q_low = KEEP * p_low + w_low * (src(0) + tx(1) * p_next + low.around(p_low))
    return p_low, q_low, w_low


def first_three(count, source, cx, layers, w, above, below):
    p1 = {x: w[x] * source[x] for x in range(-1, count)}
    p1[-2] = below[1]
    p1[count] = above[1]
    p2 = thin_pass(p1, source, cx, layers, w, -1, count)
    p2[count] = above[2] + above[3] * cx[count] * p1[count - 1]
    return thin_pass(p2, source, cx, layers, w, 0, count)


def join_kernel(slabs, firsts, joined, out_a, out_b):
    for k in range(firsts.shape[0]):
        joined[k, 0:SLAB] = slabs[k, 0:SLAB]
        joined[k, SLAB:SPAN] = firsts[k]
    count = firsts.shape[0] // ITEMS
    _, live, has_below, _ = flags()

    def item(which, x):
        return joined[x * ITEMS + which]

    def make(x):
        return Thin(item(2, x), item(3, x), item(4, x), live)

    p_low, q_low, w_low = edge_parts(item, make, has_below)
    top = count - 1
    p_top = RELAX * item(1, top - 1) / (make(top - 1).diag + item(0, top - 1) + item(0, top))

    def upward(ref):
        values = (item(0, top), p_top, item(1, top), item(4, top), item(2, top), item(3, top))
        for i, v in enumerate(values):
            ref[i] = v

    def downward(ref):
        values = (item(0, 0), p_low, q_low, w_low, item(2, 0), item(3, 0))
        for i, v in enumerate(values):
            ref[i] = v

    by_parity("sub", out_a, out_b, upward, downward)


def thin_setup(joined, above, below):
    count = joined.shape[0] // ITEMS
    _, live, has_below, has_above = flags()
    cx = {x: joined[x * ITEMS] for x in range(1, count)}
    cx[-1] = below[0]
    cx[0] = joined[0] * has_below
    cx[count] = above[0] * has_above
    source = {x: joined[x * ITEMS + 1] for x in range(count)}
    source[-1] = below[2]
    layers = {
        x: Thin(*(joined[x * ITEMS + i] for i in (2, 3, 4)), live) for x in range(count)
    }
    layers[-1] = Thin(below[4], below[5], below[3], live)
    layers[count] = Thin(above[4], above[5], above[3], live)
    w = {x: RELAX / (layers[x].diag + cx[x] + cx[x + 1]) for x in range(-1, count)}
    w[count] = above[3]
    return source, cx, layers, w


def thin_pass(p, rhs, cx, layers, weight, low, high):
    return {
        x: KEEP * p[x]
        + weight[x] * (rhs[x] + cx[x] * p[x - 1] + cx[x + 1] * p[x + 1] + layers[x].around(p[x]))
        for x in range(low, high)
    }


def edge_data(ref, p, x, beyond, link, rhs, cx, layers, weight):
    ref[0] = p[x]
    ref[1] = KEEP * p[x] + weight[x] * (rhs[x] + link * p[beyond] + layers[x].around(p[x]))
    step = thin_pass(p, rhs, cx, layers, weight, beyond, beyond + 1)
    ref[2] = rhs[x] + link * step[beyond]


def three_passes(p, above, below, rhs, cx, layers, weight, count):
    sides = ((count, count - 1, cx[count], above), (-1, 0, cx[0], below))
    for x, _, _, got in sides:
        p[x] = got[0]
    after = thin_pass(p, rhs, cx, layers, weight, 0, count)
    for x, near, link, got in sides:
        after[x] = got[1] + weight[x] * link * p[near]
    last = thin_pass(after, rhs, cx, layers, weight, 0, count)
    for x, near, link, got in sides:
        last[x] = KEEP * after[x] + weight[x] * (
            got[2] + link * after[near] + layers[x].around(after[x])
        )
    return thin_pass(last, rhs, cx, layers, weight, 0, count)


def traces(flux, bot, top, rows):
    count = len(flux)
    stacked = [f[SLAB : SLAB + 1] for f in flux] + [f[SLAB - 1 : SLAB] for f in flux]
    stacked.append(jnp.zeros((rows - len(stacked), flux[0].shape[1]), F32))
    columns = jnp.concatenate(stacked, axis=0).T
    total = sum(
        columns[:, face * count + x : face * count + x + 1] * basis[0, x]
        for face, basis in enumerate((bot, top))
        for x in range(count)
    )
    return jnp.sum(total, axis=0, keepdims=True)


def first_thin(joined, bot, top, got_a, got_b, p_out, share, above, below):
    count, rows = bot.shape[1:3]
    sort_pair((got_a, got_b), above, below)
    source, cx, layers, w = thin_setup(joined, above, below)
    p = first_three(count, source, cx, layers, w, above, below)
    for x in range(count):
        p_out[x] = p[x]
    flux = [layers[x].face * p[x] for x in range(count)]
    share[...] = traces(flux, bot, top, rows)


def with_faces(source, layers, data, count):
    known = {}
    for x in range(count):
        planes = lax.broadcasted_iota(jnp.int32, source[x].shape, 0)
        known[x] = jnp.where(planes == SLAB, data[x : x + 1], data[count + x : count + x + 1])
    return known, {x: source[x] + layers[x].face * known[x] for x in range(count)}


def face_kernel(joined, bot, top, got_a, got_b, p_in, *rest):
    parts = rest[:-6]
    data_out, edge_a, edge_b, mortar_out, above, below = rest[-6:]
    count, rows = bot.shape[1:3]
    sort_pair((got_a, got_b), above, below)
    mortar = MORTAR_STEP * sum(part[...] for part in parts)
    mortar_out[...] = mortar
    lanes = lax.broadcasted_iota(jnp.int32, (rows, rows), 1)
    columns = jnp.zeros((rows, rows), F32)
    for face, ref in enumerate((bot, top)):
        for x in range(count):
            data = jnp.sum(ref[0, x] * mortar, axis=1, keepdims=True)
            columns = jnp.where(lanes == face * count + x, data, columns)
    data = columns.T[0 : 2 * count]
    data_out[...] = data
    source, cx, layers, w = thin_setup(joined, above, below)
    rhs = with_faces(source, layers, data, count)[1]
    p = {x: p_in[x] for x in range(count)}
    last = count - 1
    by_parity(
        "sub",
        edge_a,
        edge_b,
        lambda ref: edge_data(ref, p, last, last - 1, cx[last], rhs, cx, layers, w),
        lambda ref: edge_data(ref, p, 0, 1, cx[1], rhs, cx, layers, w),
    )


def second_thin(
    joined, bot, top, got_a, got_b, p_in, data, edge_a, edge_b,
    lasts, firsts, share, above, below, edge_above, edge_below,
):
    count, rows = bot.shape[1:3]
    sort_pair((got_a, got_b), above, below)
    sort_pair((edge_a, edge_b), edge_above, edge_below)
    source, cx, layers, w = thin_setup(joined, above, below)
    known, rhs = with_faces(source, layers, data, count)
    p = {x: p_in[x] for x in range(count)}
    p = three_passes(p, edge_above, edge_below, rhs, cx, layers, w, count)
    for x in range(count):
        lasts[x] = p[x][0:SLAB]
        firsts[x] = p[x][SLAB:SPAN]
    flux = [layers[x].face * (p[x] - known[x]) for x in range(count)]
    share[...] = traces(flux, bot, top, rows)


def edge_kernel(src, tx, ty, tz, out_a, out_b):
    count = src.shape[1]
    has_bot, has_top, has_below, _ = flags()

    def make(x):
        return Layer(ty[0, x], tz[0, x], has_bot, has_top)

    p_low, q_low, w_low = edge_parts(lambda which, x: (tx, src)[which][0, x], make, has_below)
    top = count - 1
    p_top = RELAX * src[0, top - 1] / (make(top - 1).diag + tx[0, top - 1] + tx[0, top])

    def upward(ref):
        for i, v in enumerate((tx[0, top], p_top, src[0, top], src[0, top], ty[0, top], tz[0, top])):
            ref[i] = v

    def downward(ref):
        for i, v in enumerate((tx[0, 0], p_low, q_low, w_low, ty[0, 0], tz[0, 0])):
            ref[i] = v

    by_parity("sub", out_a, out_b, upward, downward)


def whole_setup(src, tx, ty, tz, above, below):
    count = src.shape[1]
    has_bot, has_top, has_below, has_above = flags()
    cx = {x: tx[0, x] for x in range(1, count)}
    cx[-1] = below[0]
    cx[0] = tx[0, 0] * has_below
    cx[count] = above[0] * has_above
    source = {x: src[0, x] for x in range(count)}
    source[-1] = below[2]
    layers = {x: Layer(ty[0, x], tz[0, x], has_bot, has_top) for x in range(count)}
    layers[-1] = Layer(below[4], below[5], has_bot, has_top)
    weight = {x: RELAX / (layers[x].diag + cx[x] + cx[x + 1]) for x in range(-1, count)}
    return source, cx, layers, weight


def first_whole(src, tx, ty, tz, got_a, got_b, after, p_out, mid_a, mid_b, above, below):
    count = src.shape[1]
    sort_pair((got_a, got_b), above, below)
    source, cx, layers, w = whole_setup(src, tx, ty, tz, above, below)
    p3 = first_three(count, source, cx, layers, w, above, below)
    for x in range(count):
        p_out[x] = p3[x]
    last = count - 1
    by_parity(
        "sub",
        mid_a,
        mid_b,
        lambda ref: edge_data(ref, p3, last, last - 1, cx[last], source, cx, layers, w),
        lambda ref: edge_data(ref, p3, 0, 1, cx[1], source, cx, layers, w),
    )


def second_whole(src, tx, ty, tz, got_a, got_b, p_in, mid_a, mid_b, p_out, above, below, p_above, p_below):
    count = src.shape[1]
    sort_pair((got_a, got_b), above, below)
    sort_pair((mid_a, mid_b), p_above, p_below)
    source, cx, layers, w = whole_setup(src, tx, ty, tz, above, below)
    has_bot, has_top, _, _ = flags()
    layers[count] = Layer(above[4], above[5], has_bot, has_top)
    w[count] = above[3]
    p3 = {x: p_in[x] for x in range(count)}
    p6 = three_passes(p3, p_above, p_below, source, cx, layers, w, count)
    for x in range(count):
        p_out[x] = p6[x]


def merge_kernel(whole, lasts, firsts, p_out):
    count, rows, cells = whole.shape
    cols = lax.broadcasted_iota(jnp.int32, (rows, cells), 1)
    face = (cols < PASSES) | (cols >= cells - PASSES)
    each = cells // SPAN
    for start in range(0, count, each):
        stop = min(start + each, count)
        here = [part[x] for x in range(start, stop) for part in (lasts, firsts)]
        if (stop - start) * SPAN < cells:
            here.append(jnp.zeros((cells - (stop - start) * SPAN, rows), F32))
        back = jnp.concatenate(here, axis=0).T
        for x in range(start, stop):
            shift = (cells - (x - start) * SPAN - SLAB) % cells
            p_out[0, x] = jnp.where(face, pltpu.roll(back, shift, 1), whole[x])


def call(kernel, outs, args, scratch=(), copies=0):
    space = pltpu.HBM if copies else pltpu.VMEM
    args = [pltpu.with_memory_space_constraint(a, space) for a in args]
    return pl.pallas_call(
        kernel,
        out_shape=[pltpu.VMEM(shape, F32) for shape in outs],
        in_specs=[pl.BlockSpec(memory_space=space)] * len(args),
        out_specs=[pl.BlockSpec(memory_space=pltpu.VMEM)] * len(outs),
        scratch_shapes=[pltpu.VMEM(shape, F32) for shape in scratch]
        + ([pltpu.SemaphoreType.DMA((copies,))] if copies else []),
        compiler_params=pltpu.CompilerParams(vmem_limit_bytes=16 << 20),
    )(*args)


def sub_swaps(blocks, subs):
    flat = lambda b, s: b * subs + s
    first = [(flat(b, s), flat(b, s ^ 1)) for b in range(blocks) for s in range(subs)]
    second = []
    for b in range(blocks):
        for s in range(subs):
            other = s + 1 if s % 2 else s - 1
            inside = 0 <= other < subs
            second.append((flat(b, s), flat(b, other) if inside else flat(b ^ 1, s)))
    return first, second


def work(source, trans_x, trans_y, trans_z, mortar_bot, mortar_top):
    count, rows, cells = source.shape[1:]
    width = mortar_bot.shape[3]
    subs = lax.axis_size("sub")
    blocks = lax.axis_size("block")
    assert subs % 2 == 0 and blocks % 2 == 0 and count > HALO
    names = ("block", "sub")
    pair_one, pair_two = sub_swaps(blocks, subs)

    def trade(a, b):
        first = lax.ppermute(a, names, pair_one)
        return first, lax.ppermute(b, names, pair_two)

    face = (rows, cells)
    kept = count * ITEMS
    slab = (SPAN, rows)
    half = (SLAB, rows)
    up = [(b, (b + 1) % blocks) for b in range(blocks)]
    down = [(b, a) for a, b in up]

    def everyone(value):
        if subs > DIRECT:
            return [lax.psum(value, "sub")]
        parts = [value]
        for k in range(subs - 1, 0, -1):
            parts.append(lax.ppermute(value, "sub", [(i, i ^ k) for i in range(subs)]))
        return parts

    *coeffs, slabs, firsts = call(
        pack_kernel,
        [source.shape] * 4 + [(kept,) + slab, (kept,) + half],
        (source, trans_x, trans_y, trans_z),
        copies=4,
    )
    firsts = lax.ppermute(firsts, "block", down)
    basis = lax.ppermute(mortar_bot, "block", down)
    joined, near_a, near_b = call(
        join_kernel, [(kept,) + slab] + [(EDGE,) + slab] * 2, (slabs, firsts)
    )
    near = trade(near_a, near_b)
    edges = call(edge_kernel, [(EDGE,) + face] * 2, coeffs)
    edges = trade(*edges)
    fixed = (joined, basis, mortar_top) + near
    sides = [(EDGE,) + slab] * 2
    third, share = call(first_thin, [(count,) + slab, (1, width)], fixed, sides)
    parts = everyone(share)
    whole, mid_a, mid_b = call(
        first_whole,
        [(count,) + face] + [(MIDDLE,) + face] * 2,
        tuple(coeffs) + edges + (share,),
        [(EDGE,) + face] * 2,
    )
    middle = trade(mid_a, mid_b)
    data, edge_a, edge_b, mortar = call(
        face_kernel,
        [(2 * count, rows)] + [(MIDDLE,) + slab] * 2 + [(1, width)],
        fixed + (third,) + tuple(parts),
        sides,
    )
    got = trade(edge_a, edge_b)
    lasts, firsts, share = call(
        second_thin,
        [(count,) + half] * 2 + [(1, width)],
        fixed + (third, data) + got,
        sides + [(MIDDLE,) + slab] * 2,
    )
    total = mortar + MORTAR_STEP * sum(everyone(share))
    columns = width // subs
    final = lax.dynamic_slice_in_dim(total[0], lax.axis_index("sub") * columns, columns, 0)
    firsts = lax.ppermute(firsts, "block", up)
    (whole,) = call(
        second_whole,
        [(count,) + face],
        tuple(coeffs) + edges + (whole,) + middle,
        [(EDGE,) + face] * 2 + [(MIDDLE,) + face] * 2,
    )
    (pressure,) = call(merge_kernel, [source.shape], (whole, lasts, firsts))
    return pressure, final[None]


def solution(mesh):
    spec = P("block", "sub", None, None)
    return jax.shard_map(
        work,
        mesh=mesh,
        in_specs=(spec,) * 6,
        out_specs=(spec, P("block", "sub")),
        check_vma=False,
    )
```

time: 50.5 us -> 44.8 us (0.89)
  waiting for transfers between devices: 21.6 us -> 17.3 us
  starting transfers between devices: 20.9 us -> 19.4 us
    ppermute x4, waiting for transfers between devices: 11.6 us -> 6.82 us  [trade(): first = lax.ppermute(a, names, pair_one)]
    ppermute x4, starting transfers between devices: 9.21 us -> 6.28 us  [trade(): first = lax.ppermute(a, names, pair_one)]
    ppermute x3, starting transfers between devices: 2.84 us -> 4.11 us  [the longest x1 3.41 us: work(): basis = lax.ppermute(mortar_bot, 'block', down)]
    ppermute x3, waiting for transfers between devices: 2.59 us -> 3.38 us  [the longest x1 3.37 us: work(): firsts = lax.ppermute(firsts, 'block', down)]
    pallas_call x7 -> x9, Pallas kernels: 5.74 us -> 5.93 us  [call(): pl.pallas_call(kernel, out_shape=[pltpu.VMEM(shape, F32) for shape in out...]
  transfers between devices with their start and end apart: 17 -> 17, of which waited for: 9 -> 7; matrix products, arithmetic and copies ran while one was open for 1% -> 1% of each run, Pallas kernels for 3% -> 11%
where the time goes in v1:
time: 44.8 us; the launch traced here: 44.7 us
  starting transfers between devices  19.4 us (43%)
  waiting for transfers between devices  17.3 us (39%)
  Pallas kernels  5.93 us (13%)
  between operations  0.75 us (2%)
  local copies, waits for them, and re-layouts  0.71 us (2%)
  other arithmetic  0.59 us (1%)
    ppermute x6, starting transfers between devices, everyone(): parts.append(lax.ppermute(value, 'sub', [(i, i ^ k) for i in range(subs)]))  8.93 us
    ppermute x6, waiting for transfers between devices, everyone(): parts.append(lax.ppermute(value, 'sub', [(i, i ^ k) for i in range(subs)]))  7.1 us
    ppermute x4, waiting for transfers between devices, trade(): first = lax.ppermute(a, names, pair_one)  6.82 us
    ppermute x4, starting transfers between devices, trade(): first = lax.ppermute(a, names, pair_one)  6.28 us
    pallas_call x9, Pallas kernels, call(): pl.pallas_call(kernel, out_shape=[pltpu.VMEM(shape, F32) for shape in out...  5.93 us
    ppermute x1, starting transfers between devices, work(): basis = lax.ppermute(mortar_bot, 'block', down)  3.41 us
    ppermute x1, waiting for transfers between devices, work(): firsts = lax.ppermute(firsts, 'block', down)  3.37 us
  transfers between devices with their start and end apart: 17, of which 7 were waited for; matrix products, arithmetic and copies ran while one was open for 1% of the time, Pallas kernels for 11%

profile of v1, /device:TPU:0, one launch (start us, length us, event | category | flops | bytes accessed | tf_op | source)
XLA Modules:
  0.0 44.7 jit_solution(10999277304966977761)
XLA Ops:
  0.6 3.4 %collective-permute-start.3 = (f32[1,4,128,256]{3,2,1,0:T(8,128)}, f32[1,4,128,256]{3,2,1,0:T(8,128)S(1)}, u32[]{:S(2)}, u32[]{:S(2)}) collective-permute-start(f32[1,4,128,256]{3,2,1,0:T(8,128)} %param.10), channel_id=1, source_target_pairs={{4,0},{8,4},{12,8},{16,12},{20,16},{24,20},{28,24},{0,28},{5,1},{9... | collective-permute-start | bytes 1572872 | tf_op jit(solution)/shard_map/ppermute | solution.py:461
  4.0 1.8 %shard_map.77 = (f32[1,4,128,128]{3,2,1,0:T(8,128)S(1)}, f32[1,4,128,128]{3,2,1,0:T(8,128)S(1)}, f32[1,4,128,128]{3,2,1,0:T(8,128)S(1)}, f32[1,4,128,128]{3,2,1,...) custom-call(f32[1,4,128,128]{3,2,1,0:T(8,128)} %src.1, f32[1,4,128,128]{3,2,1,0:T(8,128)} %tx.1, ...), custom_call_target="tpu_custom_call" | custom-call | tf_op jit(solution)/shard_map/pallas_call | solution.py:403
  6.1 1.6 %collective-permute-start = (f32[6,128,128]{2,1,0:T(8,128)S(1)}, f32[6,128,128]{2,1,0:T(8,128)S(1)}, u32[]{:S(2)}, u32[]{:S(2)}) collective-permute-start(f32[6,128,128]{2,1,0:T(8,128)S(1)} %get-tuple-element.29), channel_id=1, source_target_pairs={{0,1},{1,0},{2,3},{3,2},{4,5},{5,4},{6,7},{7,6},{8,9},{9,8},{10,11... | collective-permute-start | bytes 1179656 | tf_op jit(solution)/shard_map/ppermute | solution.py:436
  7.8 0.7 %collective-permute-start.2 = (f32[20,8,128]{2,1,0:T(8,128)S(1)}, f32[20,8,128]{2,1,0:T(8,128)S(1)}, u32[]{:S(2)}, u32[]{:S(2)}) collective-permute-start(f32[20,8,128]{2,1,0:T(8,128)S(1)} %get-tuple-element.32), channel_id=1, source_target_pairs={{4,0},{8,4},{12,8},{16,12},{20,16},{24,20},{28,24},{0,28},{5,1},{9... | collective-permute-start | bytes 245768 | tf_op jit(solution)/shard_map/ppermute | solution.py:460
  8.5 3.4 %collective-permute-done.2.firsts = f32[20,8,128]{2,1,0:T(8,128)S(1)} collective-permute-done((f32[20,8,128]{2,1,0:T(8,128)S(1)}, f32[20,8,128]{2,1,0:T(8,128)S(1)}, u32[]{:S(2)}, u32[]{:S(2)}) %collective-permute-start.2) | collective-permute-done | bytes 81952 | tf_op jit(solution)/shard_map/ppermute | solution.py:460
  12.0 1.7 %collective-permute-start.4 = (f32[6,16,128]{2,1,0:T(8,128)S(1)}, f32[6,16,128]{2,1,0:T(8,128)S(1)}, u32[]{:S(2)}, u32[]{:S(2)}) collective-permute-start(f32[6,16,128]{2,1,0:T(8,128)S(1)} %get-tuple-element.34), channel_id=1, source_target_pairs={{0,1},{1,0},{2,3},{3,2},{4,5},{5,4},{6,7},{7,6},{8,9},{9,8},{10,11... | collective-permute-start | bytes 147464 | tf_op jit(solution)/shard_map/ppermute | solution.py:436
  13.6 3.1 %collective-permute-done.4.got_a = f32[6,16,128]{2,1,0:T(8,128)S(1)} collective-permute-done((f32[6,16,128]{2,1,0:T(8,128)S(1)}, f32[6,16,128]{2,1,0:T(8,128)S(1)}, u32[]{:S(2)}, u32[]{:S(2)}) %collective-permute-start.4) | collective-permute-done | bytes 49184 | tf_op jit(solution)/shard_map/ppermute | solution.py:436
  16.7 0.7 %shard_map.80 = (f32[4,16,128]{2,1,0:T(8,128)S(1)}, f32[1,256]{1,0:T(1,128)S(1)}) custom-call(f32[20,16,128]{2,1,0:T(8,128)S(1)} %get-tuple-element.33.joined, f32[1,4,128,256]{3,2,1,0:T(8,128)S(1)} %collective-permute-done.3.bot, f32[1,4,128,256]{3,2,1,0:T(8,128)S(1)} %copy-done, f32[6,16,128]{2,1,0:T(8,128)S(1)} %collective-permute-done.4.got_a, ...), custom_call_target="tpu_custom_call" | custom-call | tf_op jit(solution)/shard_map/pallas_call | solution.py:403
  17.4 0.9 %shard_map.81 = (f32[4,128,128]{2,1,0:T(8,128)S(1)}, f32[3,128,128]{2,1,0:T(8,128)S(1)}, f32[3,128,128]{2,1,0:T(8,128)S(1)}) custom-call(f32[1,4,128,128]{3,2,1,0:T(8,128)S(1)} %get-tuple-element.25.src, f32[1,4,128,128]{3,2,1,0:T(8,128)S(1)} %get-tuple-element.26.tx, f32[1,4,128,128]{3,2,1,0:T(8,128)S(1)} %get-tuple-element.27.ty, ...), custom_call_target="tpu_custom_call" | custom-call | tf_op jit(solution)/shard_map/pallas_call | solution.py:403
  18.4 2.9 %collective-permute-start.6 = (f32[3,128,128]{2,1,0:T(8,128)S(1)}, f32[3,128,128]{2,1,0:T(8,128)S(1)}, u32[]{:S(2)}, u32[]{:S(2)}) collective-permute-start(f32[3,128,128]{2,1,0:T(8,128)S(1)} %get-tuple-element.38), channel_id=1, source_target_pairs={{0,1},{1,0},{2,3},{3,2},{4,5},{5,4},{6,7},{7,6},{8,9},{9,8},{10,11... | collective-permute-start | bytes 589832 | tf_op jit(solution)/shard_map/ppermute | solution.py:436
  21.3 2.0 %collective-permute-start.10 = (f32[1,256]{1,0:T(1,128)S(1)}, f32[1,256]{1,0:T(1,128)S(1)}, u32[]{:S(2)}, u32[]{:S(2)}) collective-permute-start(f32[1,256]{1,0:T(1,128)S(1)} %get-tuple-element.36.after.rest_0_), channel_id=1, source_target_pairs={{0,1},{1,0},{2,3},{3,2},{4,5},{5,4},{6,7},{7,6},{8,9},{9,8},{10,11... | collective-permute-start | bytes 3080 | tf_op jit(solution)/shard_map/ppermute | solution.py:451
  23.3 1.2 %collective-permute-start.9 = (f32[1,256]{1,0:T(1,128)S(1)}, f32[1,256]{1,0:T(1,128)S(1)}, u32[]{:S(2)}, u32[]{:S(2)}) collective-permute-start(f32[1,256]{1,0:T(1,128)S(1)} %get-tuple-element.36.after.rest_0_), channel_id=1, source_target_pairs={{0,2},{1,3},{2,0},{3,1},{4,6},{5,7},{6,4},{7,5},{8,10},{9,11},{10,... | collective-permute-start | bytes 3080 | tf_op jit(solution)/shard_map/ppermute | solution.py:451
  24.5 1.2 %collective-permute-start.8 = (f32[1,256]{1,0:T(1,128)S(1)}, f32[1,256]{1,0:T(1,128)S(1)}, u32[]{:S(2)}, u32[]{:S(2)}) collective-permute-start(f32[1,256]{1,0:T(1,128)S(1)} %get-tuple-element.36.after.rest_0_), channel_id=1, source_target_pairs={{0,3},{1,2},{2,1},{3,0},{4,7},{5,6},{6,5},{7,4},{8,11},{9,10},{10,... | collective-permute-start | bytes 3080 | tf_op jit(solution)/shard_map/ppermute | solution.py:451
  25.7 2.1 %collective-permute-done.9.rest_2_ = f32[1,256]{1,0:T(1,128)S(1)} collective-permute-done((f32[1,256]{1,0:T(1,128)S(1)}, f32[1,256]{1,0:T(1,128)S(1)}, u32[]{:S(2)}, u32[]{:S(2)}) %collective-permute-start.9) | collective-permute-done | bytes 1056 | tf_op jit(solution)/shard_map/ppermute | solution.py:451
  27.8 2.1 %collective-permute-done.8.rest_1_ = f32[1,256]{1,0:T(1,128)S(1)} collective-permute-done((f32[1,256]{1,0:T(1,128)S(1)}, f32[1,256]{1,0:T(1,128)S(1)}, u32[]{:S(2)}, u32[]{:S(2)}) %collective-permute-start.8) | collective-permute-done | bytes 1056 | tf_op jit(solution)/shard_map/ppermute | solution.py:451
  30.4 3.7 %collective-permute-done.11.edge_a = f32[3,16,128]{2,1,0:T(8,128)S(1)} collective-permute-done((f32[3,16,128]{2,1,0:T(8,128)S(1)}, f32[3,16,128]{2,1,0:T(8,128)S(1)}, u32[]{:S(2)}, u32[]{:S(2)}) %collective-permute-start.11) | collective-permute-done | bytes 24608 | tf_op jit(solution)/shard_map/ppermute | solution.py:436
  34.1 0.6 %shard_map.84 = (f32[4,8,128]{2,1,0:T(8,128)S(1)}, f32[4,8,128]{2,1,0:T(8,128)S(1)}, f32[1,256]{1,0:T(1,128)S(1)}) custom-call(f32[20,16,128]{2,1,0:T(8,128)S(1)} %get-tuple-element.33.joined, f32[1,4,128,256]{3,2,1,0:T(8,128)S(1)} %collective-permute-done.3.bot, f32[1,4,128,256]{3,2,1,0:T(8,128)S(1)} %copy-done, ...), custom_call_target="tpu_custom_call" | custom-call | tf_op jit(solution)/shard_map/pallas_call | solution.py:403
  34.8 2.1 %collective-permute-start.16 = (f32[1,256]{1,0:T(1,128)S(1)}, f32[1,256]{1,0:T(1,128)S(1)}, u32[]{:S(2)}, u32[]{:S(2)}) collective-permute-start(f32[1,256]{1,0:T(1,128)S(1)} %get-tuple-element.47), channel_id=1, source_target_pairs={{0,1},{1,0},{2,3},{3,2},{4,5},{5,4},{6,7},{7,6},{8,9},{9,8},{10,11... | collective-permute-start | bytes 3080 | tf_op jit(solution)/shard_map/ppermute | solution.py:451
  36.9 2.4 %collective-permute-start.14 = (f32[1,256]{1,0:T(1,128)S(1)}, f32[1,256]{1,0:T(1,128)S(1)}, u32[]{:S(2)}, u32[]{:S(2)}) collective-permute-start(f32[1,256]{1,0:T(1,128)S(1)} %get-tuple-element.47), channel_id=1, source_target_pairs={{0,3},{1,2},{2,1},{3,0},{4,7},{5,6},{6,5},{7,4},{8,11},{9,10},{10,... | collective-permute-start | bytes 3080 | tf_op jit(solution)/shard_map/ppermute | solution.py:451
  39.3 2.0 %collective-permute-done.15 = f32[1,256]{1,0:T(1,128)S(1)} collective-permute-done((f32[1,256]{1,0:T(1,128)S(1)}, f32[1,256]{1,0:T(1,128)S(1)}, u32[]{:S(2)}, u32[]{:S(2)}) %collective-permute-start.15) | collective-permute-done | bytes 1056 | tf_op jit(solution)/shard_map/ppermute | solution.py:451
  41.3 0.9 %collective-permute-done.14 = f32[1,256]{1,0:T(1,128)S(1)} collective-permute-done((f32[1,256]{1,0:T(1,128)S(1)}, f32[1,256]{1,0:T(1,128)S(1)}, u32[]{:S(2)}, u32[]{:S(2)}) %collective-permute-start.14) | collective-permute-done | bytes 1056 | tf_op jit(solution)/shard_map/ppermute | solution.py:451
  42.2 0.6 %fusion = f32[1,64]{1,0:T(1,128)} fusion(f32[1,256]{1,0:T(1,128)S(1)} %get-tuple-element.46, s32[]{:T(128)S(6)} %select_n.3, f32[1,256]{1,0:T(1,128)S(1)} %collective-permute-done.16, f32[1,256]{1,0:T(1,128)S(1)} %collective-permute-done.15, f32[1,256]{1,0:T(1,128)S(1)} %collective-permute-done.14, f32[1,256]{1,0:T(1,128)S(1)} %get-tuple-element.47), kind=kLoop, calls=%fused_computation.5 | loop fusion | flops 320 | bytes 1540 | tf_op jit(solution)/shard_map/add | solution.py:492
  42.8 0.9 %shard_map.82.whole = f32[4,128,128]{2,1,0:T(8,128)S(1)} custom-call(f32[1,4,128,128]{3,2,1,0:T(8,128)S(1)} %get-tuple-element.25.src, f32[1,4,128,128]{3,2,1,0:T(8,128)S(1)} %get-tuple-element.26.tx, f32[1,4,128,128]{3,2,1,0:T(8,128)S(1)} %get-tuple-element.27.ty, f32[1,4,128,128]{3,2,1,0:T(8,128)S(1)} %get-tuple-element.28.tz, ...), custom_call_target="tpu_custom_call" | custom-call | tf_op jit(solution)/shard_map/pallas_call | solution.py:403
  44.0 0.7 %copy.8 = f32[1,4,128,128]{3,2,1,0:T(8,128)} copy(f32[1,4,128,128]{3,2,1,0:T(8,128)S(1)} %shard_map.85) | data formatting | bytes 524288
  (23 shorter events, 1.2 us)
Async XLA Ops:
  0.6 16.1 %collective-permute-start.3 = (f32[1,4,128,256]{3,2,1,0:T(8,128)}, f32[1,4,128,256]{3,2,1,0:T(8,128)S(1)}, u32[]{:S(2)}, u32[]{:S(2)}) collective-permute-start(f32[1,4,128,256]{3,2,1,0:T(8,128)} %param.10), channel_id=1, source_target_pairs={{4,0},{8,4},{12,8},{16,12},{20,16},{24,20},{28,24},{0,28},{5,1},{9... | collective-permute-start | bytes 1572872 | tf_op jit(solution)/shard_map/ppermute | solution.py:461
  5.9 10.9 %copy-start = (f32[1,4,128,256]{3,2,1,0:T(8,128)S(1)}, f32[1,4,128,256]{3,2,1,0:T(8,128)}, u32[]{:S(2)}) copy-start(f32[1,4,128,256]{3,2,1,0:T(8,128)} %top.5) | copy-start | bytes 1572868
  6.1 11.3 %collective-permute-start = (f32[6,128,128]{2,1,0:T(8,128)S(1)}, f32[6,128,128]{2,1,0:T(8,128)S(1)}, u32[]{:S(2)}, u32[]{:S(2)}) collective-permute-start(f32[6,128,128]{2,1,0:T(8,128)S(1)} %get-tuple-element.29), channel_id=1, source_target_pairs={{0,1},{1,0},{2,3},{3,2},{4,5},{5,4},{6,7},{7,6},{8,9},{9,8},{10,11... | collective-permute-start | bytes 1179656 | tf_op jit(solution)/shard_map/ppermute | solution.py:436
  7.8 9.6 %collective-permute-start.1 = (f32[6,128,128]{2,1,0:T(8,128)S(1)}, f32[6,128,128]{2,1,0:T(8,128)S(1)}, u32[]{:S(2)}, u32[]{:S(2)}) collective-permute-start(f32[6,128,128]{2,1,0:T(8,128)S(1)} %get-tuple-element.30), channel_id=1, source_target_pairs={{0,4},{1,2},{2,1},{3,7},{4,0},{5,6},{6,5},{7,3},{8,12},{9,10},{10,... | collective-permute-start | bytes 1179656 | tf_op jit(solution)/shard_map/ppermute | solution.py:437
  7.8 4.1 %collective-permute-start.2 = (f32[20,8,128]{2,1,0:T(8,128)S(1)}, f32[20,8,128]{2,1,0:T(8,128)S(1)}, u32[]{:S(2)}, u32[]{:S(2)}) collective-permute-start(f32[20,8,128]{2,1,0:T(8,128)S(1)} %get-tuple-element.32), channel_id=1, source_target_pairs={{4,0},{8,4},{12,8},{16,12},{20,16},{24,20},{28,24},{0,28},{5,1},{9... | collective-permute-start | bytes 245768 | tf_op jit(solution)/shard_map/ppermute | solution.py:460
  12.0 4.7 %collective-permute-start.4 = (f32[6,16,128]{2,1,0:T(8,128)S(1)}, f32[6,16,128]{2,1,0:T(8,128)S(1)}, u32[]{:S(2)}, u32[]{:S(2)}) collective-permute-start(f32[6,16,128]{2,1,0:T(8,128)S(1)} %get-tuple-element.34), channel_id=1, source_target_pairs={{0,1},{1,0},{2,3},{3,2},{4,5},{5,4},{6,7},{7,6},{8,9},{9,8},{10,11... | collective-permute-start | bytes 147464 | tf_op jit(solution)/shard_map/ppermute | solution.py:436
  13.6 3.1 %collective-permute-start.5 = (f32[6,16,128]{2,1,0:T(8,128)S(1)}, f32[6,16,128]{2,1,0:T(8,128)S(1)}, u32[]{:S(2)}, u32[]{:S(2)}) collective-permute-start(f32[6,16,128]{2,1,0:T(8,128)S(1)} %get-tuple-element.35), channel_id=1, source_target_pairs={{0,4},{1,2},{2,1},{3,7},{4,0},{5,6},{6,5},{7,3},{8,12},{9,10},{10,... | collective-permute-start | bytes 147464 | tf_op jit(solution)/shard_map/ppermute | solution.py:437
  18.4 24.5 %collective-permute-start.6 = (f32[3,128,128]{2,1,0:T(8,128)S(1)}, f32[3,128,128]{2,1,0:T(8,128)S(1)}, u32[]{:S(2)}, u32[]{:S(2)}) collective-permute-start(f32[3,128,128]{2,1,0:T(8,128)S(1)} %get-tuple-element.38), channel_id=1, source_target_pairs={{0,1},{1,0},{2,3},{3,2},{4,5},{5,4},{6,7},{7,6},{8,9},{9,8},{10,11... | collective-permute-start | bytes 589832 | tf_op jit(solution)/shard_map/ppermute | solution.py:436
  21.3 21.5 %collective-permute-start.7 = (f32[3,128,128]{2,1,0:T(8,128)S(1)}, f32[3,128,128]{2,1,0:T(8,128)S(1)}, u32[]{:S(2)}, u32[]{:S(2)}) collective-permute-start(f32[3,128,128]{2,1,0:T(8,128)S(1)} %get-tuple-element.39), channel_id=1, source_target_pairs={{0,4},{1,2},{2,1},{3,7},{4,0},{5,6},{6,5},{7,3},{8,12},{9,10},{10,... | collective-permute-start | bytes 589832 | tf_op jit(solution)/shard_map/ppermute | solution.py:437
  21.3 4.4 %collective-permute-start.10 = (f32[1,256]{1,0:T(1,128)S(1)}, f32[1,256]{1,0:T(1,128)S(1)}, u32[]{:S(2)}, u32[]{:S(2)}) collective-permute-start(f32[1,256]{1,0:T(1,128)S(1)} %get-tuple-element.36.after.rest_0_), channel_id=1, source_target_pairs={{0,1},{1,0},{2,3},{3,2},{4,5},{5,4},{6,7},{7,6},{8,9},{9,8},{10,11... | collective-permute-start | bytes 3080 | tf_op jit(solution)/shard_map/ppermute | solution.py:451
  23.3 4.5 %collective-permute-start.9 = (f32[1,256]{1,0:T(1,128)S(1)}, f32[1,256]{1,0:T(1,128)S(1)}, u32[]{:S(2)}, u32[]{:S(2)}) collective-permute-start(f32[1,256]{1,0:T(1,128)S(1)} %get-tuple-element.36.after.rest_0_), channel_id=1, source_target_pairs={{0,2},{1,3},{2,0},{3,1},{4,6},{5,7},{6,4},{7,5},{8,10},{9,11},{10,... | collective-permute-start | bytes 3080 | tf_op jit(solution)/shard_map/ppermute | solution.py:451
  24.5 5.4 %collective-permute-start.8 = (f32[1,256]{1,0:T(1,128)S(1)}, f32[1,256]{1,0:T(1,128)S(1)}, u32[]{:S(2)}, u32[]{:S(2)}) collective-permute-start(f32[1,256]{1,0:T(1,128)S(1)} %get-tuple-element.36.after.rest_0_), channel_id=1, source_target_pairs={{0,3},{1,2},{2,1},{3,0},{4,7},{5,6},{6,5},{7,4},{8,11},{9,10},{10,... | collective-permute-start | bytes 3080 | tf_op jit(solution)/shard_map/ppermute | solution.py:451
  30.2 3.9 %collective-permute-start.11 = (f32[3,16,128]{2,1,0:T(8,128)S(1)}, f32[3,16,128]{2,1,0:T(8,128)S(1)}, u32[]{:S(2)}, u32[]{:S(2)}) collective-permute-start(f32[3,16,128]{2,1,0:T(8,128)S(1)} %get-tuple-element.42), channel_id=1, source_target_pairs={{0,1},{1,0},{2,3},{3,2},{4,5},{5,4},{6,7},{7,6},{8,9},{9,8},{10,11... | collective-permute-start | bytes 73736 | tf_op jit(solution)/shard_map/ppermute | solution.py:436
  30.3 3.8 %collective-permute-start.12 = (f32[3,16,128]{2,1,0:T(8,128)S(1)}, f32[3,16,128]{2,1,0:T(8,128)S(1)}, u32[]{:S(2)}, u32[]{:S(2)}) collective-permute-start(f32[3,16,128]{2,1,0:T(8,128)S(1)} %get-tuple-element.43), channel_id=1, source_target_pairs={{0,4},{1,2},{2,1},{3,7},{4,0},{5,6},{6,5},{7,3},{8,12},{9,10},{10,... | collective-permute-start | bytes 73736 | tf_op jit(solution)/shard_map/ppermute | solution.py:437
  34.8 4.5 %collective-permute-start.16 = (f32[1,256]{1,0:T(1,128)S(1)}, f32[1,256]{1,0:T(1,128)S(1)}, u32[]{:S(2)}, u32[]{:S(2)}) collective-permute-start(f32[1,256]{1,0:T(1,128)S(1)} %get-tuple-element.47), channel_id=1, source_target_pairs={{0,1},{1,0},{2,3},{3,2},{4,5},{5,4},{6,7},{7,6},{8,9},{9,8},{10,11... | collective-permute-start | bytes 3080 | tf_op jit(solution)/shard_map/ppermute | solution.py:451
  36.8 4.5 %collective-permute-start.15 = (f32[1,256]{1,0:T(1,128)S(1)}, f32[1,256]{1,0:T(1,128)S(1)}, u32[]{:S(2)}, u32[]{:S(2)}) collective-permute-start(f32[1,256]{1,0:T(1,128)S(1)} %get-tuple-element.47), channel_id=1, source_target_pairs={{0,2},{1,3},{2,0},{3,1},{4,6},{5,7},{6,4},{7,5},{8,10},{9,11},{10,... | collective-permute-start | bytes 3080 | tf_op jit(solution)/shard_map/ppermute | solution.py:451
  36.9 5.4 %collective-permute-start.14 = (f32[1,256]{1,0:T(1,128)S(1)}, f32[1,256]{1,0:T(1,128)S(1)}, u32[]{:S(2)}, u32[]{:S(2)}) collective-permute-start(f32[1,256]{1,0:T(1,128)S(1)} %get-tuple-element.47), channel_id=1, source_target_pairs={{0,3},{1,2},{2,1},{3,0},{4,7},{5,6},{6,5},{7,4},{8,11},{9,10},{10,... | collective-permute-start | bytes 3080 | tf_op jit(solution)/shard_map/ppermute | solution.py:451
  39.3 4.4 %collective-permute-start.13 = (f32[4,8,128]{2,1,0:T(8,128)S(1)}, f32[4,8,128]{2,1,0:T(8,128)S(1)}, u32[]{:S(2)}, u32[]{:S(2)}) collective-permute-start(f32[4,8,128]{2,1,0:T(8,128)S(1)} %get-tuple-element.45), channel_id=1, source_target_pairs={{0,4},{4,8},{8,12},{12,16},{16,20},{20,24},{24,28},{28,0},{1,5},{5... | collective-permute-start | bytes 49160 | tf_op jit(solution)/shard_map/ppermute | solution.py:495

commit v2 on v1

--- a/solution.py
+++ b/solution.py
@@ -54,12 +54,13 @@
 
 
 class Thin:
-    def __init__(self, trans_y, trans_z, zsum, live):
+    def __init__(self, trans_y, trans_z, zsum, has_bot, has_top):
         rows = lax.broadcasted_iota(jnp.int32, trans_y.shape, 0)
         cols = lax.broadcasted_iota(jnp.int32, trans_y.shape, 1)
         self.cy = jnp.where(cols > 0, trans_y, 0.0)
         self.cz = jnp.where(rows == SLAB, 0.0, trans_z)
-        self.face = jnp.where((rows == SLAB) | (rows == SLAB - 1), trans_z, 0.0) * live
+        top = jnp.where(rows == SLAB - 1, trans_z * has_top, 0.0)
+        self.face = jnp.where(rows == SLAB, trans_z * has_bot, top)
         self.diag = self.cy + following(self.cy, 1) + zsum
 
     def around(self, p):
@@ -105,36 +106,60 @@
     by_parity("sub", *pair, take_above, take_below)
 
 
-def pack_kernel(src, tx, ty, tz, src_v, tx_v, ty_v, tz_v, slabs, firsts, sems):
+def pack_kernel(src, tx, ty, tz, src_v, tx_v, ty_v, tz_v, slabs, out_a, out_b, sems):
+    count, rows, cells = src_v.shape[1:]
     copies = [
         pltpu.make_async_copy(here, there, sems.at[i])
         for i, (here, there) in enumerate(
-            ((tz, tz_v), (src, src_v), (tx, tx_v), (ty, ty_v))
+            ((tz, tz_v), (tx, tx_v), (src, src_v), (ty, ty_v))
         )
     ]
     for copy in copies:
         copy.start()
     for copy in copies:
         copy.wait()
-    count, rows, cells = src_v.shape[1:]
-    has_bot, has_top, _, _ = flags()
-    items = []
+    has_bot, has_top, has_below, _ = flags()
+    slot = lax.broadcasted_iota(jnp.int32, (rows, cells), 1) // SPAN
+    each = cells // SPAN
+    packed, done = jnp.zeros((rows, cells), F32), 0
+
+    def flush(packed, done):
+        turned = packed.T
+        start = (done - 1) // each * each
+        for k in range(start, done):
+            slabs[k] = turned[(k - start) * SPAN : (k - start + 1) * SPAN]
+
     for x in range(count):
         zsum = along_z(tz_v[0, x], has_bot, has_top)[1]
-        items += [tx_v[0, x], src_v[0, x], ty_v[0, x], tz_v[0, x], zsum]
-    slot = lax.broadcasted_iota(jnp.int32, (rows, cells), 1) // SPAN
-    each = cells // SPAN
-    for start in range(0, len(items), each):
-        packed = jnp.zeros((rows, cells), F32)
-        here = items[start : start + each]
-        for j, item in enumerate(here):
+        for item in (tx_v[0, x], src_v[0, x], ty_v[0, x], tz_v[0, x], zsum):
+            j = done % each
             turned = pltpu.roll(item, (SPAN * j + SLAB) % cells, 1)
             packed = jnp.where(slot == j, turned, packed)
-        turned = packed.T
-        for j in range(len(here)):
-            k = start + j
-            slabs[k] = turned[j * SPAN : (j + 1) * SPAN]
-            firsts[k] = turned[j * SPAN + SLAB : (j + 1) * SPAN]
+            done += 1
+            if done % each == 0 or done == count * ITEMS:
+                flush(packed, done)
+
+    def item(which, x):
+        return slabs[x * ITEMS + which]
+
+    def make(x):
+        return Thin(item(2, x), item(3, x), item(4, x), has_bot, has_top)
+
+    p_low, q_low, w_low = edge_parts(item, make, has_below)
+    top = count - 1
+    p_top = RELAX * item(1, top - 1) / (make(top - 1).diag + item(0, top - 1) + item(0, top))
+
+    def upward(ref):
+        values = (item(0, top), p_top, item(1, top), item(4, top), item(2, top), item(3, top))
+        for i, v in enumerate(values):
+            ref[i] = v
+
+    def downward(ref):
+        values = (item(0, 0), p_low, q_low, w_low, item(2, 0), item(3, 0))
+        for i, v in enumerate(values):
+            ref[i] = v
+
+    by_parity("sub", out_a, out_b, upward, downward)
 
 
 def edge_parts(items, make, has_below):
@@ -156,50 +181,21 @@
     return thin_pass(p2, source, cx, layers, w, 0, count)
 
 
-def join_kernel(slabs, firsts, joined, out_a, out_b):
-    for k in range(firsts.shape[0]):
-        joined[k, 0:SLAB] = slabs[k, 0:SLAB]
-        joined[k, SLAB:SPAN] = firsts[k]
-    count = firsts.shape[0] // ITEMS
-    _, live, has_below, _ = flags()
-
-    def item(which, x):
-        return joined[x * ITEMS + which]
-
-    def make(x):
-        return Thin(item(2, x), item(3, x), item(4, x), live)
-
-    p_low, q_low, w_low = edge_parts(item, make, has_below)
-    top = count - 1
-    p_top = RELAX * item(1, top - 1) / (make(top - 1).diag + item(0, top - 1) + item(0, top))
-
-    def upward(ref):
-        values = (item(0, top), p_top, item(1, top), item(4, top), item(2, top), item(3, top))
-        for i, v in enumerate(values):
-            ref[i] = v
-
-    def downward(ref):
-        values = (item(0, 0), p_low, q_low, w_low, item(2, 0), item(3, 0))
-        for i, v in enumerate(values):
-            ref[i] = v
-
-    by_parity("sub", out_a, out_b, upward, downward)
-
-
-def thin_setup(joined, above, below):
-    count = joined.shape[0] // ITEMS
-    _, live, has_below, has_above = flags()
-    cx = {x: joined[x * ITEMS] for x in range(1, count)}
+def thin_setup(slabs, above, below):
+    count = slabs.shape[0] // ITEMS
+    has_bot, has_top, has_below, has_above = flags()
+    cx = {x: slabs[x * ITEMS] for x in range(1, count)}
     cx[-1] = below[0]
-    cx[0] = joined[0] * has_below
+    cx[0] = slabs[0] * has_below
     cx[count] = above[0] * has_above
-    source = {x: joined[x * ITEMS + 1] for x in range(count)}
+    source = {x: slabs[x * ITEMS + 1] for x in range(count)}
     source[-1] = below[2]
     layers = {
-        x: Thin(*(joined[x * ITEMS + i] for i in (2, 3, 4)), live) for x in range(count)
+        x: Thin(*(slabs[x * ITEMS + i] for i in (2, 3, 4)), has_bot, has_top)
+        for x in range(count)
     }
-    layers[-1] = Thin(below[4], below[5], below[3], live)
-    layers[count] = Thin(above[4], above[5], above[3], live)
+    layers[-1] = Thin(below[4], below[5], below[3], has_bot, has_top)
+    layers[count] = Thin(above[4], above[5], above[3], has_bot, has_top)
     w = {x: RELAX / (layers[x].diag + cx[x] + cx[x + 1]) for x in range(-1, count)}
     w[count] = above[3]
     return source, cx, layers, w
@@ -235,28 +231,52 @@
     return thin_pass(last, rhs, cx, layers, weight, 0, count)
 
 
-def traces(flux, bot, top, rows):
+def traces(flux, bot, top):
     count = len(flux)
-    stacked = [f[SLAB : SLAB + 1] for f in flux] + [f[SLAB - 1 : SLAB] for f in flux]
-    stacked.append(jnp.zeros((rows - len(stacked), flux[0].shape[1]), F32))
-    columns = jnp.concatenate(stacked, axis=0).T
-    total = sum(
-        columns[:, face * count + x : face * count + x + 1] * basis[0, x]
-        for face, basis in enumerate((bot, top))
-        for x in range(count)
-    )
-    return jnp.sum(total, axis=0, keepdims=True)
-
-
-def first_thin(joined, bot, top, got_a, got_b, p_out, share, above, below):
-    count, rows = bot.shape[1:3]
+    planes = (SLAB, SLAB - 1)
+    columns = jnp.concatenate([f[at : at + 1] for at in planes for f in flux], axis=0).T
+    sums = []
+    for face, basis in enumerate((bot, top)):
+        total = sum(
+            columns[:, face * count + x : face * count + x + 1] * basis[0, x] for x in range(count)
+        )
+        sums.append(jnp.sum(total, axis=0, keepdims=True))
+    return sums
+
+
+def first_thin(slabs, bot, top, got_a, got_b, p_out, kept, sh_a, sh_b, above, below):
+    count = bot.shape[1]
     sort_pair((got_a, got_b), above, below)
-    source, cx, layers, w = thin_setup(joined, above, below)
+    source, cx, layers, w = thin_setup(slabs, above, below)
     p = first_three(count, source, cx, layers, w, above, below)
     for x in range(count):
         p_out[x] = p[x]
-    flux = [layers[x].face * p[x] for x in range(count)]
-    share[...] = traces(flux, bot, top, rows)
+    cbot, ctop = traces([layers[x].face * p[x] for x in range(count)], bot, top)
+
+    def to_above(ref):
+        ref[...] = ctop
+
+    def to_below(ref):
+        ref[...] = cbot
+
+    by_parity("block", sh_a, sh_b, to_above, to_below)
+    for x in range(-1, count + 1):
+        for i, v in enumerate((cx[x], w[x], layers[x].cy, layers[x].cz, layers[x].face)):
+            kept[x + 1, i] = v
+
+
+class Kept(Thin):
+    def __init__(self, kept, x):
+        self.cy, self.cz, self.face = (kept[x + 1, i] for i in (2, 3, 4))
+
+
+def thin_again(slabs, kept):
+    count = slabs.shape[0] // ITEMS
+    span = range(-1, count + 1)
+    cx = {x: kept[x + 1, 0] for x in span}
+    w = {x: kept[x + 1, 1] for x in span}
+    layers = {x: Kept(kept, x) for x in span}
+    return {x: slabs[x * ITEMS + 1] for x in range(count)}, cx, layers, w
 
 
 def with_faces(source, layers, data, count):
@@ -267,22 +287,23 @@
     return known, {x: source[x] + layers[x].face * known[x] for x in range(count)}
 
 
-def face_kernel(joined, bot, top, got_a, got_b, p_in, *rest):
-    parts = rest[:-6]
-    data_out, edge_a, edge_b, mortar_out, above, below = rest[-6:]
-    count, rows = bot.shape[1:3]
-    sort_pair((got_a, got_b), above, below)
-    mortar = MORTAR_STEP * sum(part[...] for part in parts)
-    mortar_out[...] = mortar
-    lanes = lax.broadcasted_iota(jnp.int32, (rows, rows), 1)
-    columns = jnp.zeros((rows, rows), F32)
-    for face, ref in enumerate((bot, top)):
-        for x in range(count):
-            data = jnp.sum(ref[0, x] * mortar, axis=1, keepdims=True)
-            columns = jnp.where(lanes == face * count + x, data, columns)
-    data = columns.T[0 : 2 * count]
+def face_kernel(slabs, bot, top, kept, p_in, *rest):
+    parts = rest[:-4]
+    data_out, edge_a, edge_b, mortar_out = rest[-4:]
+    count = bot.shape[1]
+    jumps = MORTAR_STEP * sum(part[...] for part in parts)
+    even = lax.rem(lax.axis_index("block"), 2) == 0
+    own = jnp.where(even, jumps[0:1], jumps[1:2])
+    under = jnp.where(even, jumps[1:2], jumps[0:1])
+    mortar_out[...] = own
+    columns = [
+        jnp.sum(ref[0, x] * values, axis=1, keepdims=True)
+        for ref, values in ((bot, under), (top, own))
+        for x in range(count)
+    ]
+    data = jnp.concatenate(columns, axis=1).T
     data_out[...] = data
-    source, cx, layers, w = thin_setup(joined, above, below)
+    source, cx, layers, w = thin_again(slabs, kept)
     rhs = with_faces(source, layers, data, count)[1]
     p = {x: p_in[x] for x in range(count)}
     last = count - 1
@@ -296,21 +317,19 @@
 
 
 def second_thin(
-    joined, bot, top, got_a, got_b, p_in, data, edge_a, edge_b,
-    lasts, firsts, share, above, below, edge_above, edge_below,
+    slabs, bot, top, kept, p_in, data, edge_a, edge_b,
+    p_out, cbot_out, ctop_out, edge_above, edge_below,
 ):
-    count, rows = bot.shape[1:3]
-    sort_pair((got_a, got_b), above, below)
+    count = bot.shape[1]
     sort_pair((edge_a, edge_b), edge_above, edge_below)
-    source, cx, layers, w = thin_setup(joined, above, below)
+    source, cx, layers, w = thin_again(slabs, kept)
     known, rhs = with_faces(source, layers, data, count)
     p = {x: p_in[x] for x in range(count)}
     p = three_passes(p, edge_above, edge_below, rhs, cx, layers, w, count)
     for x in range(count):
-        lasts[x] = p[x][0:SLAB]
-        firsts[x] = p[x][SLAB:SPAN]
+        p_out[x] = p[x]
     flux = [layers[x].face * (p[x] - known[x]) for x in range(count)]
-    share[...] = traces(flux, bot, top, rows)
+    cbot_out[...], ctop_out[...] = traces(flux, bot, top)
 
 
 def edge_kernel(src, tx, ty, tz, out_a, out_b):
@@ -350,7 +369,7 @@
     return source, cx, layers, weight
 
 
-def first_whole(src, tx, ty, tz, got_a, got_b, after, p_out, mid_a, mid_b, above, below):
+def first_whole(src, tx, ty, tz, got_a, got_b, p_out, mid_a, mid_b, above, below):
     count = src.shape[1]
     sort_pair((got_a, got_b), above, below)
     source, cx, layers, w = whole_setup(src, tx, ty, tz, above, below)
@@ -358,6 +377,7 @@
     for x in range(count):
         p_out[x] = p3[x]
     last = count - 1
+
     by_parity(
         "sub",
         mid_a,
@@ -367,7 +387,9 @@
     )
 
 
-def second_whole(src, tx, ty, tz, got_a, got_b, p_in, mid_a, mid_b, p_out, above, below, p_above, p_below):
+def second_whole(
+    src, tx, ty, tz, got_a, got_b, p_in, mid_a, mid_b, p_out, above, below, p_above, p_below
+):
     count = src.shape[1]
     sort_pair((got_a, got_b), above, below)
     sort_pair((mid_a, mid_b), p_above, p_below)
@@ -381,30 +403,41 @@
         p_out[x] = p6[x]
 
 
-def merge_kernel(whole, lasts, firsts, p_out):
+def finish_kernel(whole, thin, mortar, *rest):
+    parts = rest[:-5]
+    p_out, m_out, merged, piece, sems = rest[-5:]
+    total = mortar[...] + MORTAR_STEP * sum(part[...] for part in parts)
+    columns = piece.shape[1]
+    shift = total.shape[1] - lax.axis_index("sub") * columns
+    piece[...] = pltpu.roll(total, lax.rem(shift, total.shape[1]), 1)[:, 0:columns]
+    copies = [pltpu.make_async_copy(piece, m_out, sems.at[0])]
+    copies[0].start()
     count, rows, cells = whole.shape
     cols = lax.broadcasted_iota(jnp.int32, (rows, cells), 1)
     face = (cols < PASSES) | (cols >= cells - PASSES)
     each = cells // SPAN
     for start in range(0, count, each):
         stop = min(start + each, count)
-        here = [part[x] for x in range(start, stop) for part in (lasts, firsts)]
+        here = [thin[x] for x in range(start, stop)]
         if (stop - start) * SPAN < cells:
             here.append(jnp.zeros((cells - (stop - start) * SPAN, rows), F32))
         back = jnp.concatenate(here, axis=0).T
         for x in range(start, stop):
             shift = (cells - (x - start) * SPAN - SLAB) % cells
-            p_out[0, x] = jnp.where(face, pltpu.roll(back, shift, 1), whole[x])
-
-
-def call(kernel, outs, args, scratch=(), copies=0):
-    space = pltpu.HBM if copies else pltpu.VMEM
-    args = [pltpu.with_memory_space_constraint(a, space) for a in args]
+            merged[x] = jnp.where(face, pltpu.roll(back, shift, 1), whole[x])
+            copies.append(pltpu.make_async_copy(merged.at[x], p_out.at[0, x], sems.at[x + 1]))
+            copies[-1].start()
+    for copy in copies:
+        copy.wait()
+
+
+def call(kernel, outs, args, scratch=(), copies=0, source=pltpu.VMEM, target=pltpu.VMEM):
+    args = [pltpu.with_memory_space_constraint(a, source) for a in args]
     return pl.pallas_call(
         kernel,
-        out_shape=[pltpu.VMEM(shape, F32) for shape in outs],
-        in_specs=[pl.BlockSpec(memory_space=space)] * len(args),
-        out_specs=[pl.BlockSpec(memory_space=pltpu.VMEM)] * len(outs),
+        out_shape=[target(shape, F32) for shape in outs],
+        in_specs=[pl.BlockSpec(memory_space=source)] * len(args),
+        out_specs=[pl.BlockSpec(memory_space=target)] * len(outs),
         scratch_shapes=[pltpu.VMEM(shape, F32) for shape in scratch]
         + ([pltpu.SemaphoreType.DMA((copies,))] if copies else []),
         compiler_params=pltpu.CompilerParams(vmem_limit_bytes=16 << 20),
@@ -439,9 +472,6 @@
     face = (rows, cells)
     kept = count * ITEMS
     slab = (SPAN, rows)
-    half = (SLAB, rows)
-    up = [(b, (b + 1) % blocks) for b in range(blocks)]
-    down = [(b, a) for a, b in up]
 
     def everyone(value):
         if subs > DIRECT:
@@ -451,56 +481,65 @@
             parts.append(lax.ppermute(value, "sub", [(i, i ^ k) for i in range(subs)]))
         return parts
 
-    *coeffs, slabs, firsts = call(
+    *coeffs, slabs, near_a, near_b = call(
         pack_kernel,
-        [source.shape] * 4 + [(kept,) + slab, (kept,) + half],
+        [source.shape] * 4 + [(kept,) + slab] + [(EDGE,) + slab] * 2,
         (source, trans_x, trans_y, trans_z),
         copies=4,
-    )
-    firsts = lax.ppermute(firsts, "block", down)
-    basis = lax.ppermute(mortar_bot, "block", down)
-    joined, near_a, near_b = call(
-        join_kernel, [(kept,) + slab] + [(EDGE,) + slab] * 2, (slabs, firsts)
+        source=pltpu.HBM,
     )
     near = trade(near_a, near_b)
     edges = call(edge_kernel, [(EDGE,) + face] * 2, coeffs)
     edges = trade(*edges)
-    fixed = (joined, basis, mortar_top) + near
-    sides = [(EDGE,) + slab] * 2
-    third, share = call(first_thin, [(count,) + slab, (1, width)], fixed, sides)
-    parts = everyone(share)
+    fixed = (slabs, mortar_bot, mortar_top)
+    third, known, share_a, share_b = call(
+        first_thin,
+        [(count,) + slab, (count + 2, 5) + slab] + [(1, width)] * 2,
+        fixed + near,
+        [(EDGE,) + slab] * 2,
+    )
+    block_one = [(b, b ^ 1) for b in range(blocks)]
+    block_two = [(b, (b + 1 if b % 2 else b - 1) % blocks) for b in range(blocks)]
+    other_a = lax.ppermute(share_a, "block", block_one)
+    other_b = lax.ppermute(share_b, "block", block_two)
+    jumps = jnp.concatenate([share_a + other_a, share_b + other_b], axis=0)
+    parts = everyone(jumps)
     whole, mid_a, mid_b = call(
         first_whole,
         [(count,) + face] + [(MIDDLE,) + face] * 2,
-        tuple(coeffs) + edges + (share,),
+        tuple(coeffs) + edges,
         [(EDGE,) + face] * 2,
     )
     middle = trade(mid_a, mid_b)
     data, edge_a, edge_b, mortar = call(
         face_kernel,
         [(2 * count, rows)] + [(MIDDLE,) + slab] * 2 + [(1, width)],
-        fixed + (third,) + tuple(parts),
-        sides,
+        fixed + (known, third) + tuple(parts),
     )
     got = trade(edge_a, edge_b)
-    lasts, firsts, share = call(
+    slab_out, cbot, ctop = call(
         second_thin,
-        [(count,) + half] * 2 + [(1, width)],
-        fixed + (third, data) + got,
-        sides + [(MIDDLE,) + slab] * 2,
-    )
-    total = mortar + MORTAR_STEP * sum(everyone(share))
-    columns = width // subs
-    final = lax.dynamic_slice_in_dim(total[0], lax.axis_index("sub") * columns, columns, 0)
-    firsts = lax.ppermute(firsts, "block", up)
+        [(count,) + slab] + [(1, width)] * 2,
+        fixed + (known, third, data) + got,
+        [(MIDDLE,) + slab] * 2,
+    )
+    upper = lax.ppermute(cbot, "block", [((b + 1) % blocks, b) for b in range(blocks)])
+    parts = everyone(ctop + upper)
     (whole,) = call(
         second_whole,
         [(count,) + face],
         tuple(coeffs) + edges + (whole,) + middle,
         [(EDGE,) + face] * 2 + [(MIDDLE,) + face] * 2,
     )
-    (pressure,) = call(merge_kernel, [source.shape], (whole, lasts, firsts))
-    return pressure, final[None]
+    columns = width // subs
+    return call(
+        finish_kernel,
+        [source.shape, (1, columns)],
+        (whole, slab_out, mortar) + tuple(parts),
+        [(count,) + face, (1, columns)],
+        copies=count + 1,
+        target=pltpu.HBM,
+    )
 
 
 def solution(mesh):

time: 44.8 us -> 52.1 us (1.16)
  waiting for transfers between devices: 17.3 us -> 24.7 us
  local copies, waits for them, and re-layouts: 0.71 us -> 0.01 us
  Pallas kernels: 5.93 us -> 6.54 us
  starting transfers between devices: 19.4 us -> 20 us
  other arithmetic: 0.59 us -> 0.02 us
    ppermute x4, waiting for transfers between devices: 6.82 us -> 15.9 us  [trade(): first = lax.ppermute(a, names, pair_one)]
    ppermute x4, starting transfers between devices: 6.28 us -> 8.23 us  [trade(): first = lax.ppermute(a, names, pair_one)]
    ppermute x3, starting transfers between devices: 4.11 us -> 2.79 us  [the longest x1 2.55 us: work(): other_b = lax.ppermute(share_b, 'block', block_two)]
    ppermute x6, waiting for transfers between devices: 7.1 us -> 6.03 us  [everyone(): parts.append(lax.ppermute(value, 'sub', [(i, i ^ k) for i in range(subs)]))]
    unnamed x3 -> x4, local copies, waits for them, and re-layouts: 0.71 us -> 0.01 us
    ppermute x3, waiting for transfers between devices: 3.38 us -> 2.71 us  [the longest x1 1.41 us: work(): other_b = lax.ppermute(share_b, 'block', block_two)]
    pallas_call x9 -> x8, Pallas kernels: 5.93 us -> 6.54 us  [call(): pl.pallas_call(kernel, out_shape=[target(shape, F32) for shape in outs],...]
    add x1 -> x3, other arithmetic: 0.59 us -> 0.01 us  [the longest x2 0.01 us: work(): jumps = jnp.concatenate([share_a + other_a, share_b + other_b], axis=0)]
  transfers between devices with their start and end apart: 17 -> 17, of which waited for: 7 -> 9; matrix products, arithmetic and copies ran while one was open for 1% -> 0% of each run, Pallas kernels for 11% -> 5%
where the time goes in v2:
time: 52.1 us; the launch traced here: 52 us
  waiting for transfers between devices  24.7 us (47%)
  starting transfers between devices  20 us (38%)
  Pallas kernels  6.54 us (13%)
  between operations  0.72 us (1%)
    ppermute x4, waiting for transfers between devices, trade(): first = lax.ppermute(a, names, pair_one)  15.9 us
    ppermute x6, starting transfers between devices, everyone(): parts.append(lax.ppermute(value, 'sub', [(i, i ^ k) for i in range(subs)]))  8.98 us
    ppermute x4, starting transfers between devices, trade(): first = lax.ppermute(a, names, pair_one)  8.23 us
    pallas_call x8, Pallas kernels, call(): pl.pallas_call(kernel, out_shape=[target(shape, F32) for shape in outs],...  6.54 us
    ppermute x6, waiting for transfers between devices, everyone(): parts.append(lax.ppermute(value, 'sub', [(i, i ^ k) for i in range(subs)]))  6.03 us
    ppermute x1, starting transfers between devices, work(): other_b = lax.ppermute(share_b, 'block', block_two)  2.55 us
    ppermute x1, waiting for transfers between devices, work(): other_b = lax.ppermute(share_b, 'block', block_two)  1.41 us
    ppermute x1, waiting for transfers between devices, work(): lax.ppermute(cbot, 'block', [((b + 1) % blocks, b) for b in range(blocks)])  1.3 us
  transfers between devices with their start and end apart: 17, of which 9 were waited for; matrix products, arithmetic and copies ran while one was open for 0% of the time, Pallas kernels for 5%

profile of v2, /device:TPU:0, one launch (start us, length us, event | category | flops | bytes accessed | tf_op | source)
XLA Modules:
  0.0 52.0 jit_solution(2834346001490107269)
XLA Ops:
  0.6 1.9 %shard_map.77 = (f32[1,4,128,128]{3,2,1,0:T(8,128)S(1)}, f32[1,4,128,128]{3,2,1,0:T(8,128)S(1)}, f32[1,4,128,128]{3,2,1,0:T(8,128)S(1)}, f32[1,4,128,128]{3,2,1,...) custom-call(f32[1,4,128,128]{3,2,1,0:T(8,128)} %src.1, ...), custom_call_target="tpu_custom_call" | custom-call | tf_op jit(solution)/shard_map/pallas_call | solution.py:436
  2.7 3.1 %collective-permute-start = (f32[6,128,128]{2,1,0:T(8,128)S(1)}, f32[6,128,128]{2,1,0:T(8,128)S(1)}, u32[]{:S(2)}, u32[]{:S(2)}) collective-permute-start(f32[6,128,128]{2,1,0:T(8,128)S(1)} %get-tuple-element.29), channel_id=1, source_target_pairs={{0,1},{1,0},{2,3},{3,2},{4,5},{5,4},{6,7},{7,6},{8,9},{9,8},{10,11... | collective-permute-start | bytes 1179656 | tf_op jit(solution)/shard_map/ppermute | solution.py:469
  5.9 9.1 %collective-permute-done.got_a = f32[6,128,128]{2,1,0:T(8,128)S(1)} collective-permute-done((f32[6,128,128]{2,1,0:T(8,128)S(1)}, f32[6,128,128]{2,1,0:T(8,128)S(1)}, u32[]{:S(2)}, u32[]{:S(2)}) %collective-permute-start) | collective-permute-done | bytes 393248 | tf_op jit(solution)/shard_map/ppermute | solution.py:469
  15.0 0.9 %shard_map.79 = (f32[4,128,128]{2,1,0:T(8,128)S(1)}, f32[3,128,128]{2,1,0:T(8,128)S(1)}, f32[3,128,128]{2,1,0:T(8,128)S(1)}) custom-call(f32[1,4,128,128]{3,2,1,0:T(8,128)S(1)} %get-tuple-element.25.src, f32[1,4,128,128]{3,2,1,0:T(8,128)S(1)} %get-tuple-element.26.tx, f32[1,4,128,128]{3,2,1,0:T(8,128)S(1)} %get-tuple-element.27.ty, ...), custom_call_target="tpu_custom_call" | custom-call | tf_op jit(solution)/shard_map/pallas_call | solution.py:436
  15.9 2.9 %collective-permute-start.2 = (f32[3,128,128]{2,1,0:T(8,128)S(1)}, f32[3,128,128]{2,1,0:T(8,128)S(1)}, u32[]{:S(2)}, u32[]{:S(2)}) collective-permute-start(f32[3,128,128]{2,1,0:T(8,128)S(1)} %get-tuple-element.32), channel_id=1, source_target_pairs={{0,1},{1,0},{2,3},{3,2},{4,5},{5,4},{6,7},{7,6},{8,9},{9,8},{10,11... | collective-permute-start | bytes 589832 | tf_op jit(solution)/shard_map/ppermute | solution.py:469
  18.8 2.0 %collective-permute-start.4 = (f32[6,16,128]{2,1,0:T(8,128)S(1)}, f32[6,16,128]{2,1,0:T(8,128)S(1)}, u32[]{:S(2)}, u32[]{:S(2)}) collective-permute-start(f32[6,16,128]{2,1,0:T(8,128)S(1)} %get-tuple-element.35), channel_id=1, source_target_pairs={{0,1},{1,0},{2,3},{3,2},{4,5},{5,4},{6,7},{7,6},{8,9},{9,8},{10,11... | collective-permute-start | bytes 147464 | tf_op jit(solution)/shard_map/ppermute | solution.py:469
  20.9 3.1 %collective-permute-done.4.got_a = f32[6,16,128]{2,1,0:T(8,128)S(1)} collective-permute-done((f32[6,16,128]{2,1,0:T(8,128)S(1)}, f32[6,16,128]{2,1,0:T(8,128)S(1)}, u32[]{:S(2)}, u32[]{:S(2)}) %collective-permute-start.4) | collective-permute-done | bytes 49184 | tf_op jit(solution)/shard_map/ppermute | solution.py:469
  24.0 0.7 %shard_map.81 = (f32[4,16,128]{2,1,0:T(8,128)S(1)}, f32[6,5,16,128]{3,2,1,0:T(8,128)S(1)}, f32[1,256]{1,0:T(1,128)S(1)}, f32[1,256]{1,0:T(1,128)S(1)}) custom-call(f32[20,16,128]{2,1,0:T(8,128)S(1)} %get-tuple-element.34.slabs, f32[1,4,128,256]{3,2,1,0:T(8,128)S(1)} %copy-done, f32[1,4,128,256]{3,2,1,0:T(8,128)S(1)} %copy-done.1, ...), custom_call_target="tpu_custom_call" | custom-call | tf_op jit(solution)/shard_map/pallas_call | solution.py:436
  24.7 2.5 %collective-permute-start.7 = (f32[1,256]{1,0:T(1,128)S(1)}, f32[1,256]{1,0:T(1,128)S(1)}, u32[]{:S(2)}, u32[]{:S(2)}) collective-permute-start(f32[1,256]{1,0:T(1,128)S(1)} %get-tuple-element.40), channel_id=1, source_target_pairs={{0,28},{4,8},{8,4},{12,16},{16,12},{20,24},{24,20},{28,0},{1,29},{... | collective-permute-start | bytes 3080 | tf_op jit(solution)/shard_map/ppermute | solution.py:504
  27.3 1.4 %collective-permute-done.7 = f32[1,256]{1,0:T(1,128)S(1)} collective-permute-done((f32[1,256]{1,0:T(1,128)S(1)}, f32[1,256]{1,0:T(1,128)S(1)}, u32[]{:S(2)}, u32[]{:S(2)}) %collective-permute-start.7) | collective-permute-done | bytes 1056 | tf_op jit(solution)/shard_map/ppermute | solution.py:504
  28.7 1.9 %collective-permute-start.10 = (f32[2,256]{1,0:T(2,128)S(1)}, f32[2,256]{1,0:T(2,128)S(1)}, u32[]{:S(2)}, u32[]{:S(2)}) collective-permute-start(f32[2,256]{1,0:T(2,128)S(1)} %pad_maximum_fusion.rest_0_), channel_id=1, source_target_pairs={{0,1},{1,0},{2,3},{3,2},{4,5},{5,4},{6,7},{7,6},{8,9},{9,8},{10,11... | collective-permute-start | bytes 6152 | tf_op jit(solution)/shard_map/ppermute | solution.py:481
  30.6 1.4 %collective-permute-start.9 = (f32[2,256]{1,0:T(2,128)S(1)}, f32[2,256]{1,0:T(2,128)S(1)}, u32[]{:S(2)}, u32[]{:S(2)}) collective-permute-start(f32[2,256]{1,0:T(2,128)S(1)} %pad_maximum_fusion.rest_0_), channel_id=1, source_target_pairs={{0,2},{1,3},{2,0},{3,1},{4,6},{5,7},{6,4},{7,5},{8,10},{9,11},{10,... | collective-permute-start | bytes 6152 | tf_op jit(solution)/shard_map/ppermute | solution.py:481
  32.0 1.3 %collective-permute-start.8 = (f32[2,256]{1,0:T(2,128)S(1)}, f32[2,256]{1,0:T(2,128)S(1)}, u32[]{:S(2)}, u32[]{:S(2)}) collective-permute-start(f32[2,256]{1,0:T(2,128)S(1)} %pad_maximum_fusion.rest_0_), channel_id=1, source_target_pairs={{0,3},{1,2},{2,1},{3,0},{4,7},{5,6},{6,5},{7,4},{8,11},{9,10},{10,... | collective-permute-start | bytes 6152 | tf_op jit(solution)/shard_map/ppermute | solution.py:481
  33.3 1.8 %collective-permute-done.9.rest_2_ = f32[2,256]{1,0:T(2,128)S(1)} collective-permute-done((f32[2,256]{1,0:T(2,128)S(1)}, f32[2,256]{1,0:T(2,128)S(1)}, u32[]{:S(2)}, u32[]{:S(2)}) %collective-permute-start.9) | collective-permute-done | bytes 2080 | tf_op jit(solution)/shard_map/ppermute | solution.py:481
  35.0 2.3 %collective-permute-done.8.rest_1_ = f32[2,256]{1,0:T(2,128)S(1)} collective-permute-done((f32[2,256]{1,0:T(2,128)S(1)}, f32[2,256]{1,0:T(2,128)S(1)}, u32[]{:S(2)}, u32[]{:S(2)}) %collective-permute-start.8) | collective-permute-done | bytes 2080 | tf_op jit(solution)/shard_map/ppermute | solution.py:481
  37.9 3.7 %collective-permute-done.11.edge_a = f32[3,16,128]{2,1,0:T(8,128)S(1)} collective-permute-done((f32[3,16,128]{2,1,0:T(8,128)S(1)}, f32[3,16,128]{2,1,0:T(8,128)S(1)}, u32[]{:S(2)}, u32[]{:S(2)}) %collective-permute-start.11) | collective-permute-done | bytes 24608 | tf_op jit(solution)/shard_map/ppermute | solution.py:469
  41.6 0.6 %shard_map.83 = (f32[4,16,128]{2,1,0:T(8,128)S(1)}, f32[1,256]{1,0:T(1,128)S(1)}, f32[1,256]{1,0:T(1,128)S(1)}) custom-call(f32[20,16,128]{2,1,0:T(8,128)S(1)} %get-tuple-element.34.slabs, f32[1,4,128,256]{3,2,1,0:T(8,128)S(1)} %copy-done, f32[1,4,128,256]{3,2,1,0:T(8,128)S(1)} %copy-done.1, f32[6,5,16,128]{3,2,1,0:T(8,128)S(1)} %get-tuple-element.37.kept, ...), custom_call_target="tpu_custom_call" | custom-call | tf_op jit(solution)/shard_map/pallas_call | solution.py:436
  42.4 1.3 %collective-permute-done.13 = f32[1,256]{1,0:T(1,128)S(1)} collective-permute-done((f32[1,256]{1,0:T(1,128)S(1)}, f32[1,256]{1,0:T(1,128)S(1)}, u32[]{:S(2)}, u32[]{:S(2)}) %collective-permute-start.13) | collective-permute-done | bytes 1056 | tf_op jit(solution)/shard_map/ppermute | solution.py:526
  43.7 1.9 %collective-permute-start.16 = (f32[1,256]{1,0:T(1,128)S(1)}, f32[1,256]{1,0:T(1,128)S(1)}, u32[]{:S(2)}, u32[]{:S(2)}) collective-permute-start(f32[1,256]{1,0:T(1,128)S(1)} %add.11.rest_0_), channel_id=1, source_target_pairs={{0,1},{1,0},{2,3},{3,2},{4,5},{5,4},{6,7},{7,6},{8,9},{9,8},{10,11... | collective-permute-start | bytes 3080 | tf_op jit(solution)/shard_map/ppermute | solution.py:481
  45.6 2.5 %collective-permute-start.14 = (f32[1,256]{1,0:T(1,128)S(1)}, f32[1,256]{1,0:T(1,128)S(1)}, u32[]{:S(2)}, u32[]{:S(2)}) collective-permute-start(f32[1,256]{1,0:T(1,128)S(1)} %add.11.rest_0_), channel_id=1, source_target_pairs={{0,3},{1,2},{2,1},{3,0},{4,7},{5,6},{6,5},{7,4},{8,11},{9,10},{10,... | collective-permute-start | bytes 3080 | tf_op jit(solution)/shard_map/ppermute | solution.py:481
  48.1 0.9 %shard_map.80.whole = f32[4,128,128]{2,1,0:T(8,128)S(1)} custom-call(f32[1,4,128,128]{3,2,1,0:T(8,128)S(1)} %get-tuple-element.25.src, f32[1,4,128,128]{3,2,1,0:T(8,128)S(1)} %get-tuple-element.26.tx, f32[1,4,128,128]{3,2,1,0:T(8,128)S(1)} %get-tuple-element.27.ty, f32[1,4,128,128]{3,2,1,0:T(8,128)S(1)} %get-tuple-element.28.tz, ...), custom_call_target="tpu_custom_call" | custom-call | tf_op jit(solution)/shard_map/pallas_call | solution.py:436
  49.0 1.1 %collective-permute-done.15.rest_2_ = f32[1,256]{1,0:T(1,128)S(1)} collective-permute-done((f32[1,256]{1,0:T(1,128)S(1)}, f32[1,256]{1,0:T(1,128)S(1)}, u32[]{:S(2)}, u32[]{:S(2)}) %collective-permute-start.15) | collective-permute-done | bytes 1056 | tf_op jit(solution)/shard_map/ppermute | solution.py:481
  50.1 0.9 %collective-permute-done.14.rest_1_ = f32[1,256]{1,0:T(1,128)S(1)} collective-permute-done((f32[1,256]{1,0:T(1,128)S(1)}, f32[1,256]{1,0:T(1,128)S(1)}, u32[]{:S(2)}, u32[]{:S(2)}) %collective-permute-start.14) | collective-permute-done | bytes 1056 | tf_op jit(solution)/shard_map/ppermute | solution.py:481
  51.0 1.0 %shard_map.84 = (f32[1,4,128,128]{3,2,1,0:T(8,128)}, f32[1,64]{1,0:T(1,128)}) custom-call(f32[4,128,128]{2,1,0:T(8,128)S(1)} %shard_map.80.whole, f32[4,16,128]{2,1,0:T(8,128)S(1)} %get-tuple-element.44.thin, f32[1,256]{1,0:T(1,128)S(1)} %get-tuple-element.45.mortar, f32[1,256]{1,0:T(1,128)S(1)} %add.11.rest_0_, ...), custom_call_target="tpu_custom_call" | custom-call | tf_op jit(solution)/shard_map/pallas_call | solution.py:436
  (26 shorter events, 1.1 us)
Async XLA Ops:
  2.7 12.2 %collective-permute-start = (f32[6,128,128]{2,1,0:T(8,128)S(1)}, f32[6,128,128]{2,1,0:T(8,128)S(1)}, u32[]{:S(2)}, u32[]{:S(2)}) collective-permute-start(f32[6,128,128]{2,1,0:T(8,128)S(1)} %get-tuple-element.29), channel_id=1, source_target_pairs={{0,1},{1,0},{2,3},{3,2},{4,5},{5,4},{6,7},{7,6},{8,9},{9,8},{10,11... | collective-permute-start | bytes 1179656 | tf_op jit(solution)/shard_map/ppermute | solution.py:469
  5.9 18.1 %copy-start = (f32[1,4,128,256]{3,2,1,0:T(8,128)S(1)}, f32[1,4,128,256]{3,2,1,0:T(8,128)}, u32[]{:S(2)}) copy-start(f32[1,4,128,256]{3,2,1,0:T(8,128)} %bot.5) | copy-start | bytes 1572868
  5.9 18.1 %copy-start.1 = (f32[1,4,128,256]{3,2,1,0:T(8,128)S(1)}, f32[1,4,128,256]{3,2,1,0:T(8,128)}, u32[]{:S(2)}) copy-start(f32[1,4,128,256]{3,2,1,0:T(8,128)} %top.5) | copy-start | bytes 1572868
  5.9 9.1 %collective-permute-start.1 = (f32[6,128,128]{2,1,0:T(8,128)S(1)}, f32[6,128,128]{2,1,0:T(8,128)S(1)}, u32[]{:S(2)}, u32[]{:S(2)}) collective-permute-start(f32[6,128,128]{2,1,0:T(8,128)S(1)} %get-tuple-element.30), channel_id=1, source_target_pairs={{0,4},{1,2},{2,1},{3,7},{4,0},{5,6},{6,5},{7,3},{8,12},{9,10},{10,... | collective-permute-start | bytes 1179656 | tf_op jit(solution)/shard_map/ppermute | solution.py:470
  15.9 32.2 %collective-permute-start.2 = (f32[3,128,128]{2,1,0:T(8,128)S(1)}, f32[3,128,128]{2,1,0:T(8,128)S(1)}, u32[]{:S(2)}, u32[]{:S(2)}) collective-permute-start(f32[3,128,128]{2,1,0:T(8,128)S(1)} %get-tuple-element.32), channel_id=1, source_target_pairs={{0,1},{1,0},{2,3},{3,2},{4,5},{5,4},{6,7},{7,6},{8,9},{9,8},{10,11... | collective-permute-start | bytes 589832 | tf_op jit(solution)/shard_map/ppermute | solution.py:469
  18.8 29.3 %collective-permute-start.3 = (f32[3,128,128]{2,1,0:T(8,128)S(1)}, f32[3,128,128]{2,1,0:T(8,128)S(1)}, u32[]{:S(2)}, u32[]{:S(2)}) collective-permute-start(f32[3,128,128]{2,1,0:T(8,128)S(1)} %get-tuple-element.33), channel_id=1, source_target_pairs={{0,4},{1,2},{2,1},{3,7},{4,0},{5,6},{6,5},{7,3},{8,12},{9,10},{10,... | collective-permute-start | bytes 589832 | tf_op jit(solution)/shard_map/ppermute | solution.py:470
  18.8 5.1 %collective-permute-start.4 = (f32[6,16,128]{2,1,0:T(8,128)S(1)}, f32[6,16,128]{2,1,0:T(8,128)S(1)}, u32[]{:S(2)}, u32[]{:S(2)}) collective-permute-start(f32[6,16,128]{2,1,0:T(8,128)S(1)} %get-tuple-element.35), channel_id=1, source_target_pairs={{0,1},{1,0},{2,3},{3,2},{4,5},{5,4},{6,7},{7,6},{8,9},{9,8},{10,11... | collective-permute-start | bytes 147464 | tf_op jit(solution)/shard_map/ppermute | solution.py:469
  20.9 3.1 %collective-permute-start.5 = (f32[6,16,128]{2,1,0:T(8,128)S(1)}, f32[6,16,128]{2,1,0:T(8,128)S(1)}, u32[]{:S(2)}, u32[]{:S(2)}) collective-permute-start(f32[6,16,128]{2,1,0:T(8,128)S(1)} %get-tuple-element.36), channel_id=1, source_target_pairs={{0,4},{1,2},{2,1},{3,7},{4,0},{5,6},{6,5},{7,3},{8,12},{9,10},{10,... | collective-permute-start | bytes 147464 | tf_op jit(solution)/shard_map/ppermute | solution.py:470
  24.6 2.6 %collective-permute-start.6 = (f32[1,256]{1,0:T(1,128)S(1)}, f32[1,256]{1,0:T(1,128)S(1)}, u32[]{:S(2)}, u32[]{:S(2)}) collective-permute-start(f32[1,256]{1,0:T(1,128)S(1)} %get-tuple-element.39), channel_id=1, source_target_pairs={{0,4},{4,0},{8,12},{12,8},{16,20},{20,16},{24,28},{28,24},{1,5},{5... | collective-permute-start | bytes 3080 | tf_op jit(solution)/shard_map/ppermute | solution.py:503
  24.7 4.0 %collective-permute-start.7 = (f32[1,256]{1,0:T(1,128)S(1)}, f32[1,256]{1,0:T(1,128)S(1)}, u32[]{:S(2)}, u32[]{:S(2)}) collective-permute-start(f32[1,256]{1,0:T(1,128)S(1)} %get-tuple-element.40), channel_id=1, source_target_pairs={{0,28},{4,8},{8,4},{12,16},{16,12},{20,24},{24,20},{28,0},{1,29},{... | collective-permute-start | bytes 3080 | tf_op jit(solution)/shard_map/ppermute | solution.py:504
  28.7 4.6 %collective-permute-start.10 = (f32[2,256]{1,0:T(2,128)S(1)}, f32[2,256]{1,0:T(2,128)S(1)}, u32[]{:S(2)}, u32[]{:S(2)}) collective-permute-start(f32[2,256]{1,0:T(2,128)S(1)} %pad_maximum_fusion.rest_0_), channel_id=1, source_target_pairs={{0,1},{1,0},{2,3},{3,2},{4,5},{5,4},{6,7},{7,6},{8,9},{9,8},{10,11... | collective-permute-start | bytes 6152 | tf_op jit(solution)/shard_map/ppermute | solution.py:481
  30.6 4.5 %collective-permute-start.9 = (f32[2,256]{1,0:T(2,128)S(1)}, f32[2,256]{1,0:T(2,128)S(1)}, u32[]{:S(2)}, u32[]{:S(2)}) collective-permute-start(f32[2,256]{1,0:T(2,128)S(1)} %pad_maximum_fusion.rest_0_), channel_id=1, source_target_pairs={{0,2},{1,3},{2,0},{3,1},{4,6},{5,7},{6,4},{7,5},{8,10},{9,11},{10,... | collective-permute-start | bytes 6152 | tf_op jit(solution)/shard_map/ppermute | solution.py:481
  32.0 5.4 %collective-permute-start.8 = (f32[2,256]{1,0:T(2,128)S(1)}, f32[2,256]{1,0:T(2,128)S(1)}, u32[]{:S(2)}, u32[]{:S(2)}) collective-permute-start(f32[2,256]{1,0:T(2,128)S(1)} %pad_maximum_fusion.rest_0_), channel_id=1, source_target_pairs={{0,3},{1,2},{2,1},{3,0},{4,7},{5,6},{6,5},{7,4},{8,11},{9,10},{10,... | collective-permute-start | bytes 6152 | tf_op jit(solution)/shard_map/ppermute | solution.py:481
  37.7 3.9 %collective-permute-start.11 = (f32[3,16,128]{2,1,0:T(8,128)S(1)}, f32[3,16,128]{2,1,0:T(8,128)S(1)}, u32[]{:S(2)}, u32[]{:S(2)}) collective-permute-start(f32[3,16,128]{2,1,0:T(8,128)S(1)} %get-tuple-element.42), channel_id=1, source_target_pairs={{0,1},{1,0},{2,3},{3,2},{4,5},{5,4},{6,7},{7,6},{8,9},{9,8},{10,11... | collective-permute-start | bytes 73736 | tf_op jit(solution)/shard_map/ppermute | solution.py:469
  37.9 3.7 %collective-permute-start.12 = (f32[3,16,128]{2,1,0:T(8,128)S(1)}, f32[3,16,128]{2,1,0:T(8,128)S(1)}, u32[]{:S(2)}, u32[]{:S(2)}) collective-permute-start(f32[3,16,128]{2,1,0:T(8,128)S(1)} %get-tuple-element.43), channel_id=1, source_target_pairs={{0,4},{1,2},{2,1},{3,7},{4,0},{5,6},{6,5},{7,3},{8,12},{9,10},{10,... | collective-permute-start | bytes 73736 | tf_op jit(solution)/shard_map/ppermute | solution.py:470
  42.2 1.5 %collective-permute-start.13 = (f32[1,256]{1,0:T(1,128)S(1)}, f32[1,256]{1,0:T(1,128)S(1)}, u32[]{:S(2)}, u32[]{:S(2)}) collective-permute-start(f32[1,256]{1,0:T(1,128)S(1)} %get-tuple-element.47), channel_id=1, source_target_pairs={{4,0},{8,4},{12,8},{16,12},{20,16},{24,20},{28,24},{0,28},{5,1},{9... | collective-permute-start | bytes 3080 | tf_op jit(solution)/shard_map/ppermute | solution.py:526
  43.7 5.3 %collective-permute-start.16 = (f32[1,256]{1,0:T(1,128)S(1)}, f32[1,256]{1,0:T(1,128)S(1)}, u32[]{:S(2)}, u32[]{:S(2)}) collective-permute-start(f32[1,256]{1,0:T(1,128)S(1)} %add.11.rest_0_), channel_id=1, source_target_pairs={{0,1},{1,0},{2,3},{3,2},{4,5},{5,4},{6,7},{7,6},{8,9},{9,8},{10,11... | collective-permute-start | bytes 3080 | tf_op jit(solution)/shard_map/ppermute | solution.py:481
  45.6 4.5 %collective-permute-start.15 = (f32[1,256]{1,0:T(1,128)S(1)}, f32[1,256]{1,0:T(1,128)S(1)}, u32[]{:S(2)}, u32[]{:S(2)}) collective-permute-start(f32[1,256]{1,0:T(1,128)S(1)} %add.11.rest_0_), channel_id=1, source_target_pairs={{0,2},{1,3},{2,0},{3,1},{4,6},{5,7},{6,4},{7,5},{8,10},{9,11},{10,... | collective-permute-start | bytes 3080 | tf_op jit(solution)/shard_map/ppermute | solution.py:481
  45.6 5.4 %collective-permute-start.14 = (f32[1,256]{1,0:T(1,128)S(1)}, f32[1,256]{1,0:T(1,128)S(1)}, u32[]{:S(2)}, u32[]{:S(2)}) collective-permute-start(f32[1,256]{1,0:T(1,128)S(1)} %add.11.rest_0_), channel_id=1, source_target_pairs={{0,3},{1,2},{2,1},{3,0},{4,7},{5,6},{6,5},{7,4},{8,11},{9,10},{10,... | collective-permute-start | bytes 3080 | tf_op jit(solution)/shard_map/ppermute | solution.py:481

commit v3 on v2

--- a/solution.py
+++ b/solution.py
@@ -231,38 +231,42 @@
     return thin_pass(last, rhs, cx, layers, weight, 0, count)
 
 
-def traces(flux, bot, top):
-    count = len(flux)
-    planes = (SLAB, SLAB - 1)
-    columns = jnp.concatenate([f[at : at + 1] for at in planes for f in flux], axis=0).T
-    sums = []
-    for face, basis in enumerate((bot, top)):
-        total = sum(
-            columns[:, face * count + x : face * count + x + 1] * basis[0, x] for x in range(count)
-        )
-        sums.append(jnp.sum(total, axis=0, keepdims=True))
-    return sums
-
-
-def first_thin(slabs, bot, top, got_a, got_b, p_out, kept, sh_a, sh_b, above, below):
+def trace(flux, plane, basis):
+    columns = jnp.concatenate([f[plane : plane + 1] for f in flux], axis=0)
+    fill = jnp.zeros((SLAB - len(flux), flux[0].shape[1]), F32)
+    columns = jnp.concatenate([columns, fill], axis=0).T
+    total = sum(columns[:, x : x + 1] * basis[0, x] for x in range(len(flux)))
+    return jnp.sum(total, axis=0, keepdims=True)
+
+
+def share_of(flux, bot, top, first, second):
+    def to_above(ref):
+        if ref is not None:
+            ref[...] = trace(flux, SLAB - 1, top)
+
+    def to_below(ref):
+        if ref is not None:
+            ref[...] = trace(flux, SLAB, bot)
+
+    by_parity("block", first, second, to_above, to_below)
+
+
+def first_thin(slabs, bot, top, got_a, got_b, p_out, kept, share, above, below):
     count = bot.shape[1]
     sort_pair((got_a, got_b), above, below)
     source, cx, layers, w = thin_setup(slabs, above, below)
     p = first_three(count, source, cx, layers, w, above, below)
     for x in range(count):
         p_out[x] = p[x]
-    cbot, ctop = traces([layers[x].face * p[x] for x in range(count)], bot, top)
-
-    def to_above(ref):
-        ref[...] = ctop
-
-    def to_below(ref):
-        ref[...] = cbot
-
-    by_parity("block", sh_a, sh_b, to_above, to_below)
+    share_of([layers[x].face * p[x] for x in range(count)], bot, top, None, share)
     for x in range(-1, count + 1):
         for i, v in enumerate((cx[x], w[x], layers[x].cy, layers[x].cz, layers[x].face)):
             kept[x + 1, i] = v
+
+
+def other_share(bot, top, kept, p_in, share):
+    flux = [kept[x + 1, 4] * p_in[x] for x in range(bot.shape[1])]
+    share_of(flux, bot, top, share, None)
 
 
 class Kept(Thin):
@@ -317,8 +321,8 @@
 
 
 def second_thin(
-    slabs, bot, top, kept, p_in, data, edge_a, edge_b,
-    p_out, cbot_out, ctop_out, edge_above, edge_below,
+    slabs, bot, kept, p_in, data, edge_a, edge_b,
+    p_out, flux_out, cbot_out, edge_above, edge_below,
 ):
     count = bot.shape[1]
     sort_pair((edge_a, edge_b), edge_above, edge_below)
@@ -329,7 +333,13 @@
     for x in range(count):
         p_out[x] = p[x]
     flux = [layers[x].face * (p[x] - known[x]) for x in range(count)]
-    cbot_out[...], ctop_out[...] = traces(flux, bot, top)
+    cbot_out[...] = trace(flux, SLAB, bot)
+    for x in range(count):
+        flux_out[x] = flux[x]
+
+
+def top_share(top, flux, ctop_out):
+    ctop_out[...] = trace([flux[x] for x in range(top.shape[1])], SLAB - 1, top)
 
 
 def edge_kernel(src, tx, ty, tz, out_a, out_b):
@@ -388,9 +398,10 @@
 
 
 def second_whole(
-    src, tx, ty, tz, got_a, got_b, p_in, mid_a, mid_b, p_out, above, below, p_above, p_below
+    src, tx, ty, tz, got_a, got_b, p_in, mid_a, mid_b, thin,
+    p_out, above, below, p_above, p_below,
 ):
-    count = src.shape[1]
+    count, rows, cells = src.shape[1:]
     sort_pair((got_a, got_b), above, below)
     sort_pair((mid_a, mid_b), p_above, p_below)
     source, cx, layers, w = whole_setup(src, tx, ty, tz, above, below)
@@ -399,20 +410,6 @@
     w[count] = above[3]
     p3 = {x: p_in[x] for x in range(count)}
     p6 = three_passes(p3, p_above, p_below, source, cx, layers, w, count)
-    for x in range(count):
-        p_out[x] = p6[x]
-
-
-def finish_kernel(whole, thin, mortar, *rest):
-    parts = rest[:-5]
-    p_out, m_out, merged, piece, sems = rest[-5:]
-    total = mortar[...] + MORTAR_STEP * sum(part[...] for part in parts)
-    columns = piece.shape[1]
-    shift = total.shape[1] - lax.axis_index("sub") * columns
-    piece[...] = pltpu.roll(total, lax.rem(shift, total.shape[1]), 1)[:, 0:columns]
-    copies = [pltpu.make_async_copy(piece, m_out, sems.at[0])]
-    copies[0].start()
-    count, rows, cells = whole.shape
     cols = lax.broadcasted_iota(jnp.int32, (rows, cells), 1)
     face = (cols < PASSES) | (cols >= cells - PASSES)
     each = cells // SPAN
@@ -424,11 +421,22 @@
         back = jnp.concatenate(here, axis=0).T
         for x in range(start, stop):
             shift = (cells - (x - start) * SPAN - SLAB) % cells
-            merged[x] = jnp.where(face, pltpu.roll(back, shift, 1), whole[x])
-            copies.append(pltpu.make_async_copy(merged.at[x], p_out.at[0, x], sems.at[x + 1]))
-            copies[-1].start()
-    for copy in copies:
-        copy.wait()
+            p_out[0, x] = jnp.where(face, pltpu.roll(back, shift, 1), p6[x])
+
+
+def finish_kernel(merged, mortar, *rest):
+    parts = rest[:-4]
+    p_out, m_out, piece, sems = rest[-4:]
+    whole = pltpu.make_async_copy(merged, p_out, sems.at[0])
+    whole.start()
+    total = mortar[...] + MORTAR_STEP * sum(part[...] for part in parts)
+    columns = piece.shape[1]
+    shift = total.shape[1] - lax.axis_index("sub") * columns
+    piece[...] = pltpu.roll(total, lax.rem(shift, total.shape[1]), 1)[:, 0:columns]
+    copy = pltpu.make_async_copy(piece, m_out, sems.at[1])
+    copy.start()
+    whole.wait()
+    copy.wait()
 
 
 def call(kernel, outs, args, scratch=(), copies=0, source=pltpu.VMEM, target=pltpu.VMEM):
@@ -492,16 +500,17 @@
     edges = call(edge_kernel, [(EDGE,) + face] * 2, coeffs)
     edges = trade(*edges)
     fixed = (slabs, mortar_bot, mortar_top)
-    third, known, share_a, share_b = call(
+    third, known, share_b = call(
         first_thin,
-        [(count,) + slab, (count + 2, 5) + slab] + [(1, width)] * 2,
+        [(count,) + slab, (count + 2, 5) + slab, (1, width)],
         fixed + near,
         [(EDGE,) + slab] * 2,
     )
     block_one = [(b, b ^ 1) for b in range(blocks)]
     block_two = [(b, (b + 1 if b % 2 else b - 1) % blocks) for b in range(blocks)]
+    other_b = lax.ppermute(share_b, "block", block_two)
+    (share_a,) = call(other_share, [(1, width)], fixed[1:] + (known, third))
     other_a = lax.ppermute(share_a, "block", block_one)
-    other_b = lax.ppermute(share_b, "block", block_two)
     jumps = jnp.concatenate([share_a + other_a, share_b + other_b], axis=0)
     parts = everyone(jumps)
     whole, mid_a, mid_b = call(
@@ -517,27 +526,28 @@
         fixed + (known, third) + tuple(parts),
     )
     got = trade(edge_a, edge_b)
-    slab_out, cbot, ctop = call(
+    slab_out, flux, cbot = call(
         second_thin,
-        [(count,) + slab] + [(1, width)] * 2,
-        fixed + (known, third, data) + got,
+        [(count,) + slab] * 2 + [(1, width)],
+        fixed[:2] + (known, third, data) + got,
         [(MIDDLE,) + slab] * 2,
     )
+    (ctop,) = call(top_share, [(1, width)], (mortar_top, flux))
     upper = lax.ppermute(cbot, "block", [((b + 1) % blocks, b) for b in range(blocks)])
     parts = everyone(ctop + upper)
     (whole,) = call(
         second_whole,
-        [(count,) + face],
-        tuple(coeffs) + edges + (whole,) + middle,
+        [source.shape],
+        tuple(coeffs) + edges + (whole,) + middle + (slab_out,),
         [(EDGE,) + face] * 2 + [(MIDDLE,) + face] * 2,
     )
     columns = width // subs
     return call(
         finish_kernel,
         [source.shape, (1, columns)],
-        (whole, slab_out, mortar) + tuple(parts),
-        [(count,) + face, (1, columns)],
-        copies=count + 1,
+        (whole, mortar) + tuple(parts),
+        [(1, columns)],
+        copies=2,
         target=pltpu.HBM,
     )
 

time: 52.1 us -> 52 us (level)
    pallas_call x8 -> x10, Pallas kernels: 6.54 us -> 6.85 us  [call(): pl.pallas_call(kernel, out_shape=[target(shape, F32) for shape in outs],...]
  transfers between devices with their start and end apart: 17 -> 17, of which waited for: 9 -> 9; matrix products, arithmetic and copies ran while one was open for 0% -> 0% of each run, Pallas kernels for 5% -> 6%
where the time goes in v3:
time: 52 us; the launch traced here: 51.8 us
  waiting for transfers between devices  24.2 us (47%)
  starting transfers between devices  20 us (38%)
  Pallas kernels  6.85 us (13%)
  between operations  0.73 us (1%)
    ppermute x4, waiting for transfers between devices, trade(): first = lax.ppermute(a, names, pair_one)  15.9 us
    ppermute x6, starting transfers between devices, everyone(): parts.append(lax.ppermute(value, 'sub', [(i, i ^ k) for i in range(subs)]))  8.98 us
    ppermute x4, starting transfers between devices, trade(): first = lax.ppermute(a, names, pair_one)  8.23 us
    pallas_call x10, Pallas kernels, call(): pl.pallas_call(kernel, out_shape=[target(shape, F32) for shape in outs],...  6.85 us
    ppermute x6, waiting for transfers between devices, everyone(): parts.append(lax.ppermute(value, 'sub', [(i, i ^ k) for i in range(subs)]))  5.84 us
    ppermute x1, starting transfers between devices, work(): other_b = lax.ppermute(share_b, 'block', block_two)  2.55 us
    ppermute x1, waiting for transfers between devices, work(): other_b = lax.ppermute(share_b, 'block', block_two)  1.41 us
  transfers between devices with their start and end apart: 17, of which 9 were waited for; matrix products, arithmetic and copies ran while one was open for 0% of the time, Pallas kernels for 6%

profile of v3, /device:TPU:0, one launch (start us, length us, event | category | flops | bytes accessed | tf_op | source)
XLA Modules:
  0.0 51.8 jit_solution(16456343708086490010)
XLA Ops:
  0.6 1.9 %shard_map.77 = (f32[1,4,128,128]{3,2,1,0:T(8,128)S(1)}, f32[1,4,128,128]{3,2,1,0:T(8,128)S(1)}, f32[1,4,128,128]{3,2,1,0:T(8,128)S(1)}, f32[1,4,128,128]{3,2,1,...) custom-call(f32[1,4,128,128]{3,2,1,0:T(8,128)} %src.1, ...), custom_call_target="tpu_custom_call" | custom-call | tf_op jit(solution)/shard_map/pallas_call | solution.py:444
  2.7 3.1 %collective-permute-start = (f32[6,128,128]{2,1,0:T(8,128)S(1)}, f32[6,128,128]{2,1,0:T(8,128)S(1)}, u32[]{:S(2)}, u32[]{:S(2)}) collective-permute-start(f32[6,128,128]{2,1,0:T(8,128)S(1)} %get-tuple-element.28), channel_id=1, source_target_pairs={{0,1},{1,0},{2,3},{3,2},{4,5},{5,4},{6,7},{7,6},{8,9},{9,8},{10,11... | collective-permute-start | bytes 1179656 | tf_op jit(solution)/shard_map/ppermute | solution.py:477
  5.9 9.1 %collective-permute-done.got_a = f32[6,128,128]{2,1,0:T(8,128)S(1)} collective-permute-done((f32[6,128,128]{2,1,0:T(8,128)S(1)}, f32[6,128,128]{2,1,0:T(8,128)S(1)}, u32[]{:S(2)}, u32[]{:S(2)}) %collective-permute-start) | collective-permute-done | bytes 393248 | tf_op jit(solution)/shard_map/ppermute | solution.py:477
  15.0 0.9 %shard_map.79 = (f32[4,128,128]{2,1,0:T(8,128)S(1)}, f32[3,128,128]{2,1,0:T(8,128)S(1)}, f32[3,128,128]{2,1,0:T(8,128)S(1)}) custom-call(f32[1,4,128,128]{3,2,1,0:T(8,128)S(1)} %get-tuple-element.24.src, f32[1,4,128,128]{3,2,1,0:T(8,128)S(1)} %get-tuple-element.25.tx, f32[1,4,128,128]{3,2,1,0:T(8,128)S(1)} %get-tuple-element.26.ty, ...), custom_call_target="tpu_custom_call" | custom-call | tf_op jit(solution)/shard_map/pallas_call | solution.py:444
  15.9 2.9 %collective-permute-start.2 = (f32[3,128,128]{2,1,0:T(8,128)S(1)}, f32[3,128,128]{2,1,0:T(8,128)S(1)}, u32[]{:S(2)}, u32[]{:S(2)}) collective-permute-start(f32[3,128,128]{2,1,0:T(8,128)S(1)} %get-tuple-element.31), channel_id=1, source_target_pairs={{0,1},{1,0},{2,3},{3,2},{4,5},{5,4},{6,7},{7,6},{8,9},{9,8},{10,11... | collective-permute-start | bytes 589832 | tf_op jit(solution)/shard_map/ppermute | solution.py:477
  18.9 2.0 %collective-permute-start.4 = (f32[6,16,128]{2,1,0:T(8,128)S(1)}, f32[6,16,128]{2,1,0:T(8,128)S(1)}, u32[]{:S(2)}, u32[]{:S(2)}) collective-permute-start(f32[6,16,128]{2,1,0:T(8,128)S(1)} %get-tuple-element.34), channel_id=1, source_target_pairs={{0,1},{1,0},{2,3},{3,2},{4,5},{5,4},{6,7},{7,6},{8,9},{9,8},{10,11... | collective-permute-start | bytes 147464 | tf_op jit(solution)/shard_map/ppermute | solution.py:477
  20.9 3.1 %collective-permute-done.4.got_a = f32[6,16,128]{2,1,0:T(8,128)S(1)} collective-permute-done((f32[6,16,128]{2,1,0:T(8,128)S(1)}, f32[6,16,128]{2,1,0:T(8,128)S(1)}, u32[]{:S(2)}, u32[]{:S(2)}) %collective-permute-start.4) | collective-permute-done | bytes 49184 | tf_op jit(solution)/shard_map/ppermute | solution.py:477
  24.0 0.6 %shard_map.80 = (f32[4,16,128]{2,1,0:T(8,128)S(1)}, f32[6,5,16,128]{3,2,1,0:T(8,128)S(1)}, f32[1,256]{1,0:T(1,128)S(1)}) custom-call(f32[20,16,128]{2,1,0:T(8,128)S(1)} %get-tuple-element.33.slabs, f32[1,4,128,256]{3,2,1,0:T(8,128)S(1)} %copy-done, f32[1,4,128,256]{3,2,1,0:T(8,128)S(1)} %copy-done.1, f32[6,16,128]{2,1,0:T(8,128)S(1)} %collective-permute-done.4.got_a, ...), custom_call_target="tpu_custom_call" | custom-call | tf_op jit(solution)/shard_map/pallas_call | solution.py:444
  24.9 2.5 %collective-permute-start.7 = (f32[1,256]{1,0:T(1,128)S(1)}, f32[1,256]{1,0:T(1,128)S(1)}, u32[]{:S(2)}, u32[]{:S(2)}) collective-permute-start(f32[1,256]{1,0:T(1,128)S(1)} %get-tuple-element.38), channel_id=1, source_target_pairs={{0,28},{4,8},{8,4},{12,16},{16,12},{20,24},{24,20},{28,0},{1,29},{... | collective-permute-start | bytes 3080 | tf_op jit(solution)/shard_map/ppermute | solution.py:511
  27.5 1.4 %collective-permute-done.7 = f32[1,256]{1,0:T(1,128)S(1)} collective-permute-done((f32[1,256]{1,0:T(1,128)S(1)}, f32[1,256]{1,0:T(1,128)S(1)}, u32[]{:S(2)}, u32[]{:S(2)}) %collective-permute-start.7) | collective-permute-done | bytes 1056 | tf_op jit(solution)/shard_map/ppermute | solution.py:511
  28.9 1.9 %collective-permute-start.10 = (f32[2,256]{1,0:T(2,128)S(1)}, f32[2,256]{1,0:T(2,128)S(1)}, u32[]{:S(2)}, u32[]{:S(2)}) collective-permute-start(f32[2,256]{1,0:T(2,128)S(1)} %pad_maximum_fusion.rest_0_), channel_id=1, source_target_pairs={{0,1},{1,0},{2,3},{3,2},{4,5},{5,4},{6,7},{7,6},{8,9},{9,8},{10,11... | collective-permute-start | bytes 6152 | tf_op jit(solution)/shard_map/ppermute | solution.py:489
  30.8 1.4 %collective-permute-start.9 = (f32[2,256]{1,0:T(2,128)S(1)}, f32[2,256]{1,0:T(2,128)S(1)}, u32[]{:S(2)}, u32[]{:S(2)}) collective-permute-start(f32[2,256]{1,0:T(2,128)S(1)} %pad_maximum_fusion.rest_0_), channel_id=1, source_target_pairs={{0,2},{1,3},{2,0},{3,1},{4,6},{5,7},{6,4},{7,5},{8,10},{9,11},{10,... | collective-permute-start | bytes 6152 | tf_op jit(solution)/shard_map/ppermute | solution.py:489
  32.2 1.3 %collective-permute-start.8 = (f32[2,256]{1,0:T(2,128)S(1)}, f32[2,256]{1,0:T(2,128)S(1)}, u32[]{:S(2)}, u32[]{:S(2)}) collective-permute-start(f32[2,256]{1,0:T(2,128)S(1)} %pad_maximum_fusion.rest_0_), channel_id=1, source_target_pairs={{0,3},{1,2},{2,1},{3,0},{4,7},{5,6},{6,5},{7,4},{8,11},{9,10},{10,... | collective-permute-start | bytes 6152 | tf_op jit(solution)/shard_map/ppermute | solution.py:489
  33.5 1.8 %collective-permute-done.9.rest_2_ = f32[2,256]{1,0:T(2,128)S(1)} collective-permute-done((f32[2,256]{1,0:T(2,128)S(1)}, f32[2,256]{1,0:T(2,128)S(1)}, u32[]{:S(2)}, u32[]{:S(2)}) %collective-permute-start.9) | collective-permute-done | bytes 2080 | tf_op jit(solution)/shard_map/ppermute | solution.py:489
  35.2 2.3 %collective-permute-done.8.rest_1_ = f32[2,256]{1,0:T(2,128)S(1)} collective-permute-done((f32[2,256]{1,0:T(2,128)S(1)}, f32[2,256]{1,0:T(2,128)S(1)}, u32[]{:S(2)}, u32[]{:S(2)}) %collective-permute-start.8) | collective-permute-done | bytes 2080 | tf_op jit(solution)/shard_map/ppermute | solution.py:489
  38.1 3.7 %collective-permute-done.11.edge_a = f32[3,16,128]{2,1,0:T(8,128)S(1)} collective-permute-done((f32[3,16,128]{2,1,0:T(8,128)S(1)}, f32[3,16,128]{2,1,0:T(8,128)S(1)}, u32[]{:S(2)}, u32[]{:S(2)}) %collective-permute-start.11) | collective-permute-done | bytes 24608 | tf_op jit(solution)/shard_map/ppermute | solution.py:477
  41.8 0.5 %shard_map.83 = (f32[4,16,128]{2,1,0:T(8,128)S(1)}, f32[4,16,128]{2,1,0:T(8,128)S(1)}, f32[1,256]{1,0:T(1,128)S(1)}) custom-call(f32[20,16,128]{2,1,0:T(8,128)S(1)} %get-tuple-element.33.slabs, f32[1,4,128,256]{3,2,1,0:T(8,128)S(1)} %copy-done, f32[6,5,16,128]{3,2,1,0:T(8,128)S(1)} %get-tuple-element.36.kept, f32[4,16,128]{2,1,0:T(8,128)S(1)} %get-tuple-element.37.p_in, ...), custom_call_target="tpu_custom_call" | custom-call | tf_op jit(solution)/shard_map/pallas_call | solution.py:444
  42.8 1.0 %collective-permute-done.13 = f32[1,256]{1,0:T(1,128)S(1)} collective-permute-done((f32[1,256]{1,0:T(1,128)S(1)}, f32[1,256]{1,0:T(1,128)S(1)}, u32[]{:S(2)}, u32[]{:S(2)}) %collective-permute-start.13) | collective-permute-done | bytes 1056 | tf_op jit(solution)/shard_map/ppermute | solution.py:536
  43.8 1.9 %collective-permute-start.16 = (f32[1,256]{1,0:T(1,128)S(1)}, f32[1,256]{1,0:T(1,128)S(1)}, u32[]{:S(2)}, u32[]{:S(2)}) collective-permute-start(f32[1,256]{1,0:T(1,128)S(1)} %add.11.rest_0_), channel_id=1, source_target_pairs={{0,1},{1,0},{2,3},{3,2},{4,5},{5,4},{6,7},{7,6},{8,9},{9,8},{10,11... | collective-permute-start | bytes 3080 | tf_op jit(solution)/shard_map/ppermute | solution.py:489
  45.7 2.5 %collective-permute-start.14 = (f32[1,256]{1,0:T(1,128)S(1)}, f32[1,256]{1,0:T(1,128)S(1)}, u32[]{:S(2)}, u32[]{:S(2)}) collective-permute-start(f32[1,256]{1,0:T(1,128)S(1)} %add.11.rest_0_), channel_id=1, source_target_pairs={{0,3},{1,2},{2,1},{3,0},{4,7},{5,6},{6,5},{7,4},{8,11},{9,10},{10,... | collective-permute-start | bytes 3080 | tf_op jit(solution)/shard_map/ppermute | solution.py:489
  48.2 1.1 %shard_map.84.merged = f32[1,4,128,128]{3,2,1,0:T(8,128)S(1)} custom-call(f32[1,4,128,128]{3,2,1,0:T(8,128)S(1)} %get-tuple-element.24.src, f32[1,4,128,128]{3,2,1,0:T(8,128)S(1)} %get-tuple-element.25.tx, f32[1,4,128,128]{3,2,1,0:T(8,128)S(1)} %get-tuple-element.26.ty, f32[1,4,128,128]{3,2,1,0:T(8,128)S(1)} %get-tuple-element.27.tz, ...), custom_call_target="tpu_custom_call" | custom-call | tf_op jit(solution)/shard_map/pallas_call | solution.py:444
  49.3 0.9 %collective-permute-done.15.rest_2_ = f32[1,256]{1,0:T(1,128)S(1)} collective-permute-done((f32[1,256]{1,0:T(1,128)S(1)}, f32[1,256]{1,0:T(1,128)S(1)}, u32[]{:S(2)}, u32[]{:S(2)}) %collective-permute-start.15) | collective-permute-done | bytes 1056 | tf_op jit(solution)/shard_map/ppermute | solution.py:489
  50.2 0.9 %collective-permute-done.14.rest_1_ = f32[1,256]{1,0:T(1,128)S(1)} collective-permute-done((f32[1,256]{1,0:T(1,128)S(1)}, f32[1,256]{1,0:T(1,128)S(1)}, u32[]{:S(2)}, u32[]{:S(2)}) %collective-permute-start.14) | collective-permute-done | bytes 1056 | tf_op jit(solution)/shard_map/ppermute | solution.py:489
  51.1 0.7 %shard_map.86 = (f32[1,4,128,128]{3,2,1,0:T(8,128)}, f32[1,64]{1,0:T(1,128)}) custom-call(f32[1,4,128,128]{3,2,1,0:T(8,128)S(1)} %shard_map.84.merged, f32[1,256]{1,0:T(1,128)S(1)} %get-tuple-element.43.mortar, f32[1,256]{1,0:T(1,128)S(1)} %add.11.rest_0_, f32[1,256]{1,0:T(1,128)S(1)} %collective-permute-done.14.rest_1_, ...), custom_call_target="tpu_custom_call" | custom-call | tf_op jit(solution)/shard_map/pallas_call | solution.py:444
  (28 shorter events, 1.6 us)
Async XLA Ops:
  2.7 12.2 %collective-permute-start = (f32[6,128,128]{2,1,0:T(8,128)S(1)}, f32[6,128,128]{2,1,0:T(8,128)S(1)}, u32[]{:S(2)}, u32[]{:S(2)}) collective-permute-start(f32[6,128,128]{2,1,0:T(8,128)S(1)} %get-tuple-element.28), channel_id=1, source_target_pairs={{0,1},{1,0},{2,3},{3,2},{4,5},{5,4},{6,7},{7,6},{8,9},{9,8},{10,11... | collective-permute-start | bytes 1179656 | tf_op jit(solution)/shard_map/ppermute | solution.py:477
  5.9 18.1 %copy-start = (f32[1,4,128,256]{3,2,1,0:T(8,128)S(1)}, f32[1,4,128,256]{3,2,1,0:T(8,128)}, u32[]{:S(2)}) copy-start(f32[1,4,128,256]{3,2,1,0:T(8,128)} %bot.7) | copy-start | bytes 1572868
  5.9 18.1 %copy-start.1 = (f32[1,4,128,256]{3,2,1,0:T(8,128)S(1)}, f32[1,4,128,256]{3,2,1,0:T(8,128)}, u32[]{:S(2)}) copy-start(f32[1,4,128,256]{3,2,1,0:T(8,128)} %top.7) | copy-start | bytes 1572868
  5.9 9.1 %collective-permute-start.1 = (f32[6,128,128]{2,1,0:T(8,128)S(1)}, f32[6,128,128]{2,1,0:T(8,128)S(1)}, u32[]{:S(2)}, u32[]{:S(2)}) collective-permute-start(f32[6,128,128]{2,1,0:T(8,128)S(1)} %get-tuple-element.29), channel_id=1, source_target_pairs={{0,4},{1,2},{2,1},{3,7},{4,0},{5,6},{6,5},{7,3},{8,12},{9,10},{10,... | collective-permute-start | bytes 1179656 | tf_op jit(solution)/shard_map/ppermute | solution.py:478
  15.9 32.3 %collective-permute-start.2 = (f32[3,128,128]{2,1,0:T(8,128)S(1)}, f32[3,128,128]{2,1,0:T(8,128)S(1)}, u32[]{:S(2)}, u32[]{:S(2)}) collective-permute-start(f32[3,128,128]{2,1,0:T(8,128)S(1)} %get-tuple-element.31), channel_id=1, source_target_pairs={{0,1},{1,0},{2,3},{3,2},{4,5},{5,4},{6,7},{7,6},{8,9},{9,8},{10,11... | collective-permute-start | bytes 589832 | tf_op jit(solution)/shard_map/ppermute | solution.py:477
  18.9 29.3 %collective-permute-start.3 = (f32[3,128,128]{2,1,0:T(8,128)S(1)}, f32[3,128,128]{2,1,0:T(8,128)S(1)}, u32[]{:S(2)}, u32[]{:S(2)}) collective-permute-start(f32[3,128,128]{2,1,0:T(8,128)S(1)} %get-tuple-element.32), channel_id=1, source_target_pairs={{0,4},{1,2},{2,1},{3,7},{4,0},{5,6},{6,5},{7,3},{8,12},{9,10},{10,... | collective-permute-start | bytes 589832 | tf_op jit(solution)/shard_map/ppermute | solution.py:478
  18.9 5.1 %collective-permute-start.4 = (f32[6,16,128]{2,1,0:T(8,128)S(1)}, f32[6,16,128]{2,1,0:T(8,128)S(1)}, u32[]{:S(2)}, u32[]{:S(2)}) collective-permute-start(f32[6,16,128]{2,1,0:T(8,128)S(1)} %get-tuple-element.34), channel_id=1, source_target_pairs={{0,1},{1,0},{2,3},{3,2},{4,5},{5,4},{6,7},{7,6},{8,9},{9,8},{10,11... | collective-permute-start | bytes 147464 | tf_op jit(solution)/shard_map/ppermute | solution.py:477
  20.9 3.1 %collective-permute-start.5 = (f32[6,16,128]{2,1,0:T(8,128)S(1)}, f32[6,16,128]{2,1,0:T(8,128)S(1)}, u32[]{:S(2)}, u32[]{:S(2)}) collective-permute-start(f32[6,16,128]{2,1,0:T(8,128)S(1)} %get-tuple-element.35), channel_id=1, source_target_pairs={{0,4},{1,2},{2,1},{3,7},{4,0},{5,6},{6,5},{7,3},{8,12},{9,10},{10,... | collective-permute-start | bytes 147464 | tf_op jit(solution)/shard_map/ppermute | solution.py:478
  24.8 2.6 %collective-permute-start.6 = (f32[1,256]{1,0:T(1,128)S(1)}, f32[1,256]{1,0:T(1,128)S(1)}, u32[]{:S(2)}, u32[]{:S(2)}) collective-permute-start(f32[1,256]{1,0:T(1,128)S(1)} %shard_map.81), channel_id=1, source_target_pairs={{0,4},{4,0},{8,12},{12,8},{16,20},{20,16},{24,28},{28,24},{1,5},{5... | collective-permute-start | bytes 3080 | tf_op jit(solution)/shard_map/ppermute | solution.py:513
  24.9 4.0 %collective-permute-start.7 = (f32[1,256]{1,0:T(1,128)S(1)}, f32[1,256]{1,0:T(1,128)S(1)}, u32[]{:S(2)}, u32[]{:S(2)}) collective-permute-start(f32[1,256]{1,0:T(1,128)S(1)} %get-tuple-element.38), channel_id=1, source_target_pairs={{0,28},{4,8},{8,4},{12,16},{16,12},{20,24},{24,20},{28,0},{1,29},{... | collective-permute-start | bytes 3080 | tf_op jit(solution)/shard_map/ppermute | solution.py:511
  28.9 4.6 %collective-permute-start.10 = (f32[2,256]{1,0:T(2,128)S(1)}, f32[2,256]{1,0:T(2,128)S(1)}, u32[]{:S(2)}, u32[]{:S(2)}) collective-permute-start(f32[2,256]{1,0:T(2,128)S(1)} %pad_maximum_fusion.rest_0_), channel_id=1, source_target_pairs={{0,1},{1,0},{2,3},{3,2},{4,5},{5,4},{6,7},{7,6},{8,9},{9,8},{10,11... | collective-permute-start | bytes 6152 | tf_op jit(solution)/shard_map/ppermute | solution.py:489
  30.8 4.5 %collective-permute-start.9 = (f32[2,256]{1,0:T(2,128)S(1)}, f32[2,256]{1,0:T(2,128)S(1)}, u32[]{:S(2)}, u32[]{:S(2)}) collective-permute-start(f32[2,256]{1,0:T(2,128)S(1)} %pad_maximum_fusion.rest_0_), channel_id=1, source_target_pairs={{0,2},{1,3},{2,0},{3,1},{4,6},{5,7},{6,4},{7,5},{8,10},{9,11},{10,... | collective-permute-start | bytes 6152 | tf_op jit(solution)/shard_map/ppermute | solution.py:489
  32.2 5.4 %collective-permute-start.8 = (f32[2,256]{1,0:T(2,128)S(1)}, f32[2,256]{1,0:T(2,128)S(1)}, u32[]{:S(2)}, u32[]{:S(2)}) collective-permute-start(f32[2,256]{1,0:T(2,128)S(1)} %pad_maximum_fusion.rest_0_), channel_id=1, source_target_pairs={{0,3},{1,2},{2,1},{3,0},{4,7},{5,6},{6,5},{7,4},{8,11},{9,10},{10,... | collective-permute-start | bytes 6152 | tf_op jit(solution)/shard_map/ppermute | solution.py:489
  37.9 3.9 %collective-permute-start.11 = (f32[3,16,128]{2,1,0:T(8,128)S(1)}, f32[3,16,128]{2,1,0:T(8,128)S(1)}, u32[]{:S(2)}, u32[]{:S(2)}) collective-permute-start(f32[3,16,128]{2,1,0:T(8,128)S(1)} %get-tuple-element.40), channel_id=1, source_target_pairs={{0,1},{1,0},{2,3},{3,2},{4,5},{5,4},{6,7},{7,6},{8,9},{9,8},{10,11... | collective-permute-start | bytes 73736 | tf_op jit(solution)/shard_map/ppermute | solution.py:477
  38.1 3.7 %collective-permute-start.12 = (f32[3,16,128]{2,1,0:T(8,128)S(1)}, f32[3,16,128]{2,1,0:T(8,128)S(1)}, u32[]{:S(2)}, u32[]{:S(2)}) collective-permute-start(f32[3,16,128]{2,1,0:T(8,128)S(1)} %get-tuple-element.41), channel_id=1, source_target_pairs={{0,4},{1,2},{2,1},{3,7},{4,0},{5,6},{6,5},{7,3},{8,12},{9,10},{10,... | collective-permute-start | bytes 73736 | tf_op jit(solution)/shard_map/ppermute | solution.py:478
  42.3 1.5 %collective-permute-start.13 = (f32[1,256]{1,0:T(1,128)S(1)}, f32[1,256]{1,0:T(1,128)S(1)}, u32[]{:S(2)}, u32[]{:S(2)}) collective-permute-start(f32[1,256]{1,0:T(1,128)S(1)} %get-tuple-element.45), channel_id=1, source_target_pairs={{4,0},{8,4},{12,8},{16,12},{20,16},{24,20},{28,24},{0,28},{5,1},{9... | collective-permute-start | bytes 3080 | tf_op jit(solution)/shard_map/ppermute | solution.py:536
  43.8 5.5 %collective-permute-start.16 = (f32[1,256]{1,0:T(1,128)S(1)}, f32[1,256]{1,0:T(1,128)S(1)}, u32[]{:S(2)}, u32[]{:S(2)}) collective-permute-start(f32[1,256]{1,0:T(1,128)S(1)} %add.11.rest_0_), channel_id=1, source_target_pairs={{0,1},{1,0},{2,3},{3,2},{4,5},{5,4},{6,7},{7,6},{8,9},{9,8},{10,11... | collective-permute-start | bytes 3080 | tf_op jit(solution)/shard_map/ppermute | solution.py:489
  45.7 4.5 %collective-permute-start.15 = (f32[1,256]{1,0:T(1,128)S(1)}, f32[1,256]{1,0:T(1,128)S(1)}, u32[]{:S(2)}, u32[]{:S(2)}) collective-permute-start(f32[1,256]{1,0:T(1,128)S(1)} %add.11.rest_0_), channel_id=1, source_target_pairs={{0,2},{1,3},{2,0},{3,1},{4,6},{5,7},{6,4},{7,5},{8,10},{9,11},{10,... | collective-permute-start | bytes 3080 | tf_op jit(solution)/shard_map/ppermute | solution.py:489
  45.7 5.4 %collective-permute-start.14 = (f32[1,256]{1,0:T(1,128)S(1)}, f32[1,256]{1,0:T(1,128)S(1)}, u32[]{:S(2)}, u32[]{:S(2)}) collective-permute-start(f32[1,256]{1,0:T(1,128)S(1)} %add.11.rest_0_), channel_id=1, source_target_pairs={{0,3},{1,2},{2,1},{3,0},{4,7},{5,6},{6,5},{7,4},{8,11},{9,10},{10,... | collective-permute-start | bytes 3080 | tf_op jit(solution)/shard_map/ppermute | solution.py:489

commit v4 on v3

--- a/solution.py
+++ b/solution.py
@@ -54,14 +54,15 @@
 
 
 class Thin:
-    def __init__(self, trans_y, trans_z, zsum, has_bot, has_top):
+    def __init__(self, trans_y, trans_z, z_next, has_bot, has_top):
         rows = lax.broadcasted_iota(jnp.int32, trans_y.shape, 0)
         cols = lax.broadcasted_iota(jnp.int32, trans_y.shape, 1)
         self.cy = jnp.where(cols > 0, trans_y, 0.0)
         self.cz = jnp.where(rows == SLAB, 0.0, trans_z)
         top = jnp.where(rows == SLAB - 1, trans_z * has_top, 0.0)
         self.face = jnp.where(rows == SLAB, trans_z * has_bot, top)
-        self.diag = self.cy + following(self.cy, 1) + zsum
+        after = jnp.where(rows == SLAB - 1, 0.0, z_next)
+        self.diag = self.cy + following(self.cy, 1) + self.cz + after + self.face
 
     def around(self, p):
         return (
@@ -130,10 +131,10 @@
             slabs[k] = turned[(k - start) * SPAN : (k - start + 1) * SPAN]
 
     for x in range(count):
-        zsum = along_z(tz_v[0, x], has_bot, has_top)[1]
-        for item in (tx_v[0, x], src_v[0, x], ty_v[0, x], tz_v[0, x], zsum):
+        for which, ref in enumerate((tx_v, src_v, ty_v, tz_v, tz_v)):
             j = done % each
-            turned = pltpu.roll(item, (SPAN * j + SLAB) % cells, 1)
+            ahead = which // 4
+            turned = pltpu.roll(ref[0, x], (SPAN * j + SLAB - ahead) % cells, 1)
             packed = jnp.where(slot == j, turned, packed)
             done += 1
             if done % each == 0 or done == count * ITEMS:
@@ -150,7 +151,7 @@
     p_top = RELAX * item(1, top - 1) / (make(top - 1).diag + item(0, top - 1) + item(0, top))
 
     def upward(ref):
-        values = (item(0, top), p_top, item(1, top), item(4, top), item(2, top), item(3, top))
+        values = (item(0, top), p_top, item(1, top), make(top).diag, item(2, top), item(3, top))
         for i, v in enumerate(values):
             ref[i] = v
 
@@ -195,6 +196,7 @@
         for x in range(count)
     }
     layers[-1] = Thin(below[4], below[5], below[3], has_bot, has_top)
+    layers[-1].diag = below[3]
     layers[count] = Thin(above[4], above[5], above[3], has_bot, has_top)
     w = {x: RELAX / (layers[x].diag + cx[x] + cx[x + 1]) for x in range(-1, count)}
     w[count] = above[3]
@@ -232,10 +234,11 @@
 
 
 def trace(flux, plane, basis):
-    columns = jnp.concatenate([f[plane : plane + 1] for f in flux], axis=0)
-    fill = jnp.zeros((SLAB - len(flux), flux[0].shape[1]), F32)
-    columns = jnp.concatenate([columns, fill], axis=0).T
-    total = sum(columns[:, x : x + 1] * basis[0, x] for x in range(len(flux)))
+    rows, width = basis.shape[2:]
+    total = 0.0
+    for x, f in enumerate(flux):
+        turned = jnp.broadcast_to(f[plane : plane + 1], (rows, rows)).T
+        total += jnp.concatenate([turned] * (width // rows), axis=1) * basis[0, x]
     return jnp.sum(total, axis=0, keepdims=True)
 
 
@@ -300,12 +303,14 @@
     own = jnp.where(even, jumps[0:1], jumps[1:2])
     under = jnp.where(even, jumps[1:2], jumps[0:1])
     mortar_out[...] = own
-    columns = [
-        jnp.sum(ref[0, x] * values, axis=1, keepdims=True)
-        for ref, values in ((bot, under), (top, own))
-        for x in range(count)
-    ]
-    data = jnp.concatenate(columns, axis=1).T
+    rows, width = bot.shape[2:]
+    data = []
+    for ref, values in ((bot, under), (top, own)):
+        for x in range(count):
+            product = ref[0, x] * values
+            folded = sum(product[:, i : i + rows] for i in range(0, width, rows))
+            data.append(jnp.sum(folded.T, axis=0, keepdims=True))
+    data = jnp.concatenate(data, axis=0)
     data_out[...] = data
     source, cx, layers, w = thin_again(slabs, kept)
     rhs = with_faces(source, layers, data, count)[1]

time: 52 us -> 51.5 us (level)
  Pallas kernels: 6.85 us -> 6.3 us
    pallas_call x10, Pallas kernels: 6.85 us -> 6.3 us  [call(): pl.pallas_call(kernel, out_shape=[target(shape, F32) for shape in outs],...]
  transfers between devices with their start and end apart: 17 -> 17, of which waited for: 9 -> 9; matrix products, arithmetic and copies ran while one was open for 0% -> 0% of each run, Pallas kernels for 6% -> 5%
where the time goes in v4:
time: 51.5 us; the launch traced here: 51.4 us
  waiting for transfers between devices  24.3 us (47%)
  starting transfers between devices  20 us (39%)
  Pallas kernels  6.3 us (12%)
  between operations  0.73 us (1%)
    ppermute x4, waiting for transfers between devices, trade(): first = lax.ppermute(a, names, pair_one)  15.9 us
    ppermute x6, starting transfers between devices, everyone(): parts.append(lax.ppermute(value, 'sub', [(i, i ^ k) for i in range(subs)]))  8.98 us
    ppermute x4, starting transfers between devices, trade(): first = lax.ppermute(a, names, pair_one)  8.23 us
    pallas_call x10, Pallas kernels, call(): pl.pallas_call(kernel, out_shape=[target(shape, F32) for shape in outs],...  6.3 us
    ppermute x6, waiting for transfers between devices, everyone(): parts.append(lax.ppermute(value, 'sub', [(i, i ^ k) for i in range(subs)]))  5.84 us
    ppermute x1, starting transfers between devices, work(): other_b = lax.ppermute(share_b, 'block', block_two)  2.55 us
    ppermute x1, waiting for transfers between devices, work(): other_b = lax.ppermute(share_b, 'block', block_two)  1.41 us
    ppermute x1, waiting for transfers between devices, work(): lax.ppermute(cbot, 'block', [((b + 1) % blocks, b) for b in range(blocks)])  1.15 us
  transfers between devices with their start and end apart: 17, of which 9 were waited for; matrix products, arithmetic and copies ran while one was open for 0% of the time, Pallas kernels for 5%

profile of v4, /device:TPU:0, one launch (start us, length us, event | category | flops | bytes accessed | tf_op | source)
XLA Modules:
  0.0 51.4 jit_solution(7677450382074127201)
XLA Ops:
  0.6 1.9 %shard_map.77 = (f32[1,4,128,128]{3,2,1,0:T(8,128)S(1)}, f32[1,4,128,128]{3,2,1,0:T(8,128)S(1)}, f32[1,4,128,128]{3,2,1,0:T(8,128)S(1)}, f32[1,4,128,128]{3,2,1,...) custom-call(f32[1,4,128,128]{3,2,1,0:T(8,128)} %src.1, ...), custom_call_target="tpu_custom_call" | custom-call | tf_op jit(solution)/shard_map/pallas_call | solution.py:449
  2.7 3.1 %collective-permute-start = (f32[6,128,128]{2,1,0:T(8,128)S(1)}, f32[6,128,128]{2,1,0:T(8,128)S(1)}, u32[]{:S(2)}, u32[]{:S(2)}) collective-permute-start(f32[6,128,128]{2,1,0:T(8,128)S(1)} %get-tuple-element.28), channel_id=1, source_target_pairs={{0,1},{1,0},{2,3},{3,2},{4,5},{5,4},{6,7},{7,6},{8,9},{9,8},{10,11... | collective-permute-start | bytes 1179656 | tf_op jit(solution)/shard_map/ppermute | solution.py:482
  5.9 9.1 %collective-permute-done.got_a = f32[6,128,128]{2,1,0:T(8,128)S(1)} collective-permute-done((f32[6,128,128]{2,1,0:T(8,128)S(1)}, f32[6,128,128]{2,1,0:T(8,128)S(1)}, u32[]{:S(2)}, u32[]{:S(2)}) %collective-permute-start) | collective-permute-done | bytes 393248 | tf_op jit(solution)/shard_map/ppermute | solution.py:482
  15.0 0.9 %shard_map.79 = (f32[4,128,128]{2,1,0:T(8,128)S(1)}, f32[3,128,128]{2,1,0:T(8,128)S(1)}, f32[3,128,128]{2,1,0:T(8,128)S(1)}) custom-call(f32[1,4,128,128]{3,2,1,0:T(8,128)S(1)} %get-tuple-element.24.src, f32[1,4,128,128]{3,2,1,0:T(8,128)S(1)} %get-tuple-element.25.tx, f32[1,4,128,128]{3,2,1,0:T(8,128)S(1)} %get-tuple-element.26.ty, ...), custom_call_target="tpu_custom_call" | custom-call | tf_op jit(solution)/shard_map/pallas_call | solution.py:449
  15.9 2.9 %collective-permute-start.2 = (f32[3,128,128]{2,1,0:T(8,128)S(1)}, f32[3,128,128]{2,1,0:T(8,128)S(1)}, u32[]{:S(2)}, u32[]{:S(2)}) collective-permute-start(f32[3,128,128]{2,1,0:T(8,128)S(1)} %get-tuple-element.31), channel_id=1, source_target_pairs={{0,1},{1,0},{2,3},{3,2},{4,5},{5,4},{6,7},{7,6},{8,9},{9,8},{10,11... | collective-permute-start | bytes 589832 | tf_op jit(solution)/shard_map/ppermute | solution.py:482
  18.9 2.0 %collective-permute-start.4 = (f32[6,16,128]{2,1,0:T(8,128)S(1)}, f32[6,16,128]{2,1,0:T(8,128)S(1)}, u32[]{:S(2)}, u32[]{:S(2)}) collective-permute-start(f32[6,16,128]{2,1,0:T(8,128)S(1)} %get-tuple-element.34), channel_id=1, source_target_pairs={{0,1},{1,0},{2,3},{3,2},{4,5},{5,4},{6,7},{7,6},{8,9},{9,8},{10,11... | collective-permute-start | bytes 147464 | tf_op jit(solution)/shard_map/ppermute | solution.py:482
  20.9 3.1 %collective-permute-done.4.got_a = f32[6,16,128]{2,1,0:T(8,128)S(1)} collective-permute-done((f32[6,16,128]{2,1,0:T(8,128)S(1)}, f32[6,16,128]{2,1,0:T(8,128)S(1)}, u32[]{:S(2)}, u32[]{:S(2)}) %collective-permute-start.4) | collective-permute-done | bytes 49184 | tf_op jit(solution)/shard_map/ppermute | solution.py:482
  24.0 0.4 shard_map.80
  24.7 2.5 %collective-permute-start.7 = (f32[1,256]{1,0:T(1,128)S(1)}, f32[1,256]{1,0:T(1,128)S(1)}, u32[]{:S(2)}, u32[]{:S(2)}) collective-permute-start(f32[1,256]{1,0:T(1,128)S(1)} %get-tuple-element.38), channel_id=1, source_target_pairs={{0,28},{4,8},{8,4},{12,16},{16,12},{20,24},{24,20},{28,0},{1,29},{... | collective-permute-start | bytes 3080 | tf_op jit(solution)/shard_map/ppermute | solution.py:516
  27.2 1.4 %collective-permute-done.7 = f32[1,256]{1,0:T(1,128)S(1)} collective-permute-done((f32[1,256]{1,0:T(1,128)S(1)}, f32[1,256]{1,0:T(1,128)S(1)}, u32[]{:S(2)}, u32[]{:S(2)}) %collective-permute-start.7) | collective-permute-done | bytes 1056 | tf_op jit(solution)/shard_map/ppermute | solution.py:516
  28.6 1.9 %collective-permute-start.10 = (f32[2,256]{1,0:T(2,128)S(1)}, f32[2,256]{1,0:T(2,128)S(1)}, u32[]{:S(2)}, u32[]{:S(2)}) collective-permute-start(f32[2,256]{1,0:T(2,128)S(1)} %pad_maximum_fusion.rest_0_), channel_id=1, source_target_pairs={{0,1},{1,0},{2,3},{3,2},{4,5},{5,4},{6,7},{7,6},{8,9},{9,8},{10,11... | collective-permute-start | bytes 6152 | tf_op jit(solution)/shard_map/ppermute | solution.py:494
  30.5 1.4 %collective-permute-start.9 = (f32[2,256]{1,0:T(2,128)S(1)}, f32[2,256]{1,0:T(2,128)S(1)}, u32[]{:S(2)}, u32[]{:S(2)}) collective-permute-start(f32[2,256]{1,0:T(2,128)S(1)} %pad_maximum_fusion.rest_0_), channel_id=1, source_target_pairs={{0,2},{1,3},{2,0},{3,1},{4,6},{5,7},{6,4},{7,5},{8,10},{9,11},{10,... | collective-permute-start | bytes 6152 | tf_op jit(solution)/shard_map/ppermute | solution.py:494
  31.9 1.3 %collective-permute-start.8 = (f32[2,256]{1,0:T(2,128)S(1)}, f32[2,256]{1,0:T(2,128)S(1)}, u32[]{:S(2)}, u32[]{:S(2)}) collective-permute-start(f32[2,256]{1,0:T(2,128)S(1)} %pad_maximum_fusion.rest_0_), channel_id=1, source_target_pairs={{0,3},{1,2},{2,1},{3,0},{4,7},{5,6},{6,5},{7,4},{8,11},{9,10},{10,... | collective-permute-start | bytes 6152 | tf_op jit(solution)/shard_map/ppermute | solution.py:494
  33.2 1.8 %collective-permute-done.9.rest_2_ = f32[2,256]{1,0:T(2,128)S(1)} collective-permute-done((f32[2,256]{1,0:T(2,128)S(1)}, f32[2,256]{1,0:T(2,128)S(1)}, u32[]{:S(2)}, u32[]{:S(2)}) %collective-permute-start.9) | collective-permute-done | bytes 2080 | tf_op jit(solution)/shard_map/ppermute | solution.py:494
  35.0 2.3 %collective-permute-done.8.rest_1_ = f32[2,256]{1,0:T(2,128)S(1)} collective-permute-done((f32[2,256]{1,0:T(2,128)S(1)}, f32[2,256]{1,0:T(2,128)S(1)}, u32[]{:S(2)}, u32[]{:S(2)}) %collective-permute-start.8) | collective-permute-done | bytes 2080 | tf_op jit(solution)/shard_map/ppermute | solution.py:494
  37.8 3.7 %collective-permute-done.11.edge_a = f32[3,16,128]{2,1,0:T(8,128)S(1)} collective-permute-done((f32[3,16,128]{2,1,0:T(8,128)S(1)}, f32[3,16,128]{2,1,0:T(8,128)S(1)}, u32[]{:S(2)}, u32[]{:S(2)}) %collective-permute-start.11) | collective-permute-done | bytes 24608 | tf_op jit(solution)/shard_map/ppermute | solution.py:482
  41.5 0.4 shard_map.83
  42.2 1.2 %collective-permute-done.13 = f32[1,256]{1,0:T(1,128)S(1)} collective-permute-done((f32[1,256]{1,0:T(1,128)S(1)}, f32[1,256]{1,0:T(1,128)S(1)}, u32[]{:S(2)}, u32[]{:S(2)}) %collective-permute-start.13) | collective-permute-done | bytes 1056 | tf_op jit(solution)/shard_map/ppermute | solution.py:541
  43.4 1.9 %collective-permute-start.16 = (f32[1,256]{1,0:T(1,128)S(1)}, f32[1,256]{1,0:T(1,128)S(1)}, u32[]{:S(2)}, u32[]{:S(2)}) collective-permute-start(f32[1,256]{1,0:T(1,128)S(1)} %add.11.rest_0_), channel_id=1, source_target_pairs={{0,1},{1,0},{2,3},{3,2},{4,5},{5,4},{6,7},{7,6},{8,9},{9,8},{10,11... | collective-permute-start | bytes 3080 | tf_op jit(solution)/shard_map/ppermute | solution.py:494
  45.3 2.5 %collective-permute-start.14 = (f32[1,256]{1,0:T(1,128)S(1)}, f32[1,256]{1,0:T(1,128)S(1)}, u32[]{:S(2)}, u32[]{:S(2)}) collective-permute-start(f32[1,256]{1,0:T(1,128)S(1)} %add.11.rest_0_), channel_id=1, source_target_pairs={{0,3},{1,2},{2,1},{3,0},{4,7},{5,6},{6,5},{7,4},{8,11},{9,10},{10,... | collective-permute-start | bytes 3080 | tf_op jit(solution)/shard_map/ppermute | solution.py:494
  47.8 1.1 %shard_map.84.merged = f32[1,4,128,128]{3,2,1,0:T(8,128)S(1)} custom-call(f32[1,4,128,128]{3,2,1,0:T(8,128)S(1)} %get-tuple-element.24.src, f32[1,4,128,128]{3,2,1,0:T(8,128)S(1)} %get-tuple-element.25.tx, f32[1,4,128,128]{3,2,1,0:T(8,128)S(1)} %get-tuple-element.26.ty, f32[1,4,128,128]{3,2,1,0:T(8,128)S(1)} %get-tuple-element.27.tz, ...), custom_call_target="tpu_custom_call" | custom-call | tf_op jit(solution)/shard_map/pallas_call | solution.py:449
  48.9 0.9 %collective-permute-done.15.rest_2_ = f32[1,256]{1,0:T(1,128)S(1)} collective-permute-done((f32[1,256]{1,0:T(1,128)S(1)}, f32[1,256]{1,0:T(1,128)S(1)}, u32[]{:S(2)}, u32[]{:S(2)}) %collective-permute-start.15) | collective-permute-done | bytes 1056 | tf_op jit(solution)/shard_map/ppermute | solution.py:494
  49.8 0.9 %collective-permute-done.14.rest_1_ = f32[1,256]{1,0:T(1,128)S(1)} collective-permute-done((f32[1,256]{1,0:T(1,128)S(1)}, f32[1,256]{1,0:T(1,128)S(1)}, u32[]{:S(2)}, u32[]{:S(2)}) %collective-permute-start.14) | collective-permute-done | bytes 1056 | tf_op jit(solution)/shard_map/ppermute | solution.py:494
  50.7 0.7 %shard_map.86 = (f32[1,4,128,128]{3,2,1,0:T(8,128)}, f32[1,64]{1,0:T(1,128)}) custom-call(f32[1,4,128,128]{3,2,1,0:T(8,128)S(1)} %shard_map.84.merged, f32[1,256]{1,0:T(1,128)S(1)} %get-tuple-element.43.mortar, f32[1,256]{1,0:T(1,128)S(1)} %add.11.rest_0_, f32[1,256]{1,0:T(1,128)S(1)} %collective-permute-done.14.rest_1_, ...), custom_call_target="tpu_custom_call" | custom-call | tf_op jit(solution)/shard_map/pallas_call | solution.py:449
  (28 shorter events, 1.3 us)
Async XLA Ops:
  2.7 12.2 %collective-permute-start = (f32[6,128,128]{2,1,0:T(8,128)S(1)}, f32[6,128,128]{2,1,0:T(8,128)S(1)}, u32[]{:S(2)}, u32[]{:S(2)}) collective-permute-start(f32[6,128,128]{2,1,0:T(8,128)S(1)} %get-tuple-element.28), channel_id=1, source_target_pairs={{0,1},{1,0},{2,3},{3,2},{4,5},{5,4},{6,7},{7,6},{8,9},{9,8},{10,11... | collective-permute-start | bytes 1179656 | tf_op jit(solution)/shard_map/ppermute | solution.py:482
  5.9 18.1 %copy-start = (f32[1,4,128,256]{3,2,1,0:T(8,128)S(1)}, f32[1,4,128,256]{3,2,1,0:T(8,128)}, u32[]{:S(2)}) copy-start(f32[1,4,128,256]{3,2,1,0:T(8,128)} %bot.7) | copy-start | bytes 1572868
  5.9 18.1 %copy-start.1 = (f32[1,4,128,256]{3,2,1,0:T(8,128)S(1)}, f32[1,4,128,256]{3,2,1,0:T(8,128)}, u32[]{:S(2)}) copy-start(f32[1,4,128,256]{3,2,1,0:T(8,128)} %top.7) | copy-start | bytes 1572868
  5.9 9.1 %collective-permute-start.1 = (f32[6,128,128]{2,1,0:T(8,128)S(1)}, f32[6,128,128]{2,1,0:T(8,128)S(1)}, u32[]{:S(2)}, u32[]{:S(2)}) collective-permute-start(f32[6,128,128]{2,1,0:T(8,128)S(1)} %get-tuple-element.29), channel_id=1, source_target_pairs={{0,4},{1,2},{2,1},{3,7},{4,0},{5,6},{6,5},{7,3},{8,12},{9,10},{10,... | collective-permute-start | bytes 1179656 | tf_op jit(solution)/shard_map/ppermute | solution.py:483
  15.9 31.9 %collective-permute-start.2 = (f32[3,128,128]{2,1,0:T(8,128)S(1)}, f32[3,128,128]{2,1,0:T(8,128)S(1)}, u32[]{:S(2)}, u32[]{:S(2)}) collective-permute-start(f32[3,128,128]{2,1,0:T(8,128)S(1)} %get-tuple-element.31), channel_id=1, source_target_pairs={{0,1},{1,0},{2,3},{3,2},{4,5},{5,4},{6,7},{7,6},{8,9},{9,8},{10,11... | collective-permute-start | bytes 589832 | tf_op jit(solution)/shard_map/ppermute | solution.py:482
  18.9 28.9 %collective-permute-start.3 = (f32[3,128,128]{2,1,0:T(8,128)S(1)}, f32[3,128,128]{2,1,0:T(8,128)S(1)}, u32[]{:S(2)}, u32[]{:S(2)}) collective-permute-start(f32[3,128,128]{2,1,0:T(8,128)S(1)} %get-tuple-element.32), channel_id=1, source_target_pairs={{0,4},{1,2},{2,1},{3,7},{4,0},{5,6},{6,5},{7,3},{8,12},{9,10},{10,... | collective-permute-start | bytes 589832 | tf_op jit(solution)/shard_map/ppermute | solution.py:483
  18.9 5.1 %collective-permute-start.4 = (f32[6,16,128]{2,1,0:T(8,128)S(1)}, f32[6,16,128]{2,1,0:T(8,128)S(1)}, u32[]{:S(2)}, u32[]{:S(2)}) collective-permute-start(f32[6,16,128]{2,1,0:T(8,128)S(1)} %get-tuple-element.34), channel_id=1, source_target_pairs={{0,1},{1,0},{2,3},{3,2},{4,5},{5,4},{6,7},{7,6},{8,9},{9,8},{10,11... | collective-permute-start | bytes 147464 | tf_op jit(solution)/shard_map/ppermute | solution.py:482
  20.9 3.1 %collective-permute-start.5 = (f32[6,16,128]{2,1,0:T(8,128)S(1)}, f32[6,16,128]{2,1,0:T(8,128)S(1)}, u32[]{:S(2)}, u32[]{:S(2)}) collective-permute-start(f32[6,16,128]{2,1,0:T(8,128)S(1)} %get-tuple-element.35), channel_id=1, source_target_pairs={{0,4},{1,2},{2,1},{3,7},{4,0},{5,6},{6,5},{7,3},{8,12},{9,10},{10,... | collective-permute-start | bytes 147464 | tf_op jit(solution)/shard_map/ppermute | solution.py:483
  24.6 2.6 %collective-permute-start.6 = (f32[1,256]{1,0:T(1,128)S(1)}, f32[1,256]{1,0:T(1,128)S(1)}, u32[]{:S(2)}, u32[]{:S(2)}) collective-permute-start(f32[1,256]{1,0:T(1,128)S(1)} %shard_map.81), channel_id=1, source_target_pairs={{0,4},{4,0},{8,12},{12,8},{16,20},{20,16},{24,28},{28,24},{1,5},{5... | collective-permute-start | bytes 3080 | tf_op jit(solution)/shard_map/ppermute | solution.py:518
  24.7 4.0 %collective-permute-start.7 = (f32[1,256]{1,0:T(1,128)S(1)}, f32[1,256]{1,0:T(1,128)S(1)}, u32[]{:S(2)}, u32[]{:S(2)}) collective-permute-start(f32[1,256]{1,0:T(1,128)S(1)} %get-tuple-element.38), channel_id=1, source_target_pairs={{0,28},{4,8},{8,4},{12,16},{16,12},{20,24},{24,20},{28,0},{1,29},{... | collective-permute-start | bytes 3080 | tf_op jit(solution)/shard_map/ppermute | solution.py:516
  28.6 4.6 %collective-permute-start.10 = (f32[2,256]{1,0:T(2,128)S(1)}, f32[2,256]{1,0:T(2,128)S(1)}, u32[]{:S(2)}, u32[]{:S(2)}) collective-permute-start(f32[2,256]{1,0:T(2,128)S(1)} %pad_maximum_fusion.rest_0_), channel_id=1, source_target_pairs={{0,1},{1,0},{2,3},{3,2},{4,5},{5,4},{6,7},{7,6},{8,9},{9,8},{10,11... | collective-permute-start | bytes 6152 | tf_op jit(solution)/shard_map/ppermute | solution.py:494
  30.5 4.5 %collective-permute-start.9 = (f32[2,256]{1,0:T(2,128)S(1)}, f32[2,256]{1,0:T(2,128)S(1)}, u32[]{:S(2)}, u32[]{:S(2)}) collective-permute-start(f32[2,256]{1,0:T(2,128)S(1)} %pad_maximum_fusion.rest_0_), channel_id=1, source_target_pairs={{0,2},{1,3},{2,0},{3,1},{4,6},{5,7},{6,4},{7,5},{8,10},{9,11},{10,... | collective-permute-start | bytes 6152 | tf_op jit(solution)/shard_map/ppermute | solution.py:494
  31.9 5.4 %collective-permute-start.8 = (f32[2,256]{1,0:T(2,128)S(1)}, f32[2,256]{1,0:T(2,128)S(1)}, u32[]{:S(2)}, u32[]{:S(2)}) collective-permute-start(f32[2,256]{1,0:T(2,128)S(1)} %pad_maximum_fusion.rest_0_), channel_id=1, source_target_pairs={{0,3},{1,2},{2,1},{3,0},{4,7},{5,6},{6,5},{7,4},{8,11},{9,10},{10,... | collective-permute-start | bytes 6152 | tf_op jit(solution)/shard_map/ppermute | solution.py:494
  37.6 3.9 %collective-permute-start.11 = (f32[3,16,128]{2,1,0:T(8,128)S(1)}, f32[3,16,128]{2,1,0:T(8,128)S(1)}, u32[]{:S(2)}, u32[]{:S(2)}) collective-permute-start(f32[3,16,128]{2,1,0:T(8,128)S(1)} %get-tuple-element.40), channel_id=1, source_target_pairs={{0,1},{1,0},{2,3},{3,2},{4,5},{5,4},{6,7},{7,6},{8,9},{9,8},{10,11... | collective-permute-start | bytes 73736 | tf_op jit(solution)/shard_map/ppermute | solution.py:482
  37.8 3.7 %collective-permute-start.12 = (f32[3,16,128]{2,1,0:T(8,128)S(1)}, f32[3,16,128]{2,1,0:T(8,128)S(1)}, u32[]{:S(2)}, u32[]{:S(2)}) collective-permute-start(f32[3,16,128]{2,1,0:T(8,128)S(1)} %get-tuple-element.41), channel_id=1, source_target_pairs={{0,4},{1,2},{2,1},{3,7},{4,0},{5,6},{6,5},{7,3},{8,12},{9,10},{10,... | collective-permute-start | bytes 73736 | tf_op jit(solution)/shard_map/ppermute | solution.py:483
  41.9 1.5 %collective-permute-start.13 = (f32[1,256]{1,0:T(1,128)S(1)}, f32[1,256]{1,0:T(1,128)S(1)}, u32[]{:S(2)}, u32[]{:S(2)}) collective-permute-start(f32[1,256]{1,0:T(1,128)S(1)} %get-tuple-element.45), channel_id=1, source_target_pairs={{4,0},{8,4},{12,8},{16,12},{20,16},{24,20},{28,24},{0,28},{5,1},{9... | collective-permute-start | bytes 3080 | tf_op jit(solution)/shard_map/ppermute | solution.py:541
  43.4 5.5 %collective-permute-start.16 = (f32[1,256]{1,0:T(1,128)S(1)}, f32[1,256]{1,0:T(1,128)S(1)}, u32[]{:S(2)}, u32[]{:S(2)}) collective-permute-start(f32[1,256]{1,0:T(1,128)S(1)} %add.11.rest_0_), channel_id=1, source_target_pairs={{0,1},{1,0},{2,3},{3,2},{4,5},{5,4},{6,7},{7,6},{8,9},{9,8},{10,11... | collective-permute-start | bytes 3080 | tf_op jit(solution)/shard_map/ppermute | solution.py:494
  45.3 4.5 %collective-permute-start.15 = (f32[1,256]{1,0:T(1,128)S(1)}, f32[1,256]{1,0:T(1,128)S(1)}, u32[]{:S(2)}, u32[]{:S(2)}) collective-permute-start(f32[1,256]{1,0:T(1,128)S(1)} %add.11.rest_0_), channel_id=1, source_target_pairs={{0,2},{1,3},{2,0},{3,1},{4,6},{5,7},{6,4},{7,5},{8,10},{9,11},{10,... | collective-permute-start | bytes 3080 | tf_op jit(solution)/shard_map/ppermute | solution.py:494
  45.3 5.4 %collective-permute-start.14 = (f32[1,256]{1,0:T(1,128)S(1)}, f32[1,256]{1,0:T(1,128)S(1)}, u32[]{:S(2)}, u32[]{:S(2)}) collective-permute-start(f32[1,256]{1,0:T(1,128)S(1)} %add.11.rest_0_), channel_id=1, source_target_pairs={{0,3},{1,2},{2,1},{3,0},{4,7},{5,6},{6,5},{7,4},{8,11},{9,10},{10,... | collective-permute-start | bytes 3080 | tf_op jit(solution)/shard_map/ppermute | solution.py:494

commit v5 on v4

--- a/solution.py
+++ b/solution.py
@@ -13,6 +13,7 @@
 F32 = jnp.float32
 EDGE = 6
 MIDDLE = 3
+WHOLE = 5
 HALO = 2
 SLAB = 8
 SPAN = 2 * SLAB
@@ -359,11 +360,11 @@
     p_top = RELAX * src[0, top - 1] / (make(top - 1).diag + tx[0, top - 1] + tx[0, top])
 
     def upward(ref):
-        for i, v in enumerate((tx[0, top], p_top, src[0, top], src[0, top], ty[0, top], tz[0, top])):
+        for i, v in enumerate((tx[0, top], p_top, src[0, top], ty[0, top], tz[0, top])):
             ref[i] = v
 
     def downward(ref):
-        for i, v in enumerate((tx[0, 0], p_low, q_low, w_low, ty[0, 0], tz[0, 0])):
+        for i, v in enumerate((tx[0, 0], p_low, q_low, w_low)):
             ref[i] = v
 
     by_parity("sub", out_a, out_b, upward, downward)
@@ -379,7 +380,7 @@
     source = {x: src[0, x] for x in range(count)}
     source[-1] = below[2]
     layers = {x: Layer(ty[0, x], tz[0, x], has_bot, has_top) for x in range(count)}
-    layers[-1] = Layer(below[4], below[5], has_bot, has_top)
+    layers[-1] = Layer(below[3], below[4], has_bot, has_top)
     weight = {x: RELAX / (layers[x].diag + cx[x] + cx[x + 1]) for x in range(-1, count)}
     return source, cx, layers, weight
 
@@ -393,12 +394,17 @@
         p_out[x] = p3[x]
     last = count - 1
 
+    def downward(ref):
+        edge_data(ref, p3, 0, 1, cx[1], source, cx, layers, w)
+        ref[3] = ty[0, 0]
+        ref[4] = tz[0, 0]
+
     by_parity(
         "sub",
         mid_a,
         mid_b,
         lambda ref: edge_data(ref, p3, last, last - 1, cx[last], source, cx, layers, w),
-        lambda ref: edge_data(ref, p3, 0, 1, cx[1], source, cx, layers, w),
+        downward,
     )
 
 
@@ -411,7 +417,7 @@
     sort_pair((mid_a, mid_b), p_above, p_below)
     source, cx, layers, w = whole_setup(src, tx, ty, tz, above, below)
     has_bot, has_top, _, _ = flags()
-    layers[count] = Layer(above[4], above[5], has_bot, has_top)
+    layers[count] = Layer(p_above[3], p_above[4], has_bot, has_top)
     w[count] = above[3]
     p3 = {x: p_in[x] for x in range(count)}
     p6 = three_passes(p3, p_above, p_below, source, cx, layers, w, count)
@@ -502,7 +508,7 @@
         source=pltpu.HBM,
     )
     near = trade(near_a, near_b)
-    edges = call(edge_kernel, [(EDGE,) + face] * 2, coeffs)
+    edges = call(edge_kernel, [(WHOLE,) + face] * 2, coeffs)
     edges = trade(*edges)
     fixed = (slabs, mortar_bot, mortar_top)
     third, known, share_b = call(
@@ -520,9 +526,9 @@
     parts = everyone(jumps)
     whole, mid_a, mid_b = call(
         first_whole,
-        [(count,) + face] + [(MIDDLE,) + face] * 2,
+        [(count,) + face] + [(WHOLE,) + face] * 2,
         tuple(coeffs) + edges,
-        [(EDGE,) + face] * 2,
+        [(WHOLE,) + face] * 2,
     )
     middle = trade(mid_a, mid_b)
     data, edge_a, edge_b, mortar = call(
@@ -544,7 +550,7 @@
         second_whole,
         [source.shape],
         tuple(coeffs) + edges + (whole,) + middle + (slab_out,),
-        [(EDGE,) + face] * 2 + [(MIDDLE,) + face] * 2,
+        [(WHOLE,) + face] * 4,
     )
     columns = width // subs
     return call(

time: 51.5 us -> 52.9 us (1.027)
  waiting for transfers between devices: 24.3 us -> 26 us
    ppermute x4, waiting for transfers between devices: 15.9 us -> 17.3 us  [trade(): first = lax.ppermute(a, names, pair_one)]
where the time goes in v5:
time: 52.9 us; the launch traced here: 52.8 us
  waiting for transfers between devices  26 us (49%)
  starting transfers between devices  19.7 us (37%)
  Pallas kernels  6.29 us (12%)
  between operations  0.75 us (1%)
    ppermute x4, waiting for transfers between devices, trade(): first = lax.ppermute(a, names, pair_one)  17.3 us
    ppermute x6, starting transfers between devices, everyone(): parts.append(lax.ppermute(value, 'sub', [(i, i ^ k) for i in range(subs)]))  8.84 us
    ppermute x4, starting transfers between devices, trade(): first = lax.ppermute(a, names, pair_one)  8.14 us
    pallas_call x10, Pallas kernels, call(): pl.pallas_call(kernel, out_shape=[target(shape, F32) for shape in outs],...  6.29 us
    ppermute x6, waiting for transfers between devices, everyone(): parts.append(lax.ppermute(value, 'sub', [(i, i ^ k) for i in range(subs)]))  6.1 us
    ppermute x1, starting transfers between devices, work(): other_b = lax.ppermute(share_b, 'block', block_two)  2.55 us
    ppermute x1, waiting for transfers between devices, work(): other_b = lax.ppermute(share_b, 'block', block_two)  1.41 us
    ppermute x1, waiting for transfers between devices, work(): lax.ppermute(cbot, 'block', [((b + 1) % blocks, b) for b in range(blocks)])  1.14 us
  transfers between devices with their start and end apart: 17, of which 9 were waited for; matrix products, arithmetic and copies ran while one was open for 0% of the time, Pallas kernels for 5%

profile of v5, /device:TPU:0, one launch (start us, length us, event | category | flops | bytes accessed | tf_op | source)
XLA Modules:
  0.0 52.8 jit_solution(3820821610465585377)
XLA Ops:
  0.6 1.9 %shard_map.77 = (f32[1,4,128,128]{3,2,1,0:T(8,128)S(1)}, f32[1,4,128,128]{3,2,1,0:T(8,128)S(1)}, f32[1,4,128,128]{3,2,1,0:T(8,128)S(1)}, f32[1,4,128,128]{3,2,1,...) custom-call(f32[1,4,128,128]{3,2,1,0:T(8,128)} %src.1, ...), custom_call_target="tpu_custom_call" | custom-call | tf_op jit(solution)/shard_map/pallas_call | solution.py:455
  2.7 3.1 %collective-permute-start = (f32[5,128,128]{2,1,0:T(8,128)S(1)}, f32[5,128,128]{2,1,0:T(8,128)S(1)}, u32[]{:S(2)}, u32[]{:S(2)}) collective-permute-start(f32[5,128,128]{2,1,0:T(8,128)S(1)} %get-tuple-element.28), channel_id=1, source_target_pairs={{0,1},{1,0},{2,3},{3,2},{4,5},{5,4},{6,7},{7,6},{8,9},{9,8},{10,11... | collective-permute-start | bytes 983048 | tf_op jit(solution)/shard_map/ppermute | solution.py:488
  5.9 7.7 %collective-permute-done.got_a = f32[5,128,128]{2,1,0:T(8,128)S(1)} collective-permute-done((f32[5,128,128]{2,1,0:T(8,128)S(1)}, f32[5,128,128]{2,1,0:T(8,128)S(1)}, u32[]{:S(2)}, u32[]{:S(2)}) %collective-permute-start) | collective-permute-done | bytes 327712 | tf_op jit(solution)/shard_map/ppermute | solution.py:488
  13.6 0.9 %shard_map.79 = (f32[4,128,128]{2,1,0:T(8,128)S(1)}, f32[5,128,128]{2,1,0:T(8,128)S(1)}, f32[5,128,128]{2,1,0:T(8,128)S(1)}) custom-call(f32[1,4,128,128]{3,2,1,0:T(8,128)S(1)} %get-tuple-element.24.src, f32[1,4,128,128]{3,2,1,0:T(8,128)S(1)} %get-tuple-element.25.tx, f32[1,4,128,128]{3,2,1,0:T(8,128)S(1)} %get-tuple-element.26.ty, ...), custom_call_target="tpu_custom_call" | custom-call | tf_op jit(solution)/shard_map/pallas_call | solution.py:455
  14.5 2.9 %collective-permute-start.2 = (f32[5,128,128]{2,1,0:T(8,128)S(1)}, f32[5,128,128]{2,1,0:T(8,128)S(1)}, u32[]{:S(2)}, u32[]{:S(2)}) collective-permute-start(f32[5,128,128]{2,1,0:T(8,128)S(1)} %get-tuple-element.31), channel_id=1, source_target_pairs={{0,1},{1,0},{2,3},{3,2},{4,5},{5,4},{6,7},{7,6},{8,9},{9,8},{10,11... | collective-permute-start | bytes 983048 | tf_op jit(solution)/shard_map/ppermute | solution.py:488
  17.4 2.0 %collective-permute-start.4 = (f32[6,16,128]{2,1,0:T(8,128)S(1)}, f32[6,16,128]{2,1,0:T(8,128)S(1)}, u32[]{:S(2)}, u32[]{:S(2)}) collective-permute-start(f32[6,16,128]{2,1,0:T(8,128)S(1)} %get-tuple-element.34), channel_id=1, source_target_pairs={{0,1},{1,0},{2,3},{3,2},{4,5},{5,4},{6,7},{7,6},{8,9},{9,8},{10,11... | collective-permute-start | bytes 147464 | tf_op jit(solution)/shard_map/ppermute | solution.py:488
  19.5 5.9 %collective-permute-done.4.got_a = f32[6,16,128]{2,1,0:T(8,128)S(1)} collective-permute-done((f32[6,16,128]{2,1,0:T(8,128)S(1)}, f32[6,16,128]{2,1,0:T(8,128)S(1)}, u32[]{:S(2)}, u32[]{:S(2)}) %collective-permute-start.4) | collective-permute-done | bytes 49184 | tf_op jit(solution)/shard_map/ppermute | solution.py:488
  25.4 0.4 shard_map.80
  26.1 2.5 %collective-permute-start.7 = (f32[1,256]{1,0:T(1,128)S(1)}, f32[1,256]{1,0:T(1,128)S(1)}, u32[]{:S(2)}, u32[]{:S(2)}) collective-permute-start(f32[1,256]{1,0:T(1,128)S(1)} %get-tuple-element.38), channel_id=1, source_target_pairs={{0,28},{4,8},{8,4},{12,16},{16,12},{20,24},{24,20},{28,0},{1,29},{... | collective-permute-start | bytes 3080 | tf_op jit(solution)/shard_map/ppermute | solution.py:522
  28.6 1.4 %collective-permute-done.7 = f32[1,256]{1,0:T(1,128)S(1)} collective-permute-done((f32[1,256]{1,0:T(1,128)S(1)}, f32[1,256]{1,0:T(1,128)S(1)}, u32[]{:S(2)}, u32[]{:S(2)}) %collective-permute-start.7) | collective-permute-done | bytes 1056 | tf_op jit(solution)/shard_map/ppermute | solution.py:522
  30.0 1.9 %collective-permute-start.10 = (f32[2,256]{1,0:T(2,128)S(1)}, f32[2,256]{1,0:T(2,128)S(1)}, u32[]{:S(2)}, u32[]{:S(2)}) collective-permute-start(f32[2,256]{1,0:T(2,128)S(1)} %pad_maximum_fusion.rest_0_), channel_id=1, source_target_pairs={{0,1},{1,0},{2,3},{3,2},{4,5},{5,4},{6,7},{7,6},{8,9},{9,8},{10,11... | collective-permute-start | bytes 6152 | tf_op jit(solution)/shard_map/ppermute | solution.py:500
  31.9 1.4 %collective-permute-start.9 = (f32[2,256]{1,0:T(2,128)S(1)}, f32[2,256]{1,0:T(2,128)S(1)}, u32[]{:S(2)}, u32[]{:S(2)}) collective-permute-start(f32[2,256]{1,0:T(2,128)S(1)} %pad_maximum_fusion.rest_0_), channel_id=1, source_target_pairs={{0,2},{1,3},{2,0},{3,1},{4,6},{5,7},{6,4},{7,5},{8,10},{9,11},{10,... | collective-permute-start | bytes 6152 | tf_op jit(solution)/shard_map/ppermute | solution.py:500
  33.3 1.2 %collective-permute-start.8 = (f32[2,256]{1,0:T(2,128)S(1)}, f32[2,256]{1,0:T(2,128)S(1)}, u32[]{:S(2)}, u32[]{:S(2)}) collective-permute-start(f32[2,256]{1,0:T(2,128)S(1)} %pad_maximum_fusion.rest_0_), channel_id=1, source_target_pairs={{0,3},{1,2},{2,1},{3,0},{4,7},{5,6},{6,5},{7,4},{8,11},{9,10},{10,... | collective-permute-start | bytes 6152 | tf_op jit(solution)/shard_map/ppermute | solution.py:500
  34.5 1.9 %collective-permute-done.9.rest_2_ = f32[2,256]{1,0:T(2,128)S(1)} collective-permute-done((f32[2,256]{1,0:T(2,128)S(1)}, f32[2,256]{1,0:T(2,128)S(1)}, u32[]{:S(2)}, u32[]{:S(2)}) %collective-permute-start.9) | collective-permute-done | bytes 2080 | tf_op jit(solution)/shard_map/ppermute | solution.py:500
  36.4 2.3 %collective-permute-done.8.rest_1_ = f32[2,256]{1,0:T(2,128)S(1)} collective-permute-done((f32[2,256]{1,0:T(2,128)S(1)}, f32[2,256]{1,0:T(2,128)S(1)}, u32[]{:S(2)}, u32[]{:S(2)}) %collective-permute-start.8) | collective-permute-done | bytes 2080 | tf_op jit(solution)/shard_map/ppermute | solution.py:500
  39.2 3.7 %collective-permute-done.11.edge_a = f32[3,16,128]{2,1,0:T(8,128)S(1)} collective-permute-done((f32[3,16,128]{2,1,0:T(8,128)S(1)}, f32[3,16,128]{2,1,0:T(8,128)S(1)}, u32[]{:S(2)}, u32[]{:S(2)}) %collective-permute-start.11) | collective-permute-done | bytes 24608 | tf_op jit(solution)/shard_map/ppermute | solution.py:488
  42.9 0.4 shard_map.83
  43.5 1.1 %collective-permute-done.13 = f32[1,256]{1,0:T(1,128)S(1)} collective-permute-done((f32[1,256]{1,0:T(1,128)S(1)}, f32[1,256]{1,0:T(1,128)S(1)}, u32[]{:S(2)}, u32[]{:S(2)}) %collective-permute-start.13) | collective-permute-done | bytes 1056 | tf_op jit(solution)/shard_map/ppermute | solution.py:547
  44.7 2.0 %collective-permute-start.16 = (f32[1,256]{1,0:T(1,128)S(1)}, f32[1,256]{1,0:T(1,128)S(1)}, u32[]{:S(2)}, u32[]{:S(2)}) collective-permute-start(f32[1,256]{1,0:T(1,128)S(1)} %add.11.rest_0_), channel_id=1, source_target_pairs={{0,1},{1,0},{2,3},{3,2},{4,5},{5,4},{6,7},{7,6},{8,9},{9,8},{10,11... | collective-permute-start | bytes 3080 | tf_op jit(solution)/shard_map/ppermute | solution.py:500
  46.7 2.4 %collective-permute-start.14 = (f32[1,256]{1,0:T(1,128)S(1)}, f32[1,256]{1,0:T(1,128)S(1)}, u32[]{:S(2)}, u32[]{:S(2)}) collective-permute-start(f32[1,256]{1,0:T(1,128)S(1)} %add.11.rest_0_), channel_id=1, source_target_pairs={{0,3},{1,2},{2,1},{3,0},{4,7},{5,6},{6,5},{7,4},{8,11},{9,10},{10,... | collective-permute-start | bytes 3080 | tf_op jit(solution)/shard_map/ppermute | solution.py:500
  49.1 1.1 %shard_map.84.merged = f32[1,4,128,128]{3,2,1,0:T(8,128)S(1)} custom-call(f32[1,4,128,128]{3,2,1,0:T(8,128)S(1)} %get-tuple-element.24.src, f32[1,4,128,128]{3,2,1,0:T(8,128)S(1)} %get-tuple-element.25.tx, f32[1,4,128,128]{3,2,1,0:T(8,128)S(1)} %get-tuple-element.26.ty, f32[1,4,128,128]{3,2,1,0:T(8,128)S(1)} %get-tuple-element.27.tz, ...), custom_call_target="tpu_custom_call" | custom-call | tf_op jit(solution)/shard_map/pallas_call | solution.py:455
  50.2 1.0 %collective-permute-done.15.rest_2_ = f32[1,256]{1,0:T(1,128)S(1)} collective-permute-done((f32[1,256]{1,0:T(1,128)S(1)}, f32[1,256]{1,0:T(1,128)S(1)}, u32[]{:S(2)}, u32[]{:S(2)}) %collective-permute-start.15) | collective-permute-done | bytes 1056 | tf_op jit(solution)/shard_map/ppermute | solution.py:500
  51.2 0.9 %collective-permute-done.14.rest_1_ = f32[1,256]{1,0:T(1,128)S(1)} collective-permute-done((f32[1,256]{1,0:T(1,128)S(1)}, f32[1,256]{1,0:T(1,128)S(1)}, u32[]{:S(2)}, u32[]{:S(2)}) %collective-permute-start.14) | collective-permute-done | bytes 1056 | tf_op jit(solution)/shard_map/ppermute | solution.py:500
  52.1 0.7 %shard_map.86 = (f32[1,4,128,128]{3,2,1,0:T(8,128)}, f32[1,64]{1,0:T(1,128)}) custom-call(f32[1,4,128,128]{3,2,1,0:T(8,128)S(1)} %shard_map.84.merged, f32[1,256]{1,0:T(1,128)S(1)} %get-tuple-element.43.mortar, f32[1,256]{1,0:T(1,128)S(1)} %add.11.rest_0_, f32[1,256]{1,0:T(1,128)S(1)} %collective-permute-done.14.rest_1_, ...), custom_call_target="tpu_custom_call" | custom-call | tf_op jit(solution)/shard_map/pallas_call | solution.py:455
  (28 shorter events, 1.2 us)
Async XLA Ops:
  2.7 10.8 %collective-permute-start = (f32[5,128,128]{2,1,0:T(8,128)S(1)}, f32[5,128,128]{2,1,0:T(8,128)S(1)}, u32[]{:S(2)}, u32[]{:S(2)}) collective-permute-start(f32[5,128,128]{2,1,0:T(8,128)S(1)} %get-tuple-element.28), channel_id=1, source_target_pairs={{0,1},{1,0},{2,3},{3,2},{4,5},{5,4},{6,7},{7,6},{8,9},{9,8},{10,11... | collective-permute-start | bytes 983048 | tf_op jit(solution)/shard_map/ppermute | solution.py:488
  5.9 19.5 %copy-start = (f32[1,4,128,256]{3,2,1,0:T(8,128)S(1)}, f32[1,4,128,256]{3,2,1,0:T(8,128)}, u32[]{:S(2)}) copy-start(f32[1,4,128,256]{3,2,1,0:T(8,128)} %bot.7) | copy-start | bytes 1572868
  5.9 19.5 %copy-start.1 = (f32[1,4,128,256]{3,2,1,0:T(8,128)S(1)}, f32[1,4,128,256]{3,2,1,0:T(8,128)}, u32[]{:S(2)}) copy-start(f32[1,4,128,256]{3,2,1,0:T(8,128)} %top.7) | copy-start | bytes 1572868
  5.9 7.7 %collective-permute-start.1 = (f32[5,128,128]{2,1,0:T(8,128)S(1)}, f32[5,128,128]{2,1,0:T(8,128)S(1)}, u32[]{:S(2)}, u32[]{:S(2)}) collective-permute-start(f32[5,128,128]{2,1,0:T(8,128)S(1)} %get-tuple-element.29), channel_id=1, source_target_pairs={{0,4},{1,2},{2,1},{3,7},{4,0},{5,6},{6,5},{7,3},{8,12},{9,10},{10,... | collective-permute-start | bytes 983048 | tf_op jit(solution)/shard_map/ppermute | solution.py:489
  14.5 34.6 %collective-permute-start.2 = (f32[5,128,128]{2,1,0:T(8,128)S(1)}, f32[5,128,128]{2,1,0:T(8,128)S(1)}, u32[]{:S(2)}, u32[]{:S(2)}) collective-permute-start(f32[5,128,128]{2,1,0:T(8,128)S(1)} %get-tuple-element.31), channel_id=1, source_target_pairs={{0,1},{1,0},{2,3},{3,2},{4,5},{5,4},{6,7},{7,6},{8,9},{9,8},{10,11... | collective-permute-start | bytes 983048 | tf_op jit(solution)/shard_map/ppermute | solution.py:488
  17.4 31.6 %collective-permute-start.3 = (f32[5,128,128]{2,1,0:T(8,128)S(1)}, f32[5,128,128]{2,1,0:T(8,128)S(1)}, u32[]{:S(2)}, u32[]{:S(2)}) collective-permute-start(f32[5,128,128]{2,1,0:T(8,128)S(1)} %get-tuple-element.32), channel_id=1, source_target_pairs={{0,4},{1,2},{2,1},{3,7},{4,0},{5,6},{6,5},{7,3},{8,12},{9,10},{10,... | collective-permute-start | bytes 983048 | tf_op jit(solution)/shard_map/ppermute | solution.py:489
  17.4 7.9 %collective-permute-start.4 = (f32[6,16,128]{2,1,0:T(8,128)S(1)}, f32[6,16,128]{2,1,0:T(8,128)S(1)}, u32[]{:S(2)}, u32[]{:S(2)}) collective-permute-start(f32[6,16,128]{2,1,0:T(8,128)S(1)} %get-tuple-element.34), channel_id=1, source_target_pairs={{0,1},{1,0},{2,3},{3,2},{4,5},{5,4},{6,7},{7,6},{8,9},{9,8},{10,11... | collective-permute-start | bytes 147464 | tf_op jit(solution)/shard_map/ppermute | solution.py:488
  19.5 5.9 %collective-permute-start.5 = (f32[6,16,128]{2,1,0:T(8,128)S(1)}, f32[6,16,128]{2,1,0:T(8,128)S(1)}, u32[]{:S(2)}, u32[]{:S(2)}) collective-permute-start(f32[6,16,128]{2,1,0:T(8,128)S(1)} %get-tuple-element.35), channel_id=1, source_target_pairs={{0,4},{1,2},{2,1},{3,7},{4,0},{5,6},{6,5},{7,3},{8,12},{9,10},{10,... | collective-permute-start | bytes 147464 | tf_op jit(solution)/shard_map/ppermute | solution.py:489
  26.0 2.6 %collective-permute-start.6 = (f32[1,256]{1,0:T(1,128)S(1)}, f32[1,256]{1,0:T(1,128)S(1)}, u32[]{:S(2)}, u32[]{:S(2)}) collective-permute-start(f32[1,256]{1,0:T(1,128)S(1)} %shard_map.81), channel_id=1, source_target_pairs={{0,4},{4,0},{8,12},{12,8},{16,20},{20,16},{24,28},{28,24},{1,5},{5... | collective-permute-start | bytes 3080 | tf_op jit(solution)/shard_map/ppermute | solution.py:524
  26.1 4.0 %collective-permute-start.7 = (f32[1,256]{1,0:T(1,128)S(1)}, f32[1,256]{1,0:T(1,128)S(1)}, u32[]{:S(2)}, u32[]{:S(2)}) collective-permute-start(f32[1,256]{1,0:T(1,128)S(1)} %get-tuple-element.38), channel_id=1, source_target_pairs={{0,28},{4,8},{8,4},{12,16},{16,12},{20,24},{24,20},{28,0},{1,29},{... | collective-permute-start | bytes 3080 | tf_op jit(solution)/shard_map/ppermute | solution.py:522
  30.0 4.5 %collective-permute-start.10 = (f32[2,256]{1,0:T(2,128)S(1)}, f32[2,256]{1,0:T(2,128)S(1)}, u32[]{:S(2)}, u32[]{:S(2)}) collective-permute-start(f32[2,256]{1,0:T(2,128)S(1)} %pad_maximum_fusion.rest_0_), channel_id=1, source_target_pairs={{0,1},{1,0},{2,3},{3,2},{4,5},{5,4},{6,7},{7,6},{8,9},{9,8},{10,11... | collective-permute-start | bytes 6152 | tf_op jit(solution)/shard_map/ppermute | solution.py:500
  31.9 4.5 %collective-permute-start.9 = (f32[2,256]{1,0:T(2,128)S(1)}, f32[2,256]{1,0:T(2,128)S(1)}, u32[]{:S(2)}, u32[]{:S(2)}) collective-permute-start(f32[2,256]{1,0:T(2,128)S(1)} %pad_maximum_fusion.rest_0_), channel_id=1, source_target_pairs={{0,2},{1,3},{2,0},{3,1},{4,6},{5,7},{6,4},{7,5},{8,10},{9,11},{10,... | collective-permute-start | bytes 6152 | tf_op jit(solution)/shard_map/ppermute | solution.py:500
  33.3 5.4 %collective-permute-start.8 = (f32[2,256]{1,0:T(2,128)S(1)}, f32[2,256]{1,0:T(2,128)S(1)}, u32[]{:S(2)}, u32[]{:S(2)}) collective-permute-start(f32[2,256]{1,0:T(2,128)S(1)} %pad_maximum_fusion.rest_0_), channel_id=1, source_target_pairs={{0,3},{1,2},{2,1},{3,0},{4,7},{5,6},{6,5},{7,4},{8,11},{9,10},{10,... | collective-permute-start | bytes 6152 | tf_op jit(solution)/shard_map/ppermute | solution.py:500
  39.0 3.9 %collective-permute-start.11 = (f32[3,16,128]{2,1,0:T(8,128)S(1)}, f32[3,16,128]{2,1,0:T(8,128)S(1)}, u32[]{:S(2)}, u32[]{:S(2)}) collective-permute-start(f32[3,16,128]{2,1,0:T(8,128)S(1)} %get-tuple-element.40), channel_id=1, source_target_pairs={{0,1},{1,0},{2,3},{3,2},{4,5},{5,4},{6,7},{7,6},{8,9},{9,8},{10,11... | collective-permute-start | bytes 73736 | tf_op jit(solution)/shard_map/ppermute | solution.py:488
  39.1 3.8 %collective-permute-start.12 = (f32[3,16,128]{2,1,0:T(8,128)S(1)}, f32[3,16,128]{2,1,0:T(8,128)S(1)}, u32[]{:S(2)}, u32[]{:S(2)}) collective-permute-start(f32[3,16,128]{2,1,0:T(8,128)S(1)} %get-tuple-element.41), channel_id=1, source_target_pairs={{0,4},{1,2},{2,1},{3,7},{4,0},{5,6},{6,5},{7,3},{8,12},{9,10},{10,... | collective-permute-start | bytes 73736 | tf_op jit(solution)/shard_map/ppermute | solution.py:489
  43.3 1.4 %collective-permute-start.13 = (f32[1,256]{1,0:T(1,128)S(1)}, f32[1,256]{1,0:T(1,128)S(1)}, u32[]{:S(2)}, u32[]{:S(2)}) collective-permute-start(f32[1,256]{1,0:T(1,128)S(1)} %get-tuple-element.45), channel_id=1, source_target_pairs={{4,0},{8,4},{12,8},{16,12},{20,16},{24,20},{28,24},{0,28},{5,1},{9... | collective-permute-start | bytes 3080 | tf_op jit(solution)/shard_map/ppermute | solution.py:547
  44.7 5.5 %collective-permute-start.16 = (f32[1,256]{1,0:T(1,128)S(1)}, f32[1,256]{1,0:T(1,128)S(1)}, u32[]{:S(2)}, u32[]{:S(2)}) collective-permute-start(f32[1,256]{1,0:T(1,128)S(1)} %add.11.rest_0_), channel_id=1, source_target_pairs={{0,1},{1,0},{2,3},{3,2},{4,5},{5,4},{6,7},{7,6},{8,9},{9,8},{10,11... | collective-permute-start | bytes 3080 | tf_op jit(solution)/shard_map/ppermute | solution.py:500
  46.7 4.5 %collective-permute-start.15 = (f32[1,256]{1,0:T(1,128)S(1)}, f32[1,256]{1,0:T(1,128)S(1)}, u32[]{:S(2)}, u32[]{:S(2)}) collective-permute-start(f32[1,256]{1,0:T(1,128)S(1)} %add.11.rest_0_), channel_id=1, source_target_pairs={{0,2},{1,3},{2,0},{3,1},{4,6},{5,7},{6,4},{7,5},{8,10},{9,11},{10,... | collective-permute-start | bytes 3080 | tf_op jit(solution)/shard_map/ppermute | solution.py:500
  46.7 5.4 %collective-permute-start.14 = (f32[1,256]{1,0:T(1,128)S(1)}, f32[1,256]{1,0:T(1,128)S(1)}, u32[]{:S(2)}, u32[]{:S(2)}) collective-permute-start(f32[1,256]{1,0:T(1,128)S(1)} %add.11.rest_0_), channel_id=1, source_target_pairs={{0,3},{1,2},{2,1},{3,0},{4,7},{5,6},{6,5},{7,4},{8,11},{9,10},{10,... | collective-permute-start | bytes 3080 | tf_op jit(solution)/shard_map/ppermute | solution.py:500

commit v6 on v5

--- a/solution.py
+++ b/solution.py
@@ -113,13 +113,11 @@
     copies = [
         pltpu.make_async_copy(here, there, sems.at[i])
         for i, (here, there) in enumerate(
-            ((tz, tz_v), (tx, tx_v), (src, src_v), (ty, ty_v))
+            ((tx, tx_v), (src, src_v), (ty, ty_v), (tz, tz_v))
         )
     ]
     for copy in copies:
         copy.start()
-    for copy in copies:
-        copy.wait()
     has_bot, has_top, has_below, _ = flags()
     slot = lax.broadcasted_iota(jnp.int32, (rows, cells), 1) // SPAN
     each = cells // SPAN
@@ -131,10 +129,12 @@
         for k in range(start, done):
             slabs[k] = turned[(k - start) * SPAN : (k - start + 1) * SPAN]
 
-    for x in range(count):
-        for which, ref in enumerate((tx_v, src_v, ty_v, tz_v, tz_v)):
+    for which, ref in enumerate((tx_v, src_v, ty_v, tz_v, tz_v)):
+        ahead = which // 4
+        if not ahead:
+            copies[which].wait()
+        for x in range(count):
             j = done % each
-            ahead = which // 4
             turned = pltpu.roll(ref[0, x], (SPAN * j + SLAB - ahead) % cells, 1)
             packed = jnp.where(slot == j, turned, packed)
             done += 1
@@ -142,7 +142,7 @@
                 flush(packed, done)
 
     def item(which, x):
-        return slabs[x * ITEMS + which]
+        return slabs[which * count + x]
 
     def make(x):
         return Thin(item(2, x), item(3, x), item(4, x), has_bot, has_top)
@@ -186,14 +186,14 @@
 def thin_setup(slabs, above, below):
     count = slabs.shape[0] // ITEMS
     has_bot, has_top, has_below, has_above = flags()
-    cx = {x: slabs[x * ITEMS] for x in range(1, count)}
+    cx = {x: slabs[x] for x in range(1, count)}
     cx[-1] = below[0]
     cx[0] = slabs[0] * has_below
     cx[count] = above[0] * has_above
-    source = {x: slabs[x * ITEMS + 1] for x in range(count)}
+    source = {x: slabs[count + x] for x in range(count)}
     source[-1] = below[2]
     layers = {
-        x: Thin(*(slabs[x * ITEMS + i] for i in (2, 3, 4)), has_bot, has_top)
+        x: Thin(*(slabs[i * count + x] for i in (2, 3, 4)), has_bot, has_top)
         for x in range(count)
     }
     layers[-1] = Thin(below[4], below[5], below[3], has_bot, has_top)
@@ -284,7 +284,7 @@
     cx = {x: kept[x + 1, 0] for x in span}
     w = {x: kept[x + 1, 1] for x in span}
     layers = {x: Kept(kept, x) for x in span}
-    return {x: slabs[x * ITEMS + 1] for x in range(count)}, cx, layers, w
+    return {x: slabs[count + x] for x in range(count)}, cx, layers, w
 
 
 def with_faces(source, layers, data, count):

time: 52.9 us -> 53 us (level)
  no operation moved by 1% of the time
where the time goes in v6:
time: 53 us; the launch traced here: 52.9 us
  waiting for transfers between devices  26 us (49%)
  starting transfers between devices  19.8 us (37%)
  Pallas kernels  6.3 us (12%)
  between operations  0.75 us (1%)
    ppermute x4, waiting for transfers between devices, trade(): first = lax.ppermute(a, names, pair_one)  17.3 us
    ppermute x6, starting transfers between devices, everyone(): parts.append(lax.ppermute(value, 'sub', [(i, i ^ k) for i in range(subs)]))  8.84 us
    ppermute x4, starting transfers between devices, trade(): first = lax.ppermute(a, names, pair_one)  8.21 us
    pallas_call x10, Pallas kernels, call(): pl.pallas_call(kernel, out_shape=[target(shape, F32) for shape in outs],...  6.3 us
    ppermute x6, waiting for transfers between devices, everyone(): parts.append(lax.ppermute(value, 'sub', [(i, i ^ k) for i in range(subs)]))  6.1 us
    ppermute x1, starting transfers between devices, work(): other_b = lax.ppermute(share_b, 'block', block_two)  2.55 us
    ppermute x1, waiting for transfers between devices, work(): other_b = lax.ppermute(share_b, 'block', block_two)  1.41 us
    ppermute x1, waiting for transfers between devices, work(): lax.ppermute(cbot, 'block', [((b + 1) % blocks, b) for b in range(blocks)])  1.14 us
  transfers between devices with their start and end apart: 17, of which 9 were waited for; matrix products, arithmetic and copies ran while one was open for 0% of the time, Pallas kernels for 5%

profile of v6, /device:TPU:0, one launch (start us, length us, event | category | flops | bytes accessed | tf_op | source)
XLA Modules:
  0.0 52.9 jit_solution(10457547665038090062)
XLA Ops:
  0.6 1.9 %shard_map.77 = (f32[1,4,128,128]{3,2,1,0:T(8,128)S(1)}, f32[1,4,128,128]{3,2,1,0:T(8,128)S(1)}, f32[1,4,128,128]{3,2,1,0:T(8,128)S(1)}, f32[1,4,128,128]{3,2,1,...) custom-call(f32[1,4,128,128]{3,2,1,0:T(8,128)} %src.1, ...), custom_call_target="tpu_custom_call" | custom-call | tf_op jit(solution)/shard_map/pallas_call | solution.py:455
  2.7 3.2 %collective-permute-start = (f32[5,128,128]{2,1,0:T(8,128)S(1)}, f32[5,128,128]{2,1,0:T(8,128)S(1)}, u32[]{:S(2)}, u32[]{:S(2)}) collective-permute-start(f32[5,128,128]{2,1,0:T(8,128)S(1)} %get-tuple-element.28), channel_id=1, source_target_pairs={{0,1},{1,0},{2,3},{3,2},{4,5},{5,4},{6,7},{7,6},{8,9},{9,8},{10,11... | collective-permute-start | bytes 983048 | tf_op jit(solution)/shard_map/ppermute | solution.py:488
  5.9 7.7 %collective-permute-done.got_a = f32[5,128,128]{2,1,0:T(8,128)S(1)} collective-permute-done((f32[5,128,128]{2,1,0:T(8,128)S(1)}, f32[5,128,128]{2,1,0:T(8,128)S(1)}, u32[]{:S(2)}, u32[]{:S(2)}) %collective-permute-start) | collective-permute-done | bytes 327712 | tf_op jit(solution)/shard_map/ppermute | solution.py:488
  13.6 0.9 %shard_map.79 = (f32[4,128,128]{2,1,0:T(8,128)S(1)}, f32[5,128,128]{2,1,0:T(8,128)S(1)}, f32[5,128,128]{2,1,0:T(8,128)S(1)}) custom-call(f32[1,4,128,128]{3,2,1,0:T(8,128)S(1)} %get-tuple-element.24.src, f32[1,4,128,128]{3,2,1,0:T(8,128)S(1)} %get-tuple-element.25.tx, f32[1,4,128,128]{3,2,1,0:T(8,128)S(1)} %get-tuple-element.26.ty, ...), custom_call_target="tpu_custom_call" | custom-call | tf_op jit(solution)/shard_map/pallas_call | solution.py:455
  14.6 2.9 %collective-permute-start.2 = (f32[5,128,128]{2,1,0:T(8,128)S(1)}, f32[5,128,128]{2,1,0:T(8,128)S(1)}, u32[]{:S(2)}, u32[]{:S(2)}) collective-permute-start(f32[5,128,128]{2,1,0:T(8,128)S(1)} %get-tuple-element.31), channel_id=1, source_target_pairs={{0,1},{1,0},{2,3},{3,2},{4,5},{5,4},{6,7},{7,6},{8,9},{9,8},{10,11... | collective-permute-start | bytes 983048 | tf_op jit(solution)/shard_map/ppermute | solution.py:488
  17.5 2.0 %collective-permute-start.4 = (f32[6,16,128]{2,1,0:T(8,128)S(1)}, f32[6,16,128]{2,1,0:T(8,128)S(1)}, u32[]{:S(2)}, u32[]{:S(2)}) collective-permute-start(f32[6,16,128]{2,1,0:T(8,128)S(1)} %get-tuple-element.34), channel_id=1, source_target_pairs={{0,1},{1,0},{2,3},{3,2},{4,5},{5,4},{6,7},{7,6},{8,9},{9,8},{10,11... | collective-permute-start | bytes 147464 | tf_op jit(solution)/shard_map/ppermute | solution.py:488
  19.5 5.9 %collective-permute-done.4.got_a = f32[6,16,128]{2,1,0:T(8,128)S(1)} collective-permute-done((f32[6,16,128]{2,1,0:T(8,128)S(1)}, f32[6,16,128]{2,1,0:T(8,128)S(1)}, u32[]{:S(2)}, u32[]{:S(2)}) %collective-permute-start.4) | collective-permute-done | bytes 49184 | tf_op jit(solution)/shard_map/ppermute | solution.py:488
  25.4 0.4 shard_map.80
  26.1 2.5 %collective-permute-start.7 = (f32[1,256]{1,0:T(1,128)S(1)}, f32[1,256]{1,0:T(1,128)S(1)}, u32[]{:S(2)}, u32[]{:S(2)}) collective-permute-start(f32[1,256]{1,0:T(1,128)S(1)} %get-tuple-element.38), channel_id=1, source_target_pairs={{0,28},{4,8},{8,4},{12,16},{16,12},{20,24},{24,20},{28,0},{1,29},{... | collective-permute-start | bytes 3080 | tf_op jit(solution)/shard_map/ppermute | solution.py:522
  28.7 1.4 %collective-permute-done.7 = f32[1,256]{1,0:T(1,128)S(1)} collective-permute-done((f32[1,256]{1,0:T(1,128)S(1)}, f32[1,256]{1,0:T(1,128)S(1)}, u32[]{:S(2)}, u32[]{:S(2)}) %collective-permute-start.7) | collective-permute-done | bytes 1056 | tf_op jit(solution)/shard_map/ppermute | solution.py:522
  30.1 1.9 %collective-permute-start.10 = (f32[2,256]{1,0:T(2,128)S(1)}, f32[2,256]{1,0:T(2,128)S(1)}, u32[]{:S(2)}, u32[]{:S(2)}) collective-permute-start(f32[2,256]{1,0:T(2,128)S(1)} %pad_maximum_fusion.rest_0_), channel_id=1, source_target_pairs={{0,1},{1,0},{2,3},{3,2},{4,5},{5,4},{6,7},{7,6},{8,9},{9,8},{10,11... | collective-permute-start | bytes 6152 | tf_op jit(solution)/shard_map/ppermute | solution.py:500
  32.0 1.4 %collective-permute-start.9 = (f32[2,256]{1,0:T(2,128)S(1)}, f32[2,256]{1,0:T(2,128)S(1)}, u32[]{:S(2)}, u32[]{:S(2)}) collective-permute-start(f32[2,256]{1,0:T(2,128)S(1)} %pad_maximum_fusion.rest_0_), channel_id=1, source_target_pairs={{0,2},{1,3},{2,0},{3,1},{4,6},{5,7},{6,4},{7,5},{8,10},{9,11},{10,... | collective-permute-start | bytes 6152 | tf_op jit(solution)/shard_map/ppermute | solution.py:500
  33.4 1.2 %collective-permute-start.8 = (f32[2,256]{1,0:T(2,128)S(1)}, f32[2,256]{1,0:T(2,128)S(1)}, u32[]{:S(2)}, u32[]{:S(2)}) collective-permute-start(f32[2,256]{1,0:T(2,128)S(1)} %pad_maximum_fusion.rest_0_), channel_id=1, source_target_pairs={{0,3},{1,2},{2,1},{3,0},{4,7},{5,6},{6,5},{7,4},{8,11},{9,10},{10,... | collective-permute-start | bytes 6152 | tf_op jit(solution)/shard_map/ppermute | solution.py:500
  34.6 1.9 %collective-permute-done.9.rest_2_ = f32[2,256]{1,0:T(2,128)S(1)} collective-permute-done((f32[2,256]{1,0:T(2,128)S(1)}, f32[2,256]{1,0:T(2,128)S(1)}, u32[]{:S(2)}, u32[]{:S(2)}) %collective-permute-start.9) | collective-permute-done | bytes 2080 | tf_op jit(solution)/shard_map/ppermute | solution.py:500
  36.5 2.3 %collective-permute-done.8.rest_1_ = f32[2,256]{1,0:T(2,128)S(1)} collective-permute-done((f32[2,256]{1,0:T(2,128)S(1)}, f32[2,256]{1,0:T(2,128)S(1)}, u32[]{:S(2)}, u32[]{:S(2)}) %collective-permute-start.8) | collective-permute-done | bytes 2080 | tf_op jit(solution)/shard_map/ppermute | solution.py:500
  39.2 3.7 %collective-permute-done.11.edge_a = f32[3,16,128]{2,1,0:T(8,128)S(1)} collective-permute-done((f32[3,16,128]{2,1,0:T(8,128)S(1)}, f32[3,16,128]{2,1,0:T(8,128)S(1)}, u32[]{:S(2)}, u32[]{:S(2)}) %collective-permute-start.11) | collective-permute-done | bytes 24608 | tf_op jit(solution)/shard_map/ppermute | solution.py:488
  43.0 0.4 shard_map.83
  43.6 1.1 %collective-permute-done.13 = f32[1,256]{1,0:T(1,128)S(1)} collective-permute-done((f32[1,256]{1,0:T(1,128)S(1)}, f32[1,256]{1,0:T(1,128)S(1)}, u32[]{:S(2)}, u32[]{:S(2)}) %collective-permute-start.13) | collective-permute-done | bytes 1056 | tf_op jit(solution)/shard_map/ppermute | solution.py:547
  44.7 2.0 %collective-permute-start.16 = (f32[1,256]{1,0:T(1,128)S(1)}, f32[1,256]{1,0:T(1,128)S(1)}, u32[]{:S(2)}, u32[]{:S(2)}) collective-permute-start(f32[1,256]{1,0:T(1,128)S(1)} %add.11.rest_0_), channel_id=1, source_target_pairs={{0,1},{1,0},{2,3},{3,2},{4,5},{5,4},{6,7},{7,6},{8,9},{9,8},{10,11... | collective-permute-start | bytes 3080 | tf_op jit(solution)/shard_map/ppermute | solution.py:500
  46.8 2.4 %collective-permute-start.14 = (f32[1,256]{1,0:T(1,128)S(1)}, f32[1,256]{1,0:T(1,128)S(1)}, u32[]{:S(2)}, u32[]{:S(2)}) collective-permute-start(f32[1,256]{1,0:T(1,128)S(1)} %add.11.rest_0_), channel_id=1, source_target_pairs={{0,3},{1,2},{2,1},{3,0},{4,7},{5,6},{6,5},{7,4},{8,11},{9,10},{10,... | collective-permute-start | bytes 3080 | tf_op jit(solution)/shard_map/ppermute | solution.py:500
  49.1 1.1 %shard_map.84.merged = f32[1,4,128,128]{3,2,1,0:T(8,128)S(1)} custom-call(f32[1,4,128,128]{3,2,1,0:T(8,128)S(1)} %get-tuple-element.24.src, f32[1,4,128,128]{3,2,1,0:T(8,128)S(1)} %get-tuple-element.25.tx, f32[1,4,128,128]{3,2,1,0:T(8,128)S(1)} %get-tuple-element.26.ty, f32[1,4,128,128]{3,2,1,0:T(8,128)S(1)} %get-tuple-element.27.tz, ...), custom_call_target="tpu_custom_call" | custom-call | tf_op jit(solution)/shard_map/pallas_call | solution.py:455
  50.2 1.0 %collective-permute-done.15.rest_2_ = f32[1,256]{1,0:T(1,128)S(1)} collective-permute-done((f32[1,256]{1,0:T(1,128)S(1)}, f32[1,256]{1,0:T(1,128)S(1)}, u32[]{:S(2)}, u32[]{:S(2)}) %collective-permute-start.15) | collective-permute-done | bytes 1056 | tf_op jit(solution)/shard_map/ppermute | solution.py:500
  51.2 0.9 %collective-permute-done.14.rest_1_ = f32[1,256]{1,0:T(1,128)S(1)} collective-permute-done((f32[1,256]{1,0:T(1,128)S(1)}, f32[1,256]{1,0:T(1,128)S(1)}, u32[]{:S(2)}, u32[]{:S(2)}) %collective-permute-start.14) | collective-permute-done | bytes 1056 | tf_op jit(solution)/shard_map/ppermute | solution.py:500
  52.1 0.7 %shard_map.86 = (f32[1,4,128,128]{3,2,1,0:T(8,128)}, f32[1,64]{1,0:T(1,128)}) custom-call(f32[1,4,128,128]{3,2,1,0:T(8,128)S(1)} %shard_map.84.merged, f32[1,256]{1,0:T(1,128)S(1)} %get-tuple-element.43.mortar, f32[1,256]{1,0:T(1,128)S(1)} %add.11.rest_0_, f32[1,256]{1,0:T(1,128)S(1)} %collective-permute-done.14.rest_1_, ...), custom_call_target="tpu_custom_call" | custom-call | tf_op jit(solution)/shard_map/pallas_call | solution.py:455
  (28 shorter events, 1.2 us)
Async XLA Ops:
  2.7 10.9 %collective-permute-start = (f32[5,128,128]{2,1,0:T(8,128)S(1)}, f32[5,128,128]{2,1,0:T(8,128)S(1)}, u32[]{:S(2)}, u32[]{:S(2)}) collective-permute-start(f32[5,128,128]{2,1,0:T(8,128)S(1)} %get-tuple-element.28), channel_id=1, source_target_pairs={{0,1},{1,0},{2,3},{3,2},{4,5},{5,4},{6,7},{7,6},{8,9},{9,8},{10,11... | collective-permute-start | bytes 983048 | tf_op jit(solution)/shard_map/ppermute | solution.py:488
  5.9 19.5 %copy-start = (f32[1,4,128,256]{3,2,1,0:T(8,128)S(1)}, f32[1,4,128,256]{3,2,1,0:T(8,128)}, u32[]{:S(2)}) copy-start(f32[1,4,128,256]{3,2,1,0:T(8,128)} %bot.7) | copy-start | bytes 1572868
  5.9 19.5 %copy-start.1 = (f32[1,4,128,256]{3,2,1,0:T(8,128)S(1)}, f32[1,4,128,256]{3,2,1,0:T(8,128)}, u32[]{:S(2)}) copy-start(f32[1,4,128,256]{3,2,1,0:T(8,128)} %top.7) | copy-start | bytes 1572868
  5.9 7.7 %collective-permute-start.1 = (f32[5,128,128]{2,1,0:T(8,128)S(1)}, f32[5,128,128]{2,1,0:T(8,128)S(1)}, u32[]{:S(2)}, u32[]{:S(2)}) collective-permute-start(f32[5,128,128]{2,1,0:T(8,128)S(1)} %get-tuple-element.29), channel_id=1, source_target_pairs={{0,4},{1,2},{2,1},{3,7},{4,0},{5,6},{6,5},{7,3},{8,12},{9,10},{10,... | collective-permute-start | bytes 983048 | tf_op jit(solution)/shard_map/ppermute | solution.py:489
  14.6 34.6 %collective-permute-start.2 = (f32[5,128,128]{2,1,0:T(8,128)S(1)}, f32[5,128,128]{2,1,0:T(8,128)S(1)}, u32[]{:S(2)}, u32[]{:S(2)}) collective-permute-start(f32[5,128,128]{2,1,0:T(8,128)S(1)} %get-tuple-element.31), channel_id=1, source_target_pairs={{0,1},{1,0},{2,3},{3,2},{4,5},{5,4},{6,7},{7,6},{8,9},{9,8},{10,11... | collective-permute-start | bytes 983048 | tf_op jit(solution)/shard_map/ppermute | solution.py:488
  17.5 31.6 %collective-permute-start.3 = (f32[5,128,128]{2,1,0:T(8,128)S(1)}, f32[5,128,128]{2,1,0:T(8,128)S(1)}, u32[]{:S(2)}, u32[]{:S(2)}) collective-permute-start(f32[5,128,128]{2,1,0:T(8,128)S(1)} %get-tuple-element.32), channel_id=1, source_target_pairs={{0,4},{1,2},{2,1},{3,7},{4,0},{5,6},{6,5},{7,3},{8,12},{9,10},{10,... | collective-permute-start | bytes 983048 | tf_op jit(solution)/shard_map/ppermute | solution.py:489
  17.5 7.9 %collective-permute-start.4 = (f32[6,16,128]{2,1,0:T(8,128)S(1)}, f32[6,16,128]{2,1,0:T(8,128)S(1)}, u32[]{:S(2)}, u32[]{:S(2)}) collective-permute-start(f32[6,16,128]{2,1,0:T(8,128)S(1)} %get-tuple-element.34), channel_id=1, source_target_pairs={{0,1},{1,0},{2,3},{3,2},{4,5},{5,4},{6,7},{7,6},{8,9},{9,8},{10,11... | collective-permute-start | bytes 147464 | tf_op jit(solution)/shard_map/ppermute | solution.py:488
  19.5 5.9 %collective-permute-start.5 = (f32[6,16,128]{2,1,0:T(8,128)S(1)}, f32[6,16,128]{2,1,0:T(8,128)S(1)}, u32[]{:S(2)}, u32[]{:S(2)}) collective-permute-start(f32[6,16,128]{2,1,0:T(8,128)S(1)} %get-tuple-element.35), channel_id=1, source_target_pairs={{0,4},{1,2},{2,1},{3,7},{4,0},{5,6},{6,5},{7,3},{8,12},{9,10},{10,... | collective-permute-start | bytes 147464 | tf_op jit(solution)/shard_map/ppermute | solution.py:489
  26.0 2.6 %collective-permute-start.6 = (f32[1,256]{1,0:T(1,128)S(1)}, f32[1,256]{1,0:T(1,128)S(1)}, u32[]{:S(2)}, u32[]{:S(2)}) collective-permute-start(f32[1,256]{1,0:T(1,128)S(1)} %shard_map.81), channel_id=1, source_target_pairs={{0,4},{4,0},{8,12},{12,8},{16,20},{20,16},{24,28},{28,24},{1,5},{5... | collective-permute-start | bytes 3080 | tf_op jit(solution)/shard_map/ppermute | solution.py:524
  26.1 4.0 %collective-permute-start.7 = (f32[1,256]{1,0:T(1,128)S(1)}, f32[1,256]{1,0:T(1,128)S(1)}, u32[]{:S(2)}, u32[]{:S(2)}) collective-permute-start(f32[1,256]{1,0:T(1,128)S(1)} %get-tuple-element.38), channel_id=1, source_target_pairs={{0,28},{4,8},{8,4},{12,16},{16,12},{20,24},{24,20},{28,0},{1,29},{... | collective-permute-start | bytes 3080 | tf_op jit(solution)/shard_map/ppermute | solution.py:522
  30.1 4.5 %collective-permute-start.10 = (f32[2,256]{1,0:T(2,128)S(1)}, f32[2,256]{1,0:T(2,128)S(1)}, u32[]{:S(2)}, u32[]{:S(2)}) collective-permute-start(f32[2,256]{1,0:T(2,128)S(1)} %pad_maximum_fusion.rest_0_), channel_id=1, source_target_pairs={{0,1},{1,0},{2,3},{3,2},{4,5},{5,4},{6,7},{7,6},{8,9},{9,8},{10,11... | collective-permute-start | bytes 6152 | tf_op jit(solution)/shard_map/ppermute | solution.py:500
  32.0 4.5 %collective-permute-start.9 = (f32[2,256]{1,0:T(2,128)S(1)}, f32[2,256]{1,0:T(2,128)S(1)}, u32[]{:S(2)}, u32[]{:S(2)}) collective-permute-start(f32[2,256]{1,0:T(2,128)S(1)} %pad_maximum_fusion.rest_0_), channel_id=1, source_target_pairs={{0,2},{1,3},{2,0},{3,1},{4,6},{5,7},{6,4},{7,5},{8,10},{9,11},{10,... | collective-permute-start | bytes 6152 | tf_op jit(solution)/shard_map/ppermute | solution.py:500
  33.4 5.4 %collective-permute-start.8 = (f32[2,256]{1,0:T(2,128)S(1)}, f32[2,256]{1,0:T(2,128)S(1)}, u32[]{:S(2)}, u32[]{:S(2)}) collective-permute-start(f32[2,256]{1,0:T(2,128)S(1)} %pad_maximum_fusion.rest_0_), channel_id=1, source_target_pairs={{0,3},{1,2},{2,1},{3,0},{4,7},{5,6},{6,5},{7,4},{8,11},{9,10},{10,... | collective-permute-start | bytes 6152 | tf_op jit(solution)/shard_map/ppermute | solution.py:500
  39.1 3.9 %collective-permute-start.11 = (f32[3,16,128]{2,1,0:T(8,128)S(1)}, f32[3,16,128]{2,1,0:T(8,128)S(1)}, u32[]{:S(2)}, u32[]{:S(2)}) collective-permute-start(f32[3,16,128]{2,1,0:T(8,128)S(1)} %get-tuple-element.40), channel_id=1, source_target_pairs={{0,1},{1,0},{2,3},{3,2},{4,5},{5,4},{6,7},{7,6},{8,9},{9,8},{10,11... | collective-permute-start | bytes 73736 | tf_op jit(solution)/shard_map/ppermute | solution.py:488
  39.2 3.8 %collective-permute-start.12 = (f32[3,16,128]{2,1,0:T(8,128)S(1)}, f32[3,16,128]{2,1,0:T(8,128)S(1)}, u32[]{:S(2)}, u32[]{:S(2)}) collective-permute-start(f32[3,16,128]{2,1,0:T(8,128)S(1)} %get-tuple-element.41), channel_id=1, source_target_pairs={{0,4},{1,2},{2,1},{3,7},{4,0},{5,6},{6,5},{7,3},{8,12},{9,10},{10,... | collective-permute-start | bytes 73736 | tf_op jit(solution)/shard_map/ppermute | solution.py:489
  43.4 1.4 %collective-permute-start.13 = (f32[1,256]{1,0:T(1,128)S(1)}, f32[1,256]{1,0:T(1,128)S(1)}, u32[]{:S(2)}, u32[]{:S(2)}) collective-permute-start(f32[1,256]{1,0:T(1,128)S(1)} %get-tuple-element.45), channel_id=1, source_target_pairs={{4,0},{8,4},{12,8},{16,12},{20,16},{24,20},{28,24},{0,28},{5,1},{9... | collective-permute-start | bytes 3080 | tf_op jit(solution)/shard_map/ppermute | solution.py:547
  44.7 5.5 %collective-permute-start.16 = (f32[1,256]{1,0:T(1,128)S(1)}, f32[1,256]{1,0:T(1,128)S(1)}, u32[]{:S(2)}, u32[]{:S(2)}) collective-permute-start(f32[1,256]{1,0:T(1,128)S(1)} %add.11.rest_0_), channel_id=1, source_target_pairs={{0,1},{1,0},{2,3},{3,2},{4,5},{5,4},{6,7},{7,6},{8,9},{9,8},{10,11... | collective-permute-start | bytes 3080 | tf_op jit(solution)/shard_map/ppermute | solution.py:500
  46.8 4.5 %collective-permute-start.15 = (f32[1,256]{1,0:T(1,128)S(1)}, f32[1,256]{1,0:T(1,128)S(1)}, u32[]{:S(2)}, u32[]{:S(2)}) collective-permute-start(f32[1,256]{1,0:T(1,128)S(1)} %add.11.rest_0_), channel_id=1, source_target_pairs={{0,2},{1,3},{2,0},{3,1},{4,6},{5,7},{6,4},{7,5},{8,10},{9,11},{10,... | collective-permute-start | bytes 3080 | tf_op jit(solution)/shard_map/ppermute | solution.py:500
  46.8 5.4 %collective-permute-start.14 = (f32[1,256]{1,0:T(1,128)S(1)}, f32[1,256]{1,0:T(1,128)S(1)}, u32[]{:S(2)}, u32[]{:S(2)}) collective-permute-start(f32[1,256]{1,0:T(1,128)S(1)} %add.11.rest_0_), channel_id=1, source_target_pairs={{0,3},{1,2},{2,1},{3,0},{4,7},{5,6},{6,5},{7,4},{8,11},{9,10},{10,... | collective-permute-start | bytes 3080 | tf_op jit(solution)/shard_map/ppermute | solution.py:500
